TPU v7x, 32 devices: a whole 2x2x4 slice. The times are simulated.
32 devices in a mesh: block: 4 (over y, x), dp: 8 (over z, core).
Axes of the slice: x: 2, y: 2, z: 4, core: 2. Of those that a mesh axis runs over, the one named last changes fastest.
Arguments:
- tokens: bfloat16 [2048, 16384], P('dp', 'block'), may hold values from -6 to 6
- first_up: bfloat16 [128, 128, 128], P('block'), may hold values from -0.5 to 0.5
- second_up: bfloat16 [128, 128, 512], P('block'), may hold values from -0.5 to 0.5
- first_down: bfloat16 [128, 512, 128], P('block'), may hold values from -0.25 to 0.25
- second_down: bfloat16 [128, 128, 128], P('block'), may hold values from -0.5 to 0.5
- cotangent: bfloat16 [2048, 16384], P('dp', 'block'), may hold values from -6 to 6
Outputs:
- output: bfloat16 [2048, 16384], P('dp', 'block')
- input_grad: bfloat16 [2048, 16384], P('dp', 'block')
- grad_first_up: float32 [128, 128, 128], P('block', 'dp')
- grad_second_up: float32 [128, 128, 512], P('block', 'dp')
- grad_first_down: float32 [128, 512, 128], P('block', 'dp')
- grad_second_down: float32 [128, 128, 128], P('block', 'dp')
All inputs are finite; a program needn't handle non-finite values.
Results may differ from a plain program's by a relative error of at most 0.0071.
Values may be sent and summed in bfloat16 or wider, within the bound.
No kernel may reach another device: no remote copies, remote signals or barrier semaphores. Data moves between devices by JAX's collectives and lax.ppermute only.
A program may use at most 192 MiB of HBM per device.

v0:
```python
import functools
import math

import jax
import jax.numpy as jnp
from jax import lax
from jax.experimental import pallas as pl
from jax.experimental.pallas import tpu as pltpu
from jax.sharding import PartitionSpec as P


NARROW = jnp.bfloat16
WIDE = jnp.float32
LANES = 128
ROWS = 16
PITCH = 24
CHUNKS = 4
STEP = 4
CORES = 2


def gelu_pair(values):
    factor = math.sqrt(2.0 / math.pi)
    square = values * values
    tanh_part = jnp.tanh(factor * values * (1.0 + 0.044715 * square))
    half = 0.5 + 0.5 * tanh_part
    active = values * half
    slope_term = half + active * (1.0 - tanh_part) * (factor + (3.0 * 0.044715 * factor) * square)
    return (active, slope_term)


def dot(a, b, ca, cb):
    return lax.dot_general(a, b, (((ca,), (cb,)), ((), ())), preferred_element_type=WIDE)


def spread(scr, b, width, value):
    for h in range(scr.shape[0]):
        scr[h, pl.ds(b, width, stride=PITCH), :] = value[:, h * LANES : (h + 1) * LANES]


def collect(scr, b, width):
    pieces = [scr[h, pl.ds(b, width, stride=PITCH), :] for h in range(scr.shape[0])]
    return jnp.concatenate(pieces, axis=1).astype(NARROW)


def mix_in_body(groups, chunks, x_ref, g_ref, fu_ref, sd_ref, *rest):
    outs, (scr_u, scr_d) = rest[:-2], rest[-2:]
    rows, width = fu_ref.shape[0], fu_ref.shape[1]
    me = lax.axis_index("block")
    feats = width // groups
    part = feats // chunks
    for b in range(rows):
        cols = slice(b * width, (b + 1) * width)
        spread(scr_u, b, width, dot(fu_ref[b], x_ref[:, cols], 0, 1))
        spread(scr_d, b, width, dot(sd_ref[b], g_ref[:, cols], 1, 1))
    for c in range(chunks):
        for s in range(groups):
            ref = outs[c * groups + s]
            off = pl.multiple_of(((me ^ s) * feats + c * part) * PITCH, 8)
            for k, scr in enumerate((scr_u, scr_d)):
                for h in range(scr.shape[0]):
                    for n in range(part):
                        value = scr[h, pl.ds(off + n * PITCH, rows), :]
                        ref[k, n, :, h * LANES : (h + 1) * LANES] = value.astype(NARROW)


def mix_in(tokens, cotangent, first_up, second_down, groups, chunks):
    count = tokens.shape[0]
    blocks, width = first_up.shape[:2]
    part = width // groups // chunks
    shape = jax.ShapeDtypeStruct((2, part, blocks, count), NARROW)
    flat = pl.BlockSpec((count, ROWS * width), lambda i: (0, i))
    mats = pl.BlockSpec((ROWS, width, width), lambda i: (i, 0, 0))
    out = pl.BlockSpec((2, part, ROWS, count), lambda i: (0, 0, i, 0))
    n_out = chunks * groups
    res = pl.pallas_call(
        functools.partial(mix_in_body, groups, chunks),
        grid=(blocks // ROWS,),
        in_specs=[flat, flat, mats, mats],
        out_specs=[out] * n_out,
        scratch_shapes=[pltpu.VMEM((count // LANES, width * PITCH, LANES), WIDE)] * 2,
        out_shape=[shape] * n_out,
        cost_estimate=pl.CostEstimate(
            flops=4 * count * blocks * width * width, transcendentals=0, bytes_accessed=8 * count * blocks * width
        ),
        name="mix_in",
    )(tokens, cotangent, first_up, second_down)
    return [res[c * groups : (c + 1) * groups] for c in range(chunks)]


def mirrored(value, bits):
    return sum(((value >> t) & 1) << (bits - 1 - t) for t in range(bits))


def feature_body(groups, line, *rest):
    ins, (wu_ref, wd_ref) = rest[:groups], rest[groups : groups + 2]
    outs = rest[groups + 2 : 2 * groups + 2]
    keep_ref, send_ref, u_scr, d_scr, v_scr, e_scr = rest[2 * groups + 2 :]
    me = lax.axis_index("block")
    first = lax.axis_index("dp") % CORES == 0
    blocks = ins[0].shape[2]
    offs = [pl.multiple_of((me ^ s) * blocks, ROWS) for s in range(groups)]
    bits = line.bit_length() - 1
    for n in range(wu_ref.shape[0]):
        for s in range(groups):
            u_scr[n, pl.ds(offs[s], blocks), :] = ins[s][0, n]
            d_scr[n, pl.ds(offs[s], blocks), :] = ins[s][1, n]
    for n in range(wu_ref.shape[0]):
        u, d = u_scr[n], d_scr[n]
        wu, wd = wu_ref[n], wd_ref[n]
        active, slope = gelu_pair(dot(wu, u, 0, 0))
        active = active.astype(NARROW)
        v_scr[n] = dot(wd, active, 0, 0).astype(NARROW)
        back = (dot(wd, d, 1, 0) * slope).astype(NARROW)
        e_scr[n] = dot(wu, back, 1, 0).astype(NARROW)
        g_su = dot(u, back, 1, 1)
        g_fd = dot(active, d, 1, 1)
        r_su = g_su.shape[0] // (CORES * line)
        r_fd = g_fd.shape[0] // (CORES * line)
        fold = g_su.shape[1] // g_fd.shape[1]
        step = r_fd // fold
        for p in range(line):
            at = mirrored(p, bits)
            halves = []
            for k in range(CORES):
                r = p * CORES + k
                block = g_fd[r * r_fd : (r + 1) * r_fd]
                wide = jnp.concatenate([block[f * step : (f + 1) * step] for f in range(fold)], axis=1)
                halves.append((g_su[r * r_su : (r + 1) * r_su], wide))
            for h in range(2):
                rows = slice(h * r_su, (h + 1) * r_su)
                keep_ref[at, n, rows, :] = jnp.where(first, halves[0][h], halves[1][h]).astype(NARROW)
                send_ref[at, n, rows, :] = jnp.where(first, halves[1][h], halves[0][h]).astype(NARROW)
    for n in range(wu_ref.shape[0]):
        for s in range(groups):
            outs[s][0, n] = v_scr[n, pl.ds(offs[s], blocks), :]
            outs[s][1, n] = e_scr[n, pl.ds(offs[s], blocks), :]


def feature(arrays, second_up, first_down, c, line):
    groups = len(arrays)
    _, part, blocks, count = arrays[0].shape
    width, hidden = second_up.shape[1:]
    r_su = width // (CORES * line)
    each = math.gcd(STEP, part)
    steps = part // each
    data = pl.BlockSpec((2, each, blocks, count), lambda i: (0, i, 0, 0))
    grads = pl.BlockSpec((line, each, 2 * r_su, hidden), lambda i: (0, i, 0, 0))
    g_shape = jax.ShapeDtypeStruct((line, part, 2 * r_su, hidden), NARROW)
    scr = pltpu.VMEM((each, groups * blocks, count), NARROW)
    res = pl.pallas_call(
        functools.partial(feature_body, groups, line),
        grid=(steps,),
        in_specs=[data] * groups
        + [
            pl.BlockSpec((each, width, hidden), lambda i: (c * steps + i, 0, 0)),
            pl.BlockSpec((each, hidden, width), lambda i: (c * steps + i, 0, 0)),
        ],
        out_specs=[data] * groups + [grads] * 2,
        scratch_shapes=[scr] * 4,
        out_shape=[jax.ShapeDtypeStruct(arrays[0].shape, NARROW)] * groups + [g_shape] * 2,
        cost_estimate=pl.CostEstimate(
            flops=12 * part * count * width * hidden,
            transcendentals=part * count * hidden,
            bytes_accessed=part * (8 * width * hidden + 8 * count * width),
        ),
        name="feature",
    )(*arrays, second_up, first_down)
    return res[:groups], res[groups], res[groups + 1]


def mix_out_body(groups, chunks, line, *rest):
    n_in = chunks * groups
    ins = rest[:n_in]
    x_ref, g_ref, fu_ref, sd_ref, out_ref, ig_ref, keep_ref, send_ref, scr_v, scr_d = rest[n_in:]
    rows, width = fu_ref.shape[0], fu_ref.shape[1]
    me = lax.axis_index("block")
    bits = line.bit_length() - 1
    feats = width // groups
    part = feats // chunks
    for c in range(chunks):
        for s in range(groups):
            ref = ins[c * groups + s]
            off = pl.multiple_of(((me ^ s) * feats + c * part) * PITCH, 8)
            for k, scr in enumerate((scr_v, scr_d)):
                for h in range(scr.shape[0]):
                    for n in range(part):
                        value = ref[k, n, :, h * LANES : (h + 1) * LANES]
                        scr[h, pl.ds(off + n * PITCH, rows), :] = value.astype(WIDE)
    first = lax.axis_index("dp") % CORES == 0
    r_one = width // (CORES * line)
    for b in range(rows):
        cols = slice(b * width, (b + 1) * width)
        v = collect(scr_v, b, width)
        d = collect(scr_d, b, width)
        out_ref[:, cols] = dot(v, sd_ref[b], 0, 0).astype(NARROW)
        ig_ref[:, cols] = dot(d, fu_ref[b], 0, 1).astype(NARROW)
        g_sd = dot(v, g_ref[:, cols], 1, 0)
        g_fu = dot(x_ref[:, cols], d, 0, 1)
        for p in range(line):
            halves = []
            for k in range(CORES):
                r = p * CORES + k
                own = slice(r * r_one, (r + 1) * r_one)
                halves.append(jnp.concatenate([g_fu[own], g_sd[own]], axis=0))
            at = mirrored(p, bits)
            keep_ref[at, b] = jnp.where(first, halves[0], halves[1]).astype(NARROW)
            send_ref[at, b] = jnp.where(first, halves[1], halves[0]).astype(NARROW)


def mix_out(arrays, tokens, cotangent, first_up, second_down, line):
    chunks, groups = len(arrays), len(arrays[0])
    _, part, blocks, count = arrays[0][0].shape
    width = first_up.shape[1]
    r_one = width // (CORES * line)
    data = pl.BlockSpec((2, part, ROWS, count), lambda i: (0, 0, i, 0))
    flat = pl.BlockSpec((count, ROWS * width), lambda i: (0, i))
    mats = pl.BlockSpec((ROWS, width, width), lambda i: (i, 0, 0))
    grads = pl.BlockSpec((line, ROWS, 2 * r_one, width), lambda i: (0, i, 0, 0))
    g_shape = jax.ShapeDtypeStruct((line, blocks, 2 * r_one, width), NARROW)
    flat_shape = jax.ShapeDtypeStruct(tokens.shape, NARROW)
    return pl.pallas_call(
        functools.partial(mix_out_body, groups, chunks, line),
        grid=(blocks // ROWS,),
        in_specs=[data] * (chunks * groups) + [flat, flat, mats, mats],
        out_specs=[flat, flat, grads, grads],
        scratch_shapes=[pltpu.VMEM((count // LANES, width * PITCH, LANES), WIDE)] * 2,
        out_shape=[flat_shape, flat_shape, g_shape, g_shape],
        cost_estimate=pl.CostEstimate(
            flops=8 * count * blocks * width * width, transcendentals=0, bytes_accessed=16 * count * blocks * width
        ),
        name="mix_out",
    )(*[a for chunk in arrays for a in chunk], tokens, cotangent, first_up, second_down)


def settle_body(fold, n_sum, *rest):
    ins, (first_ref, second_ref) = rest[:n_sum], rest[-2:]
    total = ins[0][0].astype(WIDE)
    for ref in ins[1:]:
        total = total + ref[0].astype(WIDE)
    half = total.shape[1] // 2
    first_ref[...] = total[:, :half]
    width = total.shape[2] // fold
    for f in range(fold):
        second_ref[:, f * half : (f + 1) * half, :] = total[:, half:, f * width : (f + 1) * width]


def settle(parts, line, fold, c, chunks, before):
    _, part, rows, cols = parts[0].shape
    steps = math.gcd(part, 4)
    tile = part // steps
    bits = line.bit_length() - 1

    def spec(array):
        size = array.shape[0]

        def where(i):
            return (mirrored(lax.axis_index("dp") // CORES, bits) % size, i, 0, 0)

        return pl.BlockSpec((1, tile, rows, cols), where)

    half = rows // 2
    shapes = (
        (part * chunks, half, cols),
        (part * chunks, half * fold, cols // fold),
    )
    return pl.pallas_call(
        functools.partial(settle_body, fold, len(parts)),
        grid=(steps,),
        in_specs=[spec(a) for a in parts] + [pl.BlockSpec(memory_space=pl.ANY)] * len(before),
        out_specs=[pl.BlockSpec((tile,) + s[1:], lambda i: (c * steps + i, 0, 0)) for s in shapes],
        out_shape=[jax.ShapeDtypeStruct(s, WIDE) for s in shapes],
        input_output_aliases={len(parts) + k: k for k in range(len(before))},
        cost_estimate=pl.CostEstimate(
            flops=4 * part * rows * cols, transcendentals=0, bytes_accessed=12 * part * rows * cols
        ),
        name="settle",
    )(*parts, *before)


def line_sum(keep, send, line):
    recv = lax.ppermute(send, "dp", [(i, i ^ 1) for i in range(CORES * line)])
    parts = [keep, recv]
    bits = line.bit_length() - 1
    place = lax.axis_index("dp") // CORES
    spot = mirrored(place, bits)
    for t in range(bits):
        span = line >> t
        half = span // 2
        start = (spot // span) * span + (1 - ((place >> t) & 1)) * half
        total = sum(
            lax.dynamic_slice_in_dim(a, start % a.shape[0], half, 0).astype(WIDE) for a in parts
        ).astype(NARROW)
        hop = CORES << t
        parts.append(lax.ppermute(total, "dp", [(i, i ^ hop) for i in range(CORES * line)]))
    return parts


def local(tokens, first_up, second_up, first_down, second_down, cotangent):
    groups = lax.axis_size("block")
    line = lax.axis_size("dp") // CORES
    chunks = math.gcd(CHUNKS, second_up.shape[0])

    def exchange(arrays):
        got = [arrays[0]]
        for s in range(1, groups):
            got.append(lax.ppermute(arrays[s], "block", [(i, i ^ s) for i in range(groups)]))
        return got

    packed = mix_in(tokens, cotangent, first_up, second_down, groups, chunks)
    packed = [exchange(a) for a in packed]
    fold = second_up.shape[2] // second_up.shape[1]
    backs, done = [], ()
    for c in range(chunks):
        back, keep, send = feature(packed[c], second_up, first_down, c, line)
        backs.append(exchange(back))
        parts = line_sum(keep, send, line)
        done = settle(parts, line, fold, c, chunks, done)
    red_su, red_fd = done
    result, input_rows, keep, send = mix_out(backs, tokens, cotangent, first_up, second_down, line)
    parts = line_sum(keep, send, line)
    red_fu, red_sd = settle(parts, line, 1, 0, 1, ())
    return (result, input_rows, red_fu, red_su, red_fd, red_sd)


def plain_local(tokens, first_up, second_up, first_down, second_down, cotangent):
    groups = lax.axis_size("block")
    blocks, width = first_up.shape[:2]
    feats = width // groups
    count = tokens.shape[0]
    x = tokens.reshape(count, blocks, width)
    g = cotangent.reshape(count, blocks, width)

    def mul(spec, a, b):
        return jnp.einsum(spec, a, b, preferred_element_type=WIDE)

    def to_feats(array):
        array = array.astype(NARROW).reshape(count, blocks, groups, feats).transpose(0, 2, 1, 3)
        array = lax.all_to_all(array, "block", split_axis=1, concat_axis=1, tiled=True)
        return array.reshape(count, -1, feats)

    def to_blocks(array):
        array = array.astype(NARROW).reshape(count, groups, blocks, feats)
        array = lax.all_to_all(array, "block", split_axis=1, concat_axis=1, tiled=True)
        return array.transpose(0, 2, 1, 3).reshape(count, blocks, width)

    u = to_feats(mul("tbi,bij->tbj", x, first_up))
    d = to_feats(mul("tbi,bji->tbj", g, second_down))
    active, slope = gelu_pair(mul("tbj,jbk->tjk", u, second_up))
    active = active.astype(NARROW)
    v = to_blocks(mul("tjk,jkb->tbj", active, first_down))
    back = (mul("tbj,jkb->tjk", d, first_down) * slope).astype(NARROW)
    e = to_blocks(mul("tjk,jbk->tbj", back, second_up))
    grads = (
        mul("tbi,tbj->bij", x, e),
        mul("tbj,tjk->jbk", u, back),
        mul("tjk,tbj->jkb", active, d),
        mul("tbj,tbi->bji", v, g),
    )
    result = mul("tbj,bji->tbi", v, second_down).astype(NARROW)
    input_rows = mul("tbj,bij->tbi", e, first_up).astype(NARROW)
    reduced = tuple(lax.psum_scatter(a, "dp", scatter_dimension=1, tiled=True) for a in grads)
    return (result.reshape(count, -1), input_rows.reshape(count, -1)) + reduced


def solution(mesh):
    placed = (
        P("dp", "block"),
        P("block", None, None),
        P("block", None, None),
        P("block", None, None),
        P("block", None, None),
        P("dp", "block"),
    )
    groups, n_dp = mesh.shape["block"], mesh.shape["dp"]
    line = n_dp // CORES

    def suits(first_up, second_up, tokens):
        blocks, width, _ = first_up.shape
        blocks = blocks // groups
        hidden = second_up.shape[2]
        return (
            groups & (groups - 1) == 0
            and n_dp % CORES == 0
            and line > 1
            and line & (line - 1) == 0
            and blocks % ROWS == 0
            and width % LANES == 0
            and hidden % width == 0
            and width % (n_dp * ROWS) == 0
            and tokens.shape[0] // n_dp % LANES == 0
        )

    def step(tokens, first_up, second_up, first_down, second_down, cotangent):
        fits = suits(first_up, second_up, tokens)

        def body(*args):
            return (local if fits else plain_local)(*args)

        run = jax.shard_map(
            body,
            mesh=mesh,
            in_specs=placed,
            out_specs=(
                P("dp", "block"),
                P("dp", "block"),
                P("block", "dp", None),
                P("block", "dp", None),
                P("block", "dp", None),
                P("block", "dp", None),
            ),
            check_vma=False,
        )
        return run(tokens, first_up, second_up, first_down, second_down, cotangent)

    return step
```

profile of v0, /device:TPU:0, one launch (start us, length us, event | category | flops | bytes accessed | tf_op | source)
XLA Modules:
  0.0 221.6 jit_solution(3467014830215926846)
XLA Ops:
  0.6 6.3 %mix_in.1 = (bf16[2,8,32,256]{3,2,1,0:T(8,128)(2,1)}, bf16[2,8,32,256]{3,2,1,0:T(8,128)(2,1)}, bf16[2,8,32,256]{3,2,1,0:T(8,128)(2,1)}, bf16[2,8,32,256]{3,2,1,0...) custom-call(bf16[256,4096]{1,0:T(8,128)(2,1)} %rest_16_.1, ...), custom_call_target="tpu_custom_call" | custom-call | flops 536870912 | bytes 8388608 | tf_op jit(solution)/shard_map/mix_in/pallas_call | solution.py:76
  7.0 3.0 %collective-permute-start = (bf16[2,8,32,256]{3,2,1,0:T(8,128)(2,1)}, bf16[2,8,32,256]{3,2,1,0:T(8,128)(2,1)S(1)}, u32[]{:S(2)}, u32[]{:S(2)}) collective-permute-start(bf16[2,8,32,256]{3,2,1,0:T(8,128)(2,1)} %get-tuple-element.61), channel_id=1, source_target_pairs={{0,8},{8,0},{16,24},{24,16},{1,9},{9,1},{17,25},{25,17},{2,10},{10... | collective-permute-start | bytes 786440 | tf_op jit(solution)/shard_map/ppermute | solution.py:307
  10.0 1.5 collective-permute-start.1
  14.0 3.3 %collective-permute-done.rest_1_ = bf16[2,8,32,256]{3,2,1,0:T(8,128)(2,1)S(1)} collective-permute-done((bf16[2,8,32,256]{3,2,1,0:T(8,128)(2,1)}, bf16[2,8,32,256]{3,2,1,0:T(8,128)(2,1)S(1)}, u32[]{:S(2)}, u32[]{:S(2)}) %collective-permute-start) | collective-permute-done | bytes 262176 | tf_op jit(solution)/shard_map/ppermute | solution.py:307
  17.4 3.0 %collective-permute-start.20 = (bf16[2,8,32,256]{3,2,1,0:T(8,128)(2,1)}, bf16[2,8,32,256]{3,2,1,0:T(8,128)(2,1)S(1)}, u32[]{:S(2)}, u32[]{:S(2)}) collective-permute-start(bf16[2,8,32,256]{3,2,1,0:T(8,128)(2,1)} %get-tuple-element.87), channel_id=1, source_target_pairs={{0,24},{8,16},{16,8},{24,0},{1,25},{9,17},{17,9},{25,1},{2,26},{10... | collective-permute-start | bytes 786440 | tf_op jit(solution)/shard_map/ppermute | solution.py:307
  20.9 2.1 collective-permute-done.12.rest_1_
  23.0 3.0 %collective-permute-start.14 = (bf16[2,8,32,256]{3,2,1,0:T(8,128)(2,1)}, bf16[2,8,32,256]{3,2,1,0:T(8,128)(2,1)S(1)}, u32[]{:S(2)}, u32[]{:S(2)}) collective-permute-start(bf16[2,8,32,256]{3,2,1,0:T(8,128)(2,1)} %get-tuple-element.79), channel_id=1, source_target_pairs={{0,24},{8,16},{16,8},{24,0},{1,25},{9,17},{17,9},{25,1},{2,26},{10... | collective-permute-start | bytes 786440 | tf_op jit(solution)/shard_map/ppermute | solution.py:307
  25.9 2.6 %collective-permute-done.18.rest_1_ = bf16[2,8,32,256]{3,2,1,0:T(8,128)(2,1)S(1)} collective-permute-done((bf16[2,8,32,256]{3,2,1,0:T(8,128)(2,1)}, bf16[2,8,32,256]{3,2,1,0:T(8,128)(2,1)S(1)}, u32[]{:S(2)}, u32[]{:S(2)}) %collective-permute-start.18) | collective-permute-done | bytes 262176 | tf_op jit(solution)/shard_map/ppermute | solution.py:307
  28.6 3.0 %collective-permute-start.2 = (bf16[2,8,32,256]{3,2,1,0:T(8,128)(2,1)}, bf16[2,8,32,256]{3,2,1,0:T(8,128)(2,1)S(1)}, u32[]{:S(2)}, u32[]{:S(2)}) collective-permute-start(bf16[2,8,32,256]{3,2,1,0:T(8,128)(2,1)} %get-tuple-element.63), channel_id=1, source_target_pairs={{0,24},{8,16},{16,8},{24,0},{1,25},{9,17},{17,9},{25,1},{2,26},{10... | collective-permute-start | bytes 786440 | tf_op jit(solution)/shard_map/ppermute | solution.py:307
  32.1 3.7 %collective-permute-done.20.rest_3_ = bf16[2,8,32,256]{3,2,1,0:T(8,128)(2,1)S(1)} collective-permute-done((bf16[2,8,32,256]{3,2,1,0:T(8,128)(2,1)}, bf16[2,8,32,256]{3,2,1,0:T(8,128)(2,1)S(1)}, u32[]{:S(2)}, u32[]{:S(2)}) %collective-permute-start.20) | collective-permute-done | bytes 262176 | tf_op jit(solution)/shard_map/ppermute | solution.py:307
  36.5 8.0 %feature.7 = (bf16[2,8,32,256]{3,2,1,0:T(8,128)(2,1)}, bf16[2,8,32,256]{3,2,1,0:T(8,128)(2,1)}, bf16[2,8,32,256]{3,2,1,0:T(8,128)(2,1)}, bf16[2,8,32,256]{3,2,1,...) custom-call(bf16[2,8,32,256]{3,2,1,0:T(8,128)(2,1)} %get-tuple-element.84.rest_0_, ...), custom_call_target="tpu_custom_call" | custom-call | flops 1610612736 | bytes 6291456 | tf_op jit(solution)/shard_map/feature/pallas_call | solution.py:151
  44.5 2.1 collective-permute-done.13.rest_2_
  47.1 3.3 %collective-permute-start.21 = (bf16[2,8,32,256]{3,2,1,0:T(8,128)(2,1)}, bf16[2,8,32,256]{3,2,1,0:T(8,128)(2,1)S(1)}, u32[]{:S(2)}, u32[]{:S(2)}) collective-permute-start(bf16[2,8,32,256]{3,2,1,0:T(8,128)(2,1)} %get-tuple-element.89), channel_id=1, source_target_pairs={{0,8},{8,0},{16,24},{24,16},{1,9},{9,1},{17,25},{25,17},{2,10},{10... | collective-permute-start | bytes 786440 | tf_op jit(solution)/shard_map/ppermute | solution.py:307
  50.5 8.1 %feature.6 = (bf16[2,8,32,256]{3,2,1,0:T(8,128)(2,1)}, bf16[2,8,32,256]{3,2,1,0:T(8,128)(2,1)}, bf16[2,8,32,256]{3,2,1,0:T(8,128)(2,1)}, bf16[2,8,32,256]{3,2,1,...) custom-call(bf16[2,8,32,256]{3,2,1,0:T(8,128)(2,1)} %get-tuple-element.76.rest_0_, ...), custom_call_target="tpu_custom_call" | custom-call | flops 1610612736 | bytes 6291456 | tf_op jit(solution)/shard_map/feature/pallas_call | solution.py:151
  58.7 2.2 collective-permute-start.23
  63.3 2.0 collective-permute-start.17
  65.3 8.0 %feature.5 = (bf16[2,8,32,256]{3,2,1,0:T(8,128)(2,1)}, bf16[2,8,32,256]{3,2,1,0:T(8,128)(2,1)}, bf16[2,8,32,256]{3,2,1,0:T(8,128)(2,1)}, bf16[2,8,32,256]{3,2,1,...) custom-call(bf16[2,8,32,256]{3,2,1,0:T(8,128)(2,1)} %get-tuple-element.68.rest_0_, ...), custom_call_target="tpu_custom_call" | custom-call | flops 1610612736 | bytes 6291456 | tf_op jit(solution)/shard_map/feature/pallas_call | solution.py:151
  76.9 8.1 %feature.4 = (bf16[2,8,32,256]{3,2,1,0:T(8,128)(2,1)}, bf16[2,8,32,256]{3,2,1,0:T(8,128)(2,1)}, bf16[2,8,32,256]{3,2,1,0:T(8,128)(2,1)}, bf16[2,8,32,256]{3,2,1,...) custom-call(bf16[2,8,32,256]{3,2,1,0:T(8,128)(2,1)} %get-tuple-element.60.rest_0_, ...), custom_call_target="tpu_custom_call" | custom-call | flops 1610612736 | bytes 6291456 | tf_op jit(solution)/shard_map/feature/pallas_call | solution.py:151
  85.0 2.0 collective-permute-done.16.rest_10_
  87.6 3.4 %collective-permute-done.10.rest_6_ = bf16[2,8,32,256]{3,2,1,0:T(8,128)(2,1)S(1)} collective-permute-done((bf16[2,8,32,256]{3,2,1,0:T(8,128)(2,1)}, bf16[2,8,32,256]{3,2,1,0:T(8,128)(2,1)S(1)}, u32[]{:S(2)}, u32[]{:S(2)}) %collective-permute-start.10) | collective-permute-done | bytes 262176 | tf_op jit(solution)/shard_map/ppermute | solution.py:307
  91.0 1.5 collective-permute-start.4
  93.8 1.5 collective-permute-done.3.rest_1_
  95.3 9.0 %collective-permute-done.4.rest_2_ = bf16[2,8,32,256]{3,2,1,0:T(8,128)(2,1)S(1)} collective-permute-done((bf16[2,8,32,256]{3,2,1,0:T(8,128)(2,1)}, bf16[2,8,32,256]{3,2,1,0:T(8,128)(2,1)S(1)}, u32[]{:S(2)}, u32[]{:S(2)}) %collective-permute-start.4) | collective-permute-done | bytes 262176 | tf_op jit(solution)/shard_map/ppermute | solution.py:307
  105.1 8.4 %mix_out.1 = (bf16[256,4096]{1,0:T(8,128)(2,1)}, bf16[256,4096]{1,0:T(8,128)(2,1)}, bf16[4,32,32,128]{3,2,1,0:T(8,128)(2,1)}, bf16[4,32,32,128]{3,2,1,0:T(8,128)(2,1)}) custom-call(bf16[2,8,32,256]{3,2,1,0:T(8,128)(2,1)} %get-tuple-element.64.rest_0_, bf16[2,8,32,256]{3,2,1,0:T(8,128)(2,1)} %copy-done.20, bf16[2,8,32,256]{3,2,1,0:T(8,128)(2,1)} %copy-done.28, ...), custom_call_target="tpu_custom_call" | custom-call | flops 1073741824 | bytes 16777216 | tf_op jit(solution)/shard_map/mix_out/pallas_call | solution.py:222
  115.0 2.2 %add_convert_fusion = bf16[2,8,32,512]{3,2,1,0:T(8,128)(2,1)} fusion(bf16[4,8,32,512]{3,2,1,0:T(8,128)(2,1)} %copy-done.4, s32[]{:T(128)S(6)} %select_n.115, bf16[4,8,32,512]{3,2,1,0:T(8,128)(2,1)} %get-tuple-element.103.rest_0_), kind=kLoop, calls=%fused_computation | loop fusion | flops 1048576 | bytes 1572868 | tf_op jit(solution)/shard_map/convert_element_type | solution.py:293
  117.3 1.6 collective-permute-start.37
  118.8 2.1 add_convert_fusion.1
  121.4 2.0 add_convert_fusion.2
  123.4 1.6 collective-permute-start.31
  124.9 2.0 add_convert_fusion.3
  127.4 2.0 add_convert_fusion.4
  129.4 1.6 collective-permute-start.25
  133.6 2.7 %collective-permute-start.38 = (bf16[1,8,32,512]{3,2,1,0:T(8,128)(2,1)S(1)}, bf16[1,8,32,512]{3,2,1,0:T(8,128)(2,1)}, u32[]{:S(2)}, u32[]{:S(2)}) collective-permute-start(bf16[1,8,32,512]{3,2,1,0:T(8,128)(2,1)S(1)} %add_convert_fusion.5), channel_id=1, source_target_pairs={{0,4},{1,5},{2,6},{3,7},{4,0},{5,1},{6,2},{7,3},{8,12},{9,13},{10,... | collective-permute-start | bytes 786440 | tf_op jit(solution)/shard_map/ppermute | solution.py:295
  136.2 13.0 %collective-permute-done.34.rest_2_ = bf16[2,8,32,512]{3,2,1,0:T(8,128)(2,1)} collective-permute-done((bf16[2,8,32,512]{3,2,1,0:T(8,128)(2,1)}, bf16[2,8,32,512]{3,2,1,0:T(8,128)(2,1)}, u32[]{:S(2)}, u32[]{:S(2)}) %collective-permute-start.34) | collective-permute-done | bytes 524320 | tf_op jit(solution)/shard_map/ppermute | solution.py:295
  150.4 1.7 collective-permute-start.35
  152.1 14.0 %collective-permute-done.31.rest_2_ = bf16[2,8,32,512]{3,2,1,0:T(8,128)(2,1)} collective-permute-done((bf16[2,8,32,512]{3,2,1,0:T(8,128)(2,1)}, bf16[2,8,32,512]{3,2,1,0:T(8,128)(2,1)}, u32[]{:S(2)}, u32[]{:S(2)}) %collective-permute-start.31) | collective-permute-done | bytes 524320 | tf_op jit(solution)/shard_map/ppermute | solution.py:295
  167.2 1.7 collective-permute-start.32
  169.0 14.0 %collective-permute-done.28.rest_2_ = bf16[2,8,32,512]{3,2,1,0:T(8,128)(2,1)} collective-permute-done((bf16[2,8,32,512]{3,2,1,0:T(8,128)(2,1)}, bf16[2,8,32,512]{3,2,1,0:T(8,128)(2,1)}, u32[]{:S(2)}, u32[]{:S(2)}) %collective-permute-start.28) | collective-permute-done | bytes 524320 | tf_op jit(solution)/shard_map/ppermute | solution.py:295
  184.1 1.7 collective-permute-start.29
  185.8 7.6 %collective-permute-done.25.rest_2_ = bf16[2,32,32,128]{3,2,1,0:T(8,128)(2,1)} collective-permute-done((bf16[2,32,32,128]{3,2,1,0:T(8,128)(2,1)}, bf16[2,32,32,128]{3,2,1,0:T(8,128)(2,1)}, u32[]{:S(2)}, u32[]{:S(2)}) %collective-permute-start.25) | collective-permute-done | bytes 524320 | tf_op jit(solution)/shard_map/ppermute | solution.py:295
  194.6 1.7 collective-permute-start.26
  196.3 3.3 %settle.6 = (f32[32,16,512]{2,1,0:T(8,128)}, f32[32,64,128]{2,1,0:T(8,128)}) custom-call(bf16[4,8,32,512]{3,2,1,0:T(8,128)(2,1)} %get-tuple-element.103.rest_0_, bf16[4,8,32,512]{3,2,1,0:T(8,128)(2,1)} %copy-done.4, bf16[2,8,32,512]{3,2,1,0:T(8,128)(2,1)} %collective-permute-done.37.rest_2_, bf16[1,8,32,512]{3,2,1,0:T(8,128)(2,1)} %collective-permute-done.38.rest_3_), custom_call_target="tpu_custom_call" | custom-call | flops 524288 | bytes 1572864 | tf_op jit(solution)/shard_map/settle/pallas_call | solution.py:267
  200.3 3.2 %settle.7 = (f32[32,16,512]{2,1,0:T(8,128)}, f32[32,64,128]{2,1,0:T(8,128)}) custom-call(bf16[4,8,32,512]{3,2,1,0:T(8,128)(2,1)} %get-tuple-element.101.rest_0_, bf16[4,8,32,512]{3,2,1,0:T(8,128)(2,1)} %collective-permute-done.33.rest_1_, bf16[2,8,32,512]{3,2,1,0:T(8,128)(2,1)} %collective-permute-done.34.rest_2_, ...), custom_call_target="tpu_custom_call", output_to_operand_aliasing={{0}: (4, {}), {1}: (5, {})} | custom-call | flops 524288 | bytes 1572864 | tf_op jit(solution)/shard_map/settle/pallas_call | solution.py:267
  204.3 3.2 %settle.8 = (f32[32,16,512]{2,1,0:T(8,128)}, f32[32,64,128]{2,1,0:T(8,128)}) custom-call(bf16[4,8,32,512]{3,2,1,0:T(8,128)(2,1)} %get-tuple-element.99.rest_0_, bf16[4,8,32,512]{3,2,1,0:T(8,128)(2,1)} %collective-permute-done.30.rest_1_, bf16[2,8,32,512]{3,2,1,0:T(8,128)(2,1)} %collective-permute-done.31.rest_2_, ...), custom_call_target="tpu_custom_call", output_to_operand_aliasing={{0}: (4, {}), {1}: (5, {})} | custom-call | flops 524288 | bytes 1572864 | tf_op jit(solution)/shard_map/settle/pallas_call | solution.py:267
  207.5 4.6 %collective-permute-done.29.rest_3_ = bf16[1,8,32,512]{3,2,1,0:T(8,128)(2,1)S(1)} collective-permute-done((bf16[1,8,32,512]{3,2,1,0:T(8,128)(2,1)S(1)}, bf16[1,8,32,512]{3,2,1,0:T(8,128)(2,1)S(1)}, u32[]{:S(2)}, u32[]{:S(2)}) %collective-permute-start.29) | collective-permute-done | bytes 262176 | tf_op jit(solution)/shard_map/ppermute | solution.py:295
  212.8 3.2 %settle.9 = (f32[32,16,512]{2,1,0:T(8,128)}, f32[32,64,128]{2,1,0:T(8,128)}) custom-call(bf16[4,8,32,512]{3,2,1,0:T(8,128)(2,1)} %get-tuple-element.97.rest_0_, bf16[4,8,32,512]{3,2,1,0:T(8,128)(2,1)} %collective-permute-done.27.rest_1_, bf16[2,8,32,512]{3,2,1,0:T(8,128)(2,1)} %collective-permute-done.28.rest_2_, ...), custom_call_target="tpu_custom_call", output_to_operand_aliasing={{0}: (4, {}), {1}: (5, {})} | custom-call | flops 524288 | bytes 1572864 | tf_op jit(solution)/shard_map/settle/pallas_call | solution.py:267
  216.1 1.6 collective-permute-done.26.rest_3_
  218.4 3.2 %settle.5 = (f32[32,16,128]{2,1,0:T(8,128)}, f32[32,16,128]{2,1,0:T(8,128)}) custom-call(bf16[4,32,32,128]{3,2,1,0:T(8,128)(2,1)} %get-tuple-element.94.rest_0_, bf16[4,32,32,128]{3,2,1,0:T(8,128)(2,1)} %collective-permute-done.24.rest_1_, bf16[2,32,32,128]{3,2,1,0:T(8,128)(2,1)} %collective-permute-done.25.rest_2_, bf16[1,32,32,128]{3,2,1,0:T(8,128)(2,1)} %copy-done.32), custom_call_target="tpu_custom_call" | custom-call | flops 524288 | bytes 1572864 | tf_op jit(solution)/shard_map/settle/pallas_call | solution.py:267
  (123 shorter events, 26.1 us)
Async XLA Ops:
  7.0 10.4 %collective-permute-start = (bf16[2,8,32,256]{3,2,1,0:T(8,128)(2,1)}, bf16[2,8,32,256]{3,2,1,0:T(8,128)(2,1)S(1)}, u32[]{:S(2)}, u32[]{:S(2)}) collective-permute-start(bf16[2,8,32,256]{3,2,1,0:T(8,128)(2,1)} %get-tuple-element.61), channel_id=1, source_target_pairs={{0,8},{8,0},{16,24},{24,16},{1,9},{9,1},{17,25},{25,17},{2,10},{10... | collective-permute-start | bytes 786440 | tf_op jit(solution)/shard_map/ppermute | solution.py:307
  10.0 10.3 %collective-permute-start.1 = (bf16[2,8,32,256]{3,2,1,0:T(8,128)(2,1)}, bf16[2,8,32,256]{3,2,1,0:T(8,128)(2,1)S(1)}, u32[]{:S(2)}, u32[]{:S(2)}) collective-permute-start(bf16[2,8,32,256]{3,2,1,0:T(8,128)(2,1)} %get-tuple-element.62), channel_id=1, source_target_pairs={{0,16},{8,24},{16,0},{24,8},{1,17},{9,25},{17,1},{25,9},{2,18},{10... | collective-permute-start | bytes 786440 | tf_op jit(solution)/shard_map/ppermute | solution.py:307
  11.5 11.5 %collective-permute-start.12 = (bf16[2,8,32,256]{3,2,1,0:T(8,128)(2,1)}, bf16[2,8,32,256]{3,2,1,0:T(8,128)(2,1)S(1)}, u32[]{:S(2)}, u32[]{:S(2)}) collective-permute-start(bf16[2,8,32,256]{3,2,1,0:T(8,128)(2,1)} %get-tuple-element.77), channel_id=1, source_target_pairs={{0,8},{8,0},{16,24},{24,16},{1,9},{9,1},{17,25},{25,17},{2,10},{10... | collective-permute-start | bytes 786440 | tf_op jit(solution)/shard_map/ppermute | solution.py:307
  12.0 16.5 %collective-permute-start.18 = (bf16[2,8,32,256]{3,2,1,0:T(8,128)(2,1)}, bf16[2,8,32,256]{3,2,1,0:T(8,128)(2,1)S(1)}, u32[]{:S(2)}, u32[]{:S(2)}) collective-permute-start(bf16[2,8,32,256]{3,2,1,0:T(8,128)(2,1)} %get-tuple-element.85), channel_id=1, source_target_pairs={{0,8},{8,0},{16,24},{24,16},{1,9},{9,1},{17,25},{25,17},{2,10},{10... | collective-permute-start | bytes 786440 | tf_op jit(solution)/shard_map/ppermute | solution.py:307
  13.5 18.0 %collective-permute-start.19 = (bf16[2,8,32,256]{3,2,1,0:T(8,128)(2,1)}, bf16[2,8,32,256]{3,2,1,0:T(8,128)(2,1)S(1)}, u32[]{:S(2)}, u32[]{:S(2)}) collective-permute-start(bf16[2,8,32,256]{3,2,1,0:T(8,128)(2,1)} %get-tuple-element.86), channel_id=1, source_target_pairs={{0,16},{8,24},{16,0},{24,8},{1,17},{9,25},{17,1},{25,9},{2,18},{10... | collective-permute-start | bytes 786440 | tf_op jit(solution)/shard_map/ppermute | solution.py:307
  17.4 27.1 %copy-start.5 = (bf16[2,8,32,256]{3,2,1,0:T(8,128)(2,1)}, bf16[2,8,32,256]{3,2,1,0:T(8,128)(2,1)S(1)}, u32[]{:S(2)}) copy-start(bf16[2,8,32,256]{3,2,1,0:T(8,128)(2,1)S(1)} %collective-permute-done.rest_1_) | copy-start | bytes 786436
  17.4 18.4 %collective-permute-start.20 = (bf16[2,8,32,256]{3,2,1,0:T(8,128)(2,1)}, bf16[2,8,32,256]{3,2,1,0:T(8,128)(2,1)S(1)}, u32[]{:S(2)}, u32[]{:S(2)}) collective-permute-start(bf16[2,8,32,256]{3,2,1,0:T(8,128)(2,1)} %get-tuple-element.87), channel_id=1, source_target_pairs={{0,24},{8,16},{16,8},{24,0},{1,25},{9,17},{17,9},{25,1},{2,26},{10... | collective-permute-start | bytes 786440 | tf_op jit(solution)/shard_map/ppermute | solution.py:307
  20.3 24.1 %copy-start.6 = (bf16[2,8,32,256]{3,2,1,0:T(8,128)(2,1)}, bf16[2,8,32,256]{3,2,1,0:T(8,128)(2,1)S(1)}, u32[]{:S(2)}) copy-start(bf16[2,8,32,256]{3,2,1,0:T(8,128)(2,1)S(1)} %collective-permute-done.1.rest_2_) | copy-start | bytes 786436
  20.3 26.3 %collective-permute-start.13 = (bf16[2,8,32,256]{3,2,1,0:T(8,128)(2,1)}, bf16[2,8,32,256]{3,2,1,0:T(8,128)(2,1)S(1)}, u32[]{:S(2)}, u32[]{:S(2)}) collective-permute-start(bf16[2,8,32,256]{3,2,1,0:T(8,128)(2,1)} %get-tuple-element.78), channel_id=1, source_target_pairs={{0,16},{8,24},{16,0},{24,8},{1,17},{9,25},{17,1},{25,9},{2,18},{10... | collective-permute-start | bytes 786440 | tf_op jit(solution)/shard_map/ppermute | solution.py:307
  23.0 21.5 %copy-start.17 = (bf16[2,8,32,256]{3,2,1,0:T(8,128)(2,1)}, bf16[2,8,32,256]{3,2,1,0:T(8,128)(2,1)S(1)}, u32[]{:S(2)}) copy-start(bf16[2,8,32,256]{3,2,1,0:T(8,128)(2,1)S(1)} %collective-permute-done.12.rest_1_) | copy-start | bytes 786436
  23.0 24.1 %collective-permute-start.14 = (bf16[2,8,32,256]{3,2,1,0:T(8,128)(2,1)}, bf16[2,8,32,256]{3,2,1,0:T(8,128)(2,1)S(1)}, u32[]{:S(2)}, u32[]{:S(2)}) collective-permute-start(bf16[2,8,32,256]{3,2,1,0:T(8,128)(2,1)} %get-tuple-element.79), channel_id=1, source_target_pairs={{0,24},{8,16},{16,8},{24,0},{1,25},{9,17},{17,9},{25,1},{2,26},{10... | collective-permute-start | bytes 786440 | tf_op jit(solution)/shard_map/ppermute | solution.py:307
  28.6 29.9 %collective-permute-start.2 = (bf16[2,8,32,256]{3,2,1,0:T(8,128)(2,1)}, bf16[2,8,32,256]{3,2,1,0:T(8,128)(2,1)S(1)}, u32[]{:S(2)}, u32[]{:S(2)}) collective-permute-start(bf16[2,8,32,256]{3,2,1,0:T(8,128)(2,1)} %get-tuple-element.63), channel_id=1, source_target_pairs={{0,24},{8,16},{16,8},{24,0},{1,25},{9,17},{17,9},{25,1},{2,26},{10... | collective-permute-start | bytes 786440 | tf_op jit(solution)/shard_map/ppermute | solution.py:307
  31.6 27.1 %collective-permute-start.6 = (bf16[2,8,32,256]{3,2,1,0:T(8,128)(2,1)}, bf16[2,8,32,256]{3,2,1,0:T(8,128)(2,1)S(1)}, u32[]{:S(2)}, u32[]{:S(2)}) collective-permute-start(bf16[2,8,32,256]{3,2,1,0:T(8,128)(2,1)} %get-tuple-element.69), channel_id=1, source_target_pairs={{0,8},{8,0},{16,24},{24,16},{1,9},{9,1},{17,25},{25,17},{2,10},{10... | collective-permute-start | bytes 786440 | tf_op jit(solution)/shard_map/ppermute | solution.py:307
  35.8 25.0 %collective-permute-start.7 = (bf16[2,8,32,256]{3,2,1,0:T(8,128)(2,1)}, bf16[2,8,32,256]{3,2,1,0:T(8,128)(2,1)S(1)}, u32[]{:S(2)}, u32[]{:S(2)}) collective-permute-start(bf16[2,8,32,256]{3,2,1,0:T(8,128)(2,1)} %get-tuple-element.70), channel_id=1, source_target_pairs={{0,16},{8,24},{16,0},{24,8},{1,17},{9,25},{17,1},{25,9},{2,18},{10... | collective-permute-start | bytes 786440 | tf_op jit(solution)/shard_map/ppermute | solution.py:307
  46.6 15.6 %collective-permute-start.8 = (bf16[2,8,32,256]{3,2,1,0:T(8,128)(2,1)S(1)}, bf16[2,8,32,256]{3,2,1,0:T(8,128)(2,1)S(1)}, u32[]{:S(2)}, u32[]{:S(2)}) collective-permute-start(bf16[2,8,32,256]{3,2,1,0:T(8,128)(2,1)S(1)} %copy-done.33), channel_id=1, source_target_pairs={{0,24},{8,16},{16,8},{24,0},{1,25},{9,17},{17,9},{25,1},{2,26},{10... | collective-permute-start | bytes 786440 | tf_op jit(solution)/shard_map/ppermute | solution.py:307
  47.1 16.1 %collective-permute-start.21 = (bf16[2,8,32,256]{3,2,1,0:T(8,128)(2,1)}, bf16[2,8,32,256]{3,2,1,0:T(8,128)(2,1)S(1)}, u32[]{:S(2)}, u32[]{:S(2)}) collective-permute-start(bf16[2,8,32,256]{3,2,1,0:T(8,128)(2,1)} %get-tuple-element.89), channel_id=1, source_target_pairs={{0,8},{8,0},{16,24},{24,16},{1,9},{9,1},{17,25},{25,17},{2,10},{10... | collective-permute-start | bytes 786440 | tf_op jit(solution)/shard_map/ppermute | solution.py:307
  58.5 14.7 %copy-start.9 = (bf16[2,8,32,256]{3,2,1,0:T(8,128)(2,1)}, bf16[2,8,32,256]{3,2,1,0:T(8,128)(2,1)S(1)}, u32[]{:S(2)}) copy-start(bf16[2,8,32,256]{3,2,1,0:T(8,128)(2,1)S(1)} %collective-permute-done.2.rest_3_) | copy-start | bytes 786436
  58.5 14.7 %collective-permute-start.22 = (bf16[2,8,32,256]{3,2,1,0:T(8,128)(2,1)S(1)}, bf16[2,8,32,256]{3,2,1,0:T(8,128)(2,1)S(1)}, u32[]{:S(2)}, u32[]{:S(2)}) collective-permute-start(bf16[2,8,32,256]{3,2,1,0:T(8,128)(2,1)S(1)} %copy-done.35), channel_id=1, source_target_pairs={{0,16},{8,24},{16,0},{24,8},{1,17},{9,25},{17,1},{25,9},{2,18},{10... | collective-permute-start | bytes 786440 | tf_op jit(solution)/shard_map/ppermute | solution.py:307
  58.7 15.3 %collective-permute-start.23 = (bf16[2,8,32,256]{3,2,1,0:T(8,128)(2,1)S(1)}, bf16[2,8,32,256]{3,2,1,0:T(8,128)(2,1)S(1)}, u32[]{:S(2)}, u32[]{:S(2)}) collective-permute-start(bf16[2,8,32,256]{3,2,1,0:T(8,128)(2,1)S(1)} %copy-done.34), channel_id=1, source_target_pairs={{0,24},{8,16},{16,8},{24,0},{1,25},{9,17},{17,9},{25,1},{2,26},{10... | collective-permute-start | bytes 786440 | tf_op jit(solution)/shard_map/ppermute | solution.py:307
  60.8 14.6 %collective-permute-start.15 = (bf16[2,8,32,256]{3,2,1,0:T(8,128)(2,1)}, bf16[2,8,32,256]{3,2,1,0:T(8,128)(2,1)S(1)}, u32[]{:S(2)}, u32[]{:S(2)}) collective-permute-start(bf16[2,8,32,256]{3,2,1,0:T(8,128)(2,1)} %get-tuple-element.81), channel_id=1, source_target_pairs={{0,8},{8,0},{16,24},{24,16},{1,9},{9,1},{17,25},{25,17},{2,10},{10... | collective-permute-start | bytes 786440 | tf_op jit(solution)/shard_map/ppermute | solution.py:307
  62.2 24.8 %collective-permute-start.16 = (bf16[2,8,32,256]{3,2,1,0:T(8,128)(2,1)}, bf16[2,8,32,256]{3,2,1,0:T(8,128)(2,1)S(1)}, u32[]{:S(2)}, u32[]{:S(2)}) collective-permute-start(bf16[2,8,32,256]{3,2,1,0:T(8,128)(2,1)} %get-tuple-element.82), channel_id=1, source_target_pairs={{0,16},{8,24},{16,0},{24,8},{1,17},{9,25},{17,1},{25,9},{2,18},{10... | collective-permute-start | bytes 786440 | tf_op jit(solution)/shard_map/ppermute | solution.py:307
  63.3 24.3 %collective-permute-start.17 = (bf16[2,8,32,256]{3,2,1,0:T(8,128)(2,1)}, bf16[2,8,32,256]{3,2,1,0:T(8,128)(2,1)S(1)}, u32[]{:S(2)}, u32[]{:S(2)}) collective-permute-start(bf16[2,8,32,256]{3,2,1,0:T(8,128)(2,1)} %get-tuple-element.83), channel_id=1, source_target_pairs={{0,24},{8,16},{16,8},{24,0},{1,25},{9,17},{17,9},{25,1},{2,26},{10... | collective-permute-start | bytes 786440 | tf_op jit(solution)/shard_map/ppermute | solution.py:307
  73.3 17.7 %collective-permute-start.10 = (bf16[2,8,32,256]{3,2,1,0:T(8,128)(2,1)}, bf16[2,8,32,256]{3,2,1,0:T(8,128)(2,1)S(1)}, u32[]{:S(2)}, u32[]{:S(2)}) collective-permute-start(bf16[2,8,32,256]{3,2,1,0:T(8,128)(2,1)} %get-tuple-element.74), channel_id=1, source_target_pairs={{0,16},{8,24},{16,0},{24,8},{1,17},{9,25},{17,1},{25,9},{2,18},{10... | collective-permute-start | bytes 786440 | tf_op jit(solution)/shard_map/ppermute | solution.py:307
  73.9 18.6 %collective-permute-start.11 = (bf16[2,8,32,256]{3,2,1,0:T(8,128)(2,1)}, bf16[2,8,32,256]{3,2,1,0:T(8,128)(2,1)S(1)}, u32[]{:S(2)}, u32[]{:S(2)}) collective-permute-start(bf16[2,8,32,256]{3,2,1,0:T(8,128)(2,1)} %get-tuple-element.75), channel_id=1, source_target_pairs={{0,24},{8,16},{16,8},{24,0},{1,25},{9,17},{17,9},{25,1},{2,26},{10... | collective-permute-start | bytes 786440 | tf_op jit(solution)/shard_map/ppermute | solution.py:307
  75.4 17.1 %collective-permute-start.9 = (bf16[2,8,32,256]{3,2,1,0:T(8,128)(2,1)}, bf16[2,8,32,256]{3,2,1,0:T(8,128)(2,1)S(1)}, u32[]{:S(2)}, u32[]{:S(2)}) collective-permute-start(bf16[2,8,32,256]{3,2,1,0:T(8,128)(2,1)} %get-tuple-element.73), channel_id=1, source_target_pairs={{0,8},{8,0},{16,24},{24,16},{1,9},{9,1},{17,25},{25,17},{2,10},{10... | collective-permute-start | bytes 786440 | tf_op jit(solution)/shard_map/ppermute | solution.py:307
  87.0 17.4 %copy-start.12 = (bf16[2,8,32,256]{3,2,1,0:T(8,128)(2,1)}, bf16[2,8,32,256]{3,2,1,0:T(8,128)(2,1)S(1)}, u32[]{:S(2)}) copy-start(bf16[2,8,32,256]{3,2,1,0:T(8,128)(2,1)S(1)} %collective-permute-done.16.rest_10_) | copy-start | bytes 786436
  87.0 8.3 %collective-permute-start.3 = (bf16[2,8,32,256]{3,2,1,0:T(8,128)(2,1)}, bf16[2,8,32,256]{3,2,1,0:T(8,128)(2,1)S(1)}, u32[]{:S(2)}, u32[]{:S(2)}) collective-permute-start(bf16[2,8,32,256]{3,2,1,0:T(8,128)(2,1)} %get-tuple-element.65), channel_id=1, source_target_pairs={{0,8},{8,0},{16,24},{24,16},{1,9},{9,1},{17,25},{25,17},{2,10},{10... | collective-permute-start | bytes 786440 | tf_op jit(solution)/shard_map/ppermute | solution.py:307
  87.6 16.7 %copy-start.13 = (bf16[2,8,32,256]{3,2,1,0:T(8,128)(2,1)}, bf16[2,8,32,256]{3,2,1,0:T(8,128)(2,1)S(1)}, u32[]{:S(2)}) copy-start(bf16[2,8,32,256]{3,2,1,0:T(8,128)(2,1)S(1)} %collective-permute-done.17.rest_11_) | copy-start | bytes 786436
  87.6 26.4 %collective-permute-start.36 = (bf16[4,8,32,512]{3,2,1,0:T(8,128)(2,1)}, bf16[4,8,32,512]{3,2,1,0:T(8,128)(2,1)S(1)}, u32[]{:S(2)}, u32[]{:S(2)}) collective-permute-start(bf16[4,8,32,512]{3,2,1,0:T(8,128)(2,1)} %get-tuple-element.104), channel_id=1, source_target_pairs={{0,1},{1,0},{2,3},{3,2},{4,5},{5,4},{6,7},{7,6},{8,9},{9,8},{10,11... | collective-permute-start | bytes 3145736 | tf_op jit(solution)/shard_map/ppermute | solution.py:282
  91.0 13.4 %copy-start.14 = (bf16[2,8,32,256]{3,2,1,0:T(8,128)(2,1)}, bf16[2,8,32,256]{3,2,1,0:T(8,128)(2,1)S(1)}, u32[]{:S(2)}) copy-start(bf16[2,8,32,256]{3,2,1,0:T(8,128)(2,1)S(1)} %collective-permute-done.10.rest_6_) | copy-start | bytes 786436
  91.0 13.3 %collective-permute-start.4 = (bf16[2,8,32,256]{3,2,1,0:T(8,128)(2,1)}, bf16[2,8,32,256]{3,2,1,0:T(8,128)(2,1)S(1)}, u32[]{:S(2)}, u32[]{:S(2)}) collective-permute-start(bf16[2,8,32,256]{3,2,1,0:T(8,128)(2,1)} %get-tuple-element.66), channel_id=1, source_target_pairs={{0,16},{8,24},{16,0},{24,8},{1,17},{9,25},{17,1},{25,9},{2,18},{10... | collective-permute-start | bytes 786440 | tf_op jit(solution)/shard_map/ppermute | solution.py:307
  92.5 11.9 %copy-start.15 = (bf16[2,8,32,256]{3,2,1,0:T(8,128)(2,1)}, bf16[2,8,32,256]{3,2,1,0:T(8,128)(2,1)S(1)}, u32[]{:S(2)}) copy-start(bf16[2,8,32,256]{3,2,1,0:T(8,128)(2,1)S(1)} %collective-permute-done.11.rest_7_) | copy-start | bytes 786436
  92.5 26.3 %collective-permute-start.33 = (bf16[4,8,32,512]{3,2,1,0:T(8,128)(2,1)}, bf16[4,8,32,512]{3,2,1,0:T(8,128)(2,1)}, u32[]{:S(2)}, u32[]{:S(2)}) collective-permute-start(bf16[4,8,32,512]{3,2,1,0:T(8,128)(2,1)} %get-tuple-element.102), channel_id=1, source_target_pairs={{0,1},{1,0},{2,3},{3,2},{4,5},{5,4},{6,7},{7,6},{8,9},{9,8},{10,11... | collective-permute-start | bytes 3145736 | tf_op jit(solution)/shard_map/ppermute | solution.py:282
  92.5 11.8 %collective-permute-start.5 = (bf16[2,8,32,256]{3,2,1,0:T(8,128)(2,1)}, bf16[2,8,32,256]{3,2,1,0:T(8,128)(2,1)S(1)}, u32[]{:S(2)}, u32[]{:S(2)}) collective-permute-start(bf16[2,8,32,256]{3,2,1,0:T(8,128)(2,1)} %get-tuple-element.67), channel_id=1, source_target_pairs={{0,24},{8,16},{16,8},{24,0},{1,25},{9,17},{17,9},{25,1},{2,26},{10... | collective-permute-start | bytes 786440 | tf_op jit(solution)/shard_map/ppermute | solution.py:307
  95.3 26.0 %collective-permute-start.30 = (bf16[4,8,32,512]{3,2,1,0:T(8,128)(2,1)}, bf16[4,8,32,512]{3,2,1,0:T(8,128)(2,1)}, u32[]{:S(2)}, u32[]{:S(2)}) collective-permute-start(bf16[4,8,32,512]{3,2,1,0:T(8,128)(2,1)} %get-tuple-element.100), channel_id=1, source_target_pairs={{0,1},{1,0},{2,3},{3,2},{4,5},{5,4},{6,7},{7,6},{8,9},{9,8},{10,11... | collective-permute-start | bytes 3145736 | tf_op jit(solution)/shard_map/ppermute | solution.py:282
  104.3 20.6 %collective-permute-start.27 = (bf16[4,8,32,512]{3,2,1,0:T(8,128)(2,1)}, bf16[4,8,32,512]{3,2,1,0:T(8,128)(2,1)}, u32[]{:S(2)}, u32[]{:S(2)}) collective-permute-start(bf16[4,8,32,512]{3,2,1,0:T(8,128)(2,1)} %get-tuple-element.98), channel_id=1, source_target_pairs={{0,1},{1,0},{2,3},{3,2},{4,5},{5,4},{6,7},{7,6},{8,9},{9,8},{10,11... | collective-permute-start | bytes 3145736 | tf_op jit(solution)/shard_map/ppermute | solution.py:282
  105.1 13.7 %copy-start.2 = (bf16[4,8,32,512]{3,2,1,0:T(8,128)(2,1)S(1)}, bf16[4,8,32,512]{3,2,1,0:T(8,128)(2,1)}, u32[]{:S(2)}) copy-start(bf16[4,8,32,512]{3,2,1,0:T(8,128)(2,1)} %get-tuple-element.101.rest_0_) | copy-start | bytes 3145732
  113.5 13.9 %collective-permute-start.24 = (bf16[4,32,32,128]{3,2,1,0:T(8,128)(2,1)}, bf16[4,32,32,128]{3,2,1,0:T(8,128)(2,1)}, u32[]{:S(2)}, u32[]{:S(2)}) collective-permute-start(bf16[4,32,32,128]{3,2,1,0:T(8,128)(2,1)} %get-tuple-element.95), channel_id=1, source_target_pairs={{0,1},{1,0},{2,3},{3,2},{4,5},{5,4},{6,7},{7,6},{8,9},{9,8},{10,11... | collective-permute-start | bytes 3145736 | tf_op jit(solution)/shard_map/ppermute | solution.py:282
  117.3 15.1 %collective-permute-start.37 = (bf16[2,8,32,512]{3,2,1,0:T(8,128)(2,1)}, bf16[2,8,32,512]{3,2,1,0:T(8,128)(2,1)}, u32[]{:S(2)}, u32[]{:S(2)}) collective-permute-start(bf16[2,8,32,512]{3,2,1,0:T(8,128)(2,1)} %add_convert_fusion), channel_id=1, source_target_pairs={{0,2},{1,3},{2,0},{3,1},{4,6},{5,7},{6,4},{7,5},{8,10},{9,11},{10,... | collective-permute-start | bytes 1572872 | tf_op jit(solution)/shard_map/ppermute | solution.py:295
  120.9 28.3 %collective-permute-start.34 = (bf16[2,8,32,512]{3,2,1,0:T(8,128)(2,1)}, bf16[2,8,32,512]{3,2,1,0:T(8,128)(2,1)}, u32[]{:S(2)}, u32[]{:S(2)}) collective-permute-start(bf16[2,8,32,512]{3,2,1,0:T(8,128)(2,1)} %add_convert_fusion.1), channel_id=1, source_target_pairs={{0,2},{1,3},{2,0},{3,1},{4,6},{5,7},{6,4},{7,5},{8,10},{9,11},{10,... | collective-permute-start | bytes 1572872 | tf_op jit(solution)/shard_map/ppermute | solution.py:295
  123.4 42.7 %collective-permute-start.31 = (bf16[2,8,32,512]{3,2,1,0:T(8,128)(2,1)}, bf16[2,8,32,512]{3,2,1,0:T(8,128)(2,1)}, u32[]{:S(2)}, u32[]{:S(2)}) collective-permute-start(bf16[2,8,32,512]{3,2,1,0:T(8,128)(2,1)} %add_convert_fusion.2), channel_id=1, source_target_pairs={{0,2},{1,3},{2,0},{3,1},{4,6},{5,7},{6,4},{7,5},{8,10},{9,11},{10,... | collective-permute-start | bytes 1572872 | tf_op jit(solution)/shard_map/ppermute | solution.py:295
  126.9 56.0 %collective-permute-start.28 = (bf16[2,8,32,512]{3,2,1,0:T(8,128)(2,1)}, bf16[2,8,32,512]{3,2,1,0:T(8,128)(2,1)}, u32[]{:S(2)}, u32[]{:S(2)}) collective-permute-start(bf16[2,8,32,512]{3,2,1,0:T(8,128)(2,1)} %add_convert_fusion.3), channel_id=1, source_target_pairs={{0,2},{1,3},{2,0},{3,1},{4,6},{5,7},{6,4},{7,5},{8,10},{9,11},{10,... | collective-permute-start | bytes 1572872 | tf_op jit(solution)/shard_map/ppermute | solution.py:295
  129.4 64.0 %collective-permute-start.25 = (bf16[2,32,32,128]{3,2,1,0:T(8,128)(2,1)}, bf16[2,32,32,128]{3,2,1,0:T(8,128)(2,1)}, u32[]{:S(2)}, u32[]{:S(2)}) collective-permute-start(bf16[2,32,32,128]{3,2,1,0:T(8,128)(2,1)} %add_convert_fusion.4), channel_id=1, source_target_pairs={{0,2},{1,3},{2,0},{3,1},{4,6},{5,7},{6,4},{7,5},{8,10},{9,11},{10,... | collective-permute-start | bytes 1572872 | tf_op jit(solution)/shard_map/ppermute | solution.py:295
  133.6 62.8 %collective-permute-start.38 = (bf16[1,8,32,512]{3,2,1,0:T(8,128)(2,1)S(1)}, bf16[1,8,32,512]{3,2,1,0:T(8,128)(2,1)}, u32[]{:S(2)}, u32[]{:S(2)}) collective-permute-start(bf16[1,8,32,512]{3,2,1,0:T(8,128)(2,1)S(1)} %add_convert_fusion.5), channel_id=1, source_target_pairs={{0,4},{1,5},{2,6},{3,7},{4,0},{5,1},{6,2},{7,3},{8,12},{9,13},{10,... | collective-permute-start | bytes 786440 | tf_op jit(solution)/shard_map/ppermute | solution.py:295
  150.4 49.3 %collective-permute-start.35 = (bf16[1,8,32,512]{3,2,1,0:T(8,128)(2,1)S(1)}, bf16[1,8,32,512]{3,2,1,0:T(8,128)(2,1)S(1)}, u32[]{:S(2)}, u32[]{:S(2)}) collective-permute-start(bf16[1,8,32,512]{3,2,1,0:T(8,128)(2,1)S(1)} %add_convert_fusion.6), channel_id=1, source_target_pairs={{0,4},{1,5},{2,6},{3,7},{4,0},{5,1},{6,2},{7,3},{8,12},{9,13},{10,... | collective-permute-start | bytes 786440 | tf_op jit(solution)/shard_map/ppermute | solution.py:295
  167.2 36.4 %collective-permute-start.32 = (bf16[1,8,32,512]{3,2,1,0:T(8,128)(2,1)S(1)}, bf16[1,8,32,512]{3,2,1,0:T(8,128)(2,1)S(1)}, u32[]{:S(2)}, u32[]{:S(2)}) collective-permute-start(bf16[1,8,32,512]{3,2,1,0:T(8,128)(2,1)S(1)} %add_convert_fusion.7), channel_id=1, source_target_pairs={{0,4},{1,5},{2,6},{3,7},{4,0},{5,1},{6,2},{7,3},{8,12},{9,13},{10,... | collective-permute-start | bytes 786440 | tf_op jit(solution)/shard_map/ppermute | solution.py:295
  184.1 28.1 %collective-permute-start.29 = (bf16[1,8,32,512]{3,2,1,0:T(8,128)(2,1)S(1)}, bf16[1,8,32,512]{3,2,1,0:T(8,128)(2,1)S(1)}, u32[]{:S(2)}, u32[]{:S(2)}) collective-permute-start(bf16[1,8,32,512]{3,2,1,0:T(8,128)(2,1)S(1)} %add_convert_fusion.8), channel_id=1, source_target_pairs={{0,4},{1,5},{2,6},{3,7},{4,0},{5,1},{6,2},{7,3},{8,12},{9,13},{10,... | collective-permute-start | bytes 786440 | tf_op jit(solution)/shard_map/ppermute | solution.py:295
  194.6 23.1 %collective-permute-start.26 = (bf16[1,32,32,128]{3,2,1,0:T(8,128)(2,1)S(1)}, bf16[1,32,32,128]{3,2,1,0:T(8,128)(2,1)S(1)}, u32[]{:S(2)}, u32[]{:S(2)}) collective-permute-start(bf16[1,32,32,128]{3,2,1,0:T(8,128)(2,1)S(1)} %add_convert_fusion.9), channel_id=1, source_target_pairs={{0,4},{1,5},{2,6},{3,7},{4,0},{5,1},{6,2},{7,3},{8,12},{9,13},{10,... | collective-permute-start | bytes 786440 | tf_op jit(solution)/shard_map/ppermute | solution.py:295
  (27 other events, 154.9 us)
where the time goes:
time: 223 us; the launch traced here: 222 us
  waiting for transfers between devices  86.8 us (39%)
  Pallas kernels  63.1 us (28%)
  starting transfers between devices  49.4 us (22%)
  other arithmetic  16.1 us (7%)
  local copies, waits for them, and re-layouts  5.27 us (2%)
    ppermute x10, waiting for transfers between devices, line_sum(): lax.ppermute(total, 'dp', [(i, i ^ hop) for i in range(CORES * line)])  56.1 us
    ppermute x24, starting transfers between devices, exchange(): lax.ppermute(arrays[s], 'block', [(i, i ^ s) for i in range(groups)])  33.6 us
    pallas_call x4, Pallas kernels, feature(): pl.pallas_call(functools.partial(feature_body, groups, line), grid=(steps...  32.1 us
    ppermute x24, waiting for transfers between devices, exchange(): lax.ppermute(arrays[s], 'block', [(i, i ^ s) for i in range(groups)])  30.7 us
    pallas_call x5, Pallas kernels, settle(): pl.pallas_call(functools.partial(settle_body, fold, len(parts)), grid=(st...  16.3 us
    convert_element_type x10, other arithmetic, line_sum(): total = sum((lax.dynamic_slice_in_dim(a, start % a.shape[0], half, 0).ast...  16.1 us
    ppermute x10, starting transfers between devices, line_sum(): lax.ppermute(total, 'dp', [(i, i ^ hop) for i in range(CORES * line)])  15.3 us
    pallas_call x1, Pallas kernels, mix_out(): pl.pallas_call(functools.partial(mix_out_body, groups, chunks, line), gri...  8.4 us
  transfers between devices with their start and end apart: 39, of which 17 were waited for; matrix products, arithmetic and copies ran while one was open for 7% of the time, Pallas kernels for 24%

commit v1 on v0

v1 whole, which is shorter than its diff:
```python
import functools
import math

import jax
import jax.numpy as jnp
from jax import lax
from jax.experimental import pallas as pl
from jax.experimental.pallas import tpu as pltpu
from jax.sharding import PartitionSpec as P


NARROW = jnp.bfloat16
WIDE = jnp.float32
LANES = 128
ROWS = 16
PITCH = 24
SHARES = (2, 2, 2, 2)
TILE = 128
MIB = 1 << 20
STEP = 4
CORES = 2


def gelu_pair(values):
    factor = math.sqrt(2.0 / math.pi)
    square = values * values
    tanh_part = jnp.tanh(factor * values * (1.0 + 0.044715 * square))
    half = 0.5 + 0.5 * tanh_part
    active = values * half
    slope_term = half + active * (1.0 - tanh_part) * (factor + (3.0 * 0.044715 * factor) * square)
    return (active, slope_term)


def dot(a, b, ca, cb):
    return lax.dot_general(a, b, (((ca,), (cb,)), ((), ())), preferred_element_type=WIDE)


def spread(scr, b, width, value):
    for h in range(scr.shape[0]):
        scr[h, pl.ds(b, width, stride=PITCH), :] = value[:, h * LANES : (h + 1) * LANES]


def split(feats):
    unit, rest = divmod(feats, sum(SHARES))
    sizes = [feats] if rest else [unit * share for share in SHARES]
    return [(size, sum(sizes[:c])) for c, size in enumerate(sizes)]


def mix_in_body(groups, x_ref, g_ref, fu_ref, sd_ref, *rest):
    outs, (scr_u, scr_d) = rest[:-2], rest[-2:]
    rows, width = fu_ref.shape[0], fu_ref.shape[1]
    me = lax.axis_index("block")
    feats = width // groups
    for b in range(rows):
        cols = slice(b * width, (b + 1) * width)
        spread(scr_u, b, width, dot(fu_ref[b], x_ref[:, cols], 0, 1))
        spread(scr_d, b, width, dot(sd_ref[b], g_ref[:, cols], 1, 1))
    for c, (part, begin) in enumerate(split(feats)):
        for s in range(groups):
            ref = outs[c * groups + s]
            off = pl.multiple_of(((me ^ s) * feats + begin) * PITCH, 8)
            for k, scr in enumerate((scr_u, scr_d)):
                for h in range(scr.shape[0]):
                    for n in range(part):
                        value = scr[h, pl.ds(off + n * PITCH, rows), :]
                        ref[k, n, :, h * LANES : (h + 1) * LANES] = value.astype(NARROW)


def mix_in(tokens, cotangent, first_up, second_down, groups):
    count = tokens.shape[0]
    blocks, width = first_up.shape[:2]
    parts = [size for size, _ in split(width // groups)]
    flat = pl.BlockSpec((count, ROWS * width), lambda i: (0, i))
    mats = pl.BlockSpec((ROWS, width, width), lambda i: (i, 0, 0))
    outs = [pl.BlockSpec((2, n, ROWS, count), lambda i: (0, 0, i, 0)) for n in parts for _ in range(groups)]
    res = pl.pallas_call(
        functools.partial(mix_in_body, groups),
        grid=(blocks // ROWS,),
        in_specs=[flat, flat, mats, mats],
        out_specs=outs,
        scratch_shapes=[pltpu.VMEM((count // LANES, width * PITCH, LANES), WIDE)] * 2,
        out_shape=[
            jax.ShapeDtypeStruct((2, n, blocks, count), NARROW) for n in parts for _ in range(groups)
        ],
        cost_estimate=pl.CostEstimate(
            flops=4 * count * blocks * width * width, transcendentals=0, bytes_accessed=8 * count * blocks * width
        ),
        compiler_params=pltpu.CompilerParams(vmem_limit_bytes=24 * MIB),
        name="mix_in",
    )(tokens, cotangent, first_up, second_down)
    return [res[c * groups : (c + 1) * groups] for c in range(len(parts))]


def mirrored(value, bits):
    return sum(((value >> t) & 1) << (bits - 1 - t) for t in range(bits))


def line_slots(line):
    bits = line.bit_length() - 1
    own = mirrored(lax.axis_index("dp") // CORES, bits)
    return [own ^ mirrored(p, bits) for p in range(line)]


def feature_body(groups, line, *rest):
    ins, (wu_ref, wd_ref) = rest[:groups], rest[groups : groups + 2]
    outs = rest[groups + 2 : -8]
    keep_ref, send_ref, u_scr, d_scr, v_scr, e_scr, a_scr, b_scr = rest[-8:]
    me = lax.axis_index("block")
    first = lax.axis_index("dp") % CORES == 0
    blocks = ins[0].shape[2]
    offs = [pl.multiple_of((me ^ s) * blocks, ROWS) for s in range(groups)]
    slots = line_slots(line)
    for n in range(wu_ref.shape[0]):
        for s in range(groups):
            u_scr[n, pl.ds(offs[s], blocks), :] = ins[s][0, n]
            d_scr[n, pl.ds(offs[s], blocks), :] = ins[s][1, n]
    hidden = wd_ref.shape[1]
    for n in range(wu_ref.shape[0]):
        u, d = u_scr[n], d_scr[n]
        for k in range(0, hidden, TILE):
            tile = slice(k, k + TILE)
            active, slope = gelu_pair(dot(wu_ref[n, :, tile], u, 0, 0))
            a_scr[n, tile, :] = active.astype(NARROW)
            b_scr[n, tile, :] = (dot(wd_ref[n, tile, :], d, 1, 0) * slope).astype(NARROW)
    for n in range(wu_ref.shape[0]):
        u, d = u_scr[n], d_scr[n]
        active, back = a_scr[n], b_scr[n]
        v_scr[n] = dot(wd_ref[n], active, 0, 0).astype(NARROW)
        e_scr[n] = dot(wu_ref[n], back, 1, 0).astype(NARROW)
        g_su = dot(u, back, 1, 1).astype(NARROW)
        g_fd = dot(active, d, 1, 1).astype(NARROW)
        r_su = g_su.shape[0] // (CORES * line)
        r_fd = g_fd.shape[0] // (CORES * line)
        fold = g_su.shape[1] // g_fd.shape[1]
        step = r_fd // fold
        for p, at in enumerate(slots):
            halves = []
            for k in range(CORES):
                r = p * CORES + k
                block = g_fd[r * r_fd : (r + 1) * r_fd]
                wide = jnp.concatenate([block[f * step : (f + 1) * step] for f in range(fold)], axis=1)
                halves.append((g_su[r * r_su : (r + 1) * r_su], wide))
            for h in range(2):
                rows = slice(h * r_su, (h + 1) * r_su)
                keep_ref[at, n, rows, :] = jnp.where(first, halves[0][h], halves[1][h])
                send_ref[at, n, rows, :] = jnp.where(first, halves[1][h], halves[0][h])
    for n in range(wu_ref.shape[0]):
        for s in range(groups):
            outs[s][0, n] = v_scr[n, pl.ds(offs[s], blocks), :]
            outs[len(outs) - groups + s][outs[0].shape[0] - 1, n] = e_scr[n, pl.ds(offs[s], blocks), :]


def feature(arrays, second_up, first_down, begin, joint, line):
    groups = len(arrays)
    _, part, blocks, count = arrays[0].shape
    width, hidden = second_up.shape[1:]
    r_su = width // (CORES * line)
    each = math.gcd(STEP, part, begin)
    first = begin // each
    steps = part // each
    kinds = 2 if joint else 1
    n_out = 2 * groups // kinds
    back = pl.BlockSpec((kinds, each, blocks, count), lambda i: (0, i, 0, 0))
    data = pl.BlockSpec((2, each, blocks, count), lambda i: (0, i, 0, 0))
    grads = pl.BlockSpec((line, each, 2 * r_su, hidden), lambda i: (0, i, 0, 0))
    g_shape = jax.ShapeDtypeStruct((line, part, 2 * r_su, hidden), NARROW)
    scr = pltpu.VMEM((each, groups * blocks, count), NARROW)
    res = pl.pallas_call(
        functools.partial(feature_body, groups, line),
        grid=(steps,),
        in_specs=[data] * groups
        + [
            pl.BlockSpec((each, width, hidden), lambda i: (first + i, 0, 0)),
            pl.BlockSpec((each, hidden, width), lambda i: (first + i, 0, 0)),
        ],
        out_specs=[back] * n_out + [grads] * 2,
        scratch_shapes=[scr] * 4 + [pltpu.VMEM((each, hidden, count), NARROW)] * 2,
        out_shape=[jax.ShapeDtypeStruct((kinds, part, blocks, count), NARROW)] * n_out + [g_shape] * 2,
        cost_estimate=pl.CostEstimate(
            flops=12 * part * count * width * hidden,
            transcendentals=part * count * hidden,
            bytes_accessed=part * (8 * width * hidden + 8 * count * width),
        ),
        compiler_params=pltpu.CompilerParams(vmem_limit_bytes=20 * MIB),
        name="feature",
    )(*arrays, second_up, first_down)
    return res[:-2], res[-2], res[-1]


def mix_out_body(groups, line, to_output, *rest):
    ins = rest[:-6]
    flat_ref, mats_ref, out_ref, keep_ref, send_ref, scr = rest[-6:]
    rows, width = mats_ref.shape[0], mats_ref.shape[1]
    me = lax.axis_index("block")
    first = lax.axis_index("dp") % CORES == 0
    slots = line_slots(line)
    feats = width // groups
    for c, (part, begin) in enumerate(split(feats)):
        for s in range(groups):
            ref = ins[c * groups + s]
            off = pl.multiple_of(((me ^ s) * feats + begin) * PITCH, 8)
            for h in range(scr.shape[0]):
                for n in range(part):
                    value = ref[0, n, :, h * LANES : (h + 1) * LANES]
                    scr[h, pl.ds(off + n * PITCH, rows), :] = value.astype(WIDE)
    r_one = width // (CORES * line)
    for b in range(rows):
        cols = slice(b * width, (b + 1) * width)
        pieces = [scr[h, pl.ds(b, width, stride=PITCH), :] for h in range(scr.shape[0])]
        y = jnp.concatenate(pieces, axis=1).astype(NARROW)
        if to_output:
            out_ref[:, cols] = dot(y, mats_ref[b], 0, 0).astype(NARROW)
            grad = dot(y, flat_ref[:, cols], 1, 0).astype(NARROW)
        else:
            out_ref[:, cols] = dot(y, mats_ref[b], 0, 1).astype(NARROW)
            grad = dot(flat_ref[:, cols], y, 0, 1).astype(NARROW)
        for p, at in enumerate(slots):
            halves = [grad[(p * CORES + k) * r_one : (p * CORES + k + 1) * r_one] for k in range(CORES)]
            keep_ref[at, b] = jnp.where(first, halves[0], halves[1])
            send_ref[at, b] = jnp.where(first, halves[1], halves[0])


def mix_out(arrays, flat_in, mats_in, to_output, line):
    groups = len(arrays[0])
    blocks, width = mats_in.shape[:2]
    count = flat_in.shape[0]
    r_one = width // (CORES * line)

    def data(array):
        kind = 0 if to_output or array.shape[0] == 1 else 1
        return pl.BlockSpec((1, array.shape[1], ROWS, count), lambda i: (kind, 0, i, 0))

    flat = pl.BlockSpec((count, ROWS * width), lambda i: (0, i))
    mats = pl.BlockSpec((ROWS, width, width), lambda i: (i, 0, 0))
    grads = pl.BlockSpec((line, ROWS, r_one, width), lambda i: (0, i, 0, 0))
    g_shape = jax.ShapeDtypeStruct((line, blocks, r_one, width), NARROW)
    pieces = [a for chunk in arrays for a in chunk]
    return pl.pallas_call(
        functools.partial(mix_out_body, groups, line, to_output),
        grid=(blocks // ROWS,),
        in_specs=[data(a) for a in pieces] + [flat, mats],
        out_specs=[flat, grads, grads],
        scratch_shapes=[pltpu.VMEM((count // LANES, width * PITCH, LANES), WIDE)],
        out_shape=[jax.ShapeDtypeStruct(flat_in.shape, NARROW), g_shape, g_shape],
        cost_estimate=pl.CostEstimate(
            flops=4 * count * blocks * width * width, transcendentals=0, bytes_accessed=8 * count * blocks * width
        ),
        compiler_params=pltpu.CompilerParams(vmem_limit_bytes=18 * MIB),
        name="mix_out",
    )(*pieces, flat_in, mats_in)


def settle_body(fold, n_sum, *rest):
    ins, first_ref = rest[:n_sum], rest[-2 if fold else -1]
    total = ins[0][0].astype(WIDE)
    for ref in ins[1:]:
        total = total + ref[0].astype(WIDE)
    half = first_ref.shape[1]
    first_ref[...] = total[:, :half]
    for f in range(fold):
        second_ref = rest[-1]
        width = second_ref.shape[2]
        second_ref[:, f * half : (f + 1) * half, :] = total[:, half:, f * width : (f + 1) * width]


def settle(parts, fold, begin, feats, before):
    _, part, rows, cols = parts[0].shape
    tile = math.gcd(part, begin) if begin else part
    tile = math.gcd(tile, 2 * STEP)
    first = begin // tile
    here = pl.BlockSpec((1, tile, rows, cols), lambda i: (0, i, 0, 0))
    half = rows // 2
    shapes = [(feats, half, cols), (feats, half * fold, cols // fold)] if fold else [(feats, rows, cols)]
    return pl.pallas_call(
        functools.partial(settle_body, fold, len(parts)),
        grid=(part // tile,),
        in_specs=[here] * len(parts) + [pl.BlockSpec(memory_space=pl.ANY)] * len(before),
        out_specs=[pl.BlockSpec((tile,) + s[1:], lambda i: (first + i, 0, 0)) for s in shapes],
        out_shape=[jax.ShapeDtypeStruct(s, WIDE) for s in shapes],
        input_output_aliases={len(parts) + k: k for k in range(len(before))},
        cost_estimate=pl.CostEstimate(
            flops=4 * part * rows * cols, transcendentals=0, bytes_accessed=12 * part * rows * cols
        ),
        compiler_params=pltpu.CompilerParams(vmem_limit_bytes=6 * MIB),
        name="settle",
    )(*parts, *before)


def line_sum(keep, send, line):
    parts = [keep, lax.ppermute(send, "dp", [(i, i ^ 1) for i in range(CORES * line)])]
    for t in range(line.bit_length() - 1):
        half = line >> (t + 1)
        total = sum(a[half : 2 * half].astype(WIDE) for a in parts).astype(NARROW)
        hop = CORES << t
        parts.append(lax.ppermute(total, "dp", [(i, i ^ hop) for i in range(CORES * line)]))
    return parts


def is_joint(c, chunks):
    return c < chunks - 2


def local(tokens, first_up, second_up, first_down, second_down, cotangent):
    groups = lax.axis_size("block")
    line = lax.axis_size("dp") // CORES
    feats = second_up.shape[0]
    blocks = first_up.shape[0]
    chunks = split(feats)

    def exchange(arrays):
        got = [arrays[0]]
        for s in range(1, groups):
            got.append(lax.ppermute(arrays[s], "block", [(i, i ^ s) for i in range(groups)]))
        return got

    packed = mix_in(tokens, cotangent, first_up, second_down, groups)
    packed = [exchange(a) for a in packed]
    fold = second_up.shape[2] // second_up.shape[1]
    for_v, for_d, sums = [], [], []
    for c, (_, begin) in enumerate(chunks):
        joint = is_joint(c, len(chunks))
        back, keep, send = feature(packed[c], second_up, first_down, begin, joint, line)
        for_v.append(exchange(back[:groups]))
        for_d.append(for_v[-1] if joint else exchange(back[groups:]))
        sums.append(line_sum(keep, send, line))
    done = ()
    for c, (_, begin) in enumerate(chunks):
        done = settle(sums[c], fold, begin, feats, done)
    red_su, red_fd = done
    result, keep, send = mix_out(for_v, cotangent, second_down, True, line)
    sum_v = line_sum(keep, send, line)
    input_rows, keep, send = mix_out(for_d, tokens, first_up, False, line)
    sum_d = line_sum(keep, send, line)
    (red_sd,) = settle(sum_v, 0, 0, blocks, ())
    (red_fu,) = settle(sum_d, 0, 0, blocks, ())
    return (result, input_rows, red_fu, red_su, red_fd, red_sd)


def plain_local(tokens, first_up, second_up, first_down, second_down, cotangent):
    groups = lax.axis_size("block")
    blocks, width = first_up.shape[:2]
    feats = width // groups
    count = tokens.shape[0]
    x = tokens.reshape(count, blocks, width)
    g = cotangent.reshape(count, blocks, width)

    def mul(spec, a, b):
        return jnp.einsum(spec, a, b, preferred_element_type=WIDE)

    def to_feats(array):
        array = array.astype(NARROW).reshape(count, blocks, groups, feats).transpose(0, 2, 1, 3)
        array = lax.all_to_all(array, "block", split_axis=1, concat_axis=1, tiled=True)
        return array.reshape(count, -1, feats)

    def to_blocks(array):
        array = array.astype(NARROW).reshape(count, groups, blocks, feats)
        array = lax.all_to_all(array, "block", split_axis=1, concat_axis=1, tiled=True)
        return array.transpose(0, 2, 1, 3).reshape(count, blocks, width)

    u = to_feats(mul("tbi,bij->tbj", x, first_up))
    d = to_feats(mul("tbi,bji->tbj", g, second_down))
    active, slope = gelu_pair(mul("tbj,jbk->tjk", u, second_up))
    active = active.astype(NARROW)
    v = to_blocks(mul("tjk,jkb->tbj", active, first_down))
    back = (mul("tbj,jkb->tjk", d, first_down) * slope).astype(NARROW)
    e = to_blocks(mul("tjk,jbk->tbj", back, second_up))
    grads = (
        mul("tbi,tbj->bij", x, e),
        mul("tbj,tjk->jbk", u, back),
        mul("tjk,tbj->jkb", active, d),
        mul("tbj,tbi->bji", v, g),
    )
    result = mul("tbj,bji->tbi", v, second_down).astype(NARROW)
    input_rows = mul("tbj,bij->tbi", e, first_up).astype(NARROW)
    reduced = tuple(lax.psum_scatter(a, "dp", scatter_dimension=1, tiled=True) for a in grads)
    return (result.reshape(count, -1), input_rows.reshape(count, -1)) + reduced


def solution(mesh):
    placed = (
        P("dp", "block"),
        P("block", None, None),
        P("block", None, None),
        P("block", None, None),
        P("block", None, None),
        P("dp", "block"),
    )
    groups, n_dp = mesh.shape["block"], mesh.shape["dp"]
    line = n_dp // CORES

    def suits(first_up, second_up, tokens):
        blocks, width, _ = first_up.shape
        blocks = blocks // groups
        hidden = second_up.shape[2]
        return (
            groups & (groups - 1) == 0
            and n_dp % CORES == 0
            and line > 1
            and line & (line - 1) == 0
            and blocks % ROWS == 0
            and width % LANES == 0
            and hidden % width == 0
            and width % (n_dp * ROWS) == 0
            and tokens.shape[0] // n_dp % LANES == 0
        )

    def step(tokens, first_up, second_up, first_down, second_down, cotangent):
        fits = suits(first_up, second_up, tokens)

        def body(*args):
            return (local if fits else plain_local)(*args)

        run = jax.shard_map(
            body,
            mesh=mesh,
            in_specs=placed,
            out_specs=(
                P("dp", "block"),
                P("dp", "block"),
                P("block", "dp", None),
                P("block", "dp", None),
                P("block", "dp", None),
                P("block", "dp", None),
            ),
            check_vma=False,
        )
        return run(tokens, first_up, second_up, first_down, second_down, cotangent)

    return step
```

time: 223 us -> 233 us (1.045)
  waiting for transfers between devices: 86.8 us -> 132 us
  Pallas kernels: 63.1 us -> 35 us
  other arithmetic: 16.1 us -> 1.29 us
  starting transfers between devices: 49.4 us -> 55.9 us
  local copies, waits for them, and re-layouts: 5.27 us -> 7.84 us
    ppermute x10 -> x12, waiting for transfers between devices: 56.1 us -> 87.5 us  [line_sum(): lax.ppermute(total, 'dp', [(i, i ^ hop) for i in range(CORES * line)])]
    convert_element_type x10 -> x12, other arithmetic: 16.1 us -> 1.29 us  [line_sum(): total = sum((a[half:2 * half].astype(WIDE) for a in parts)).astype(NARROW)]
    pallas_call x7 -> x9, Pallas kernels: 31 us -> 16.8 us  [the longest x2 7.1 us: mix_out(): pl.pallas_call(functools.partial(mix_out_body, groups, line, to_output),...]
    pallas_call x4, Pallas kernels: 32.1 us -> 18.2 us  [feature(): pl.pallas_call(functools.partial(feature_body, groups, line), grid=(steps...]
    ppermute x24 -> x30, waiting for transfers between devices: 30.7 us -> 43.2 us  [exchange(): lax.ppermute(arrays[s], 'block', [(i, i ^ s) for i in range(groups)])]
    ppermute x24 -> x30, starting transfers between devices: 33.6 us -> 38.4 us  [exchange(): lax.ppermute(arrays[s], 'block', [(i, i ^ s) for i in range(groups)])]
    unnamed x72 -> x22, local copies, waits for them, and re-layouts: 5.27 us -> 7.84 us
    ppermute x10 -> x12, starting transfers between devices: 15.3 us -> 16.5 us  [line_sum(): lax.ppermute(total, 'dp', [(i, i ^ hop) for i in range(CORES * line)])]
  transfers between devices with their start and end apart: 39 -> 48, of which waited for: 17 -> 17; matrix products, arithmetic and copies ran while one was open for 7% -> 1% of each run, Pallas kernels for 24% -> 13%
where the time goes in v1:
time: 233 us
  waiting for transfers between devices  132 us (57%)
  starting transfers between devices  55.9 us (24%)
  Pallas kernels  35 us (15%)
  local copies, waits for them, and re-layouts  7.84 us (3%)
    ppermute x12, waiting for transfers between devices, line_sum(): lax.ppermute(total, 'dp', [(i, i ^ hop) for i in range(CORES * line)])  87.5 us
    ppermute x30, waiting for transfers between devices, exchange(): lax.ppermute(arrays[s], 'block', [(i, i ^ s) for i in range(groups)])  43.2 us
    ppermute x30, starting transfers between devices, exchange(): lax.ppermute(arrays[s], 'block', [(i, i ^ s) for i in range(groups)])  38.4 us
    pallas_call x4, Pallas kernels, feature(): pl.pallas_call(functools.partial(feature_body, groups, line), grid=(steps...  18.2 us
    ppermute x12, starting transfers between devices, line_sum(): lax.ppermute(total, 'dp', [(i, i ^ hop) for i in range(CORES * line)])  16.5 us
    unnamed x22, local copies, waits for them, and re-layouts  7.84 us
    pallas_call x2, Pallas kernels, mix_out(): pl.pallas_call(functools.partial(mix_out_body, groups, line, to_output),...  7.1 us
    pallas_call x6, Pallas kernels, settle(): pl.pallas_call(functools.partial(settle_body, fold, len(parts)), grid=(pa...  6.08 us
  transfers between devices with their start and end apart: 48, of which 17 were waited for; matrix products, arithmetic and copies ran while one was open for 1% of the time, Pallas kernels for 13%

profile of v1, /device:TPU:0, one launch (start us, length us, event | category | flops | bytes accessed | tf_op | source)
XLA Modules:
  0.0 232.9 jit_solution(16992223429245003050)
XLA Ops:
  0.6 1.6 copy-done.3
  2.2 1.6 copy-done.5
  6.3 3.6 %mix_in.1 = (bf16[2,8,32,256]{3,2,1,0:T(8,128)(2,1)S(1)}, bf16[2,8,32,256]{3,2,1,0:T(8,128)(2,1)S(1)}, bf16[2,8,32,256]{3,2,1,0:T(8,128)(2,1)S(1)}, bf16[2,8,32,...) custom-call(bf16[256,4096]{1,0:T(8,128)(2,1)S(1)} %copy-done.5, ...), custom_call_target="tpu_custom_call" | custom-call | flops 536870912 | bytes 8388608 | tf_op jit(solution)/shard_map/mix_in/pallas_call | solution.py:76
  9.9 3.0 %collective-permute-start = (bf16[2,8,32,256]{3,2,1,0:T(8,128)(2,1)S(1)}, bf16[2,8,32,256]{3,2,1,0:T(8,128)(2,1)S(1)}, u32[]{:S(2)}, u32[]{:S(2)}) collective-permute-start(bf16[2,8,32,256]{3,2,1,0:T(8,128)(2,1)S(1)} %get-tuple-element.69), channel_id=1, source_target_pairs={{0,8},{8,0},{16,24},{24,16},{1,9},{9,1},{17,25},{25,17},{2,10},{10... | collective-permute-start | bytes 786440 | tf_op jit(solution)/shard_map/ppermute | solution.py:313
  13.0 2.0 collective-permute-start.7
  16.5 3.6 %collective-permute-done.rest_1_ = bf16[2,8,32,256]{3,2,1,0:T(8,128)(2,1)S(1)} collective-permute-done((bf16[2,8,32,256]{3,2,1,0:T(8,128)(2,1)S(1)}, bf16[2,8,32,256]{3,2,1,0:T(8,128)(2,1)S(1)}, u32[]{:S(2)}, u32[]{:S(2)}) %collective-permute-start) | collective-permute-done | bytes 262176 | tf_op jit(solution)/shard_map/ppermute | solution.py:313
  20.1 2.0 collective-permute-start.19
  22.1 3.6 %collective-permute-done.6.rest_1_ = bf16[2,8,32,256]{3,2,1,0:T(8,128)(2,1)S(1)} collective-permute-done((bf16[2,8,32,256]{3,2,1,0:T(8,128)(2,1)S(1)}, bf16[2,8,32,256]{3,2,1,0:T(8,128)(2,1)S(1)}, u32[]{:S(2)}, u32[]{:S(2)}) %collective-permute-start.6) | collective-permute-done | bytes 262176 | tf_op jit(solution)/shard_map/ppermute | solution.py:313
  25.7 3.0 %collective-permute-start.20 = (bf16[2,8,32,256]{3,2,1,0:T(8,128)(2,1)S(1)}, bf16[2,8,32,256]{3,2,1,0:T(8,128)(2,1)S(1)}, u32[]{:S(2)}, u32[]{:S(2)}) collective-permute-start(bf16[2,8,32,256]{3,2,1,0:T(8,128)(2,1)S(1)} %get-tuple-element.95), channel_id=1, source_target_pairs={{0,24},{8,16},{16,8},{24,0},{1,25},{9,17},{17,9},{25,1},{2,26},{10... | collective-permute-start | bytes 786440 | tf_op jit(solution)/shard_map/ppermute | solution.py:313
  29.2 3.6 %collective-permute-done.8.rest_3_ = bf16[2,8,32,256]{3,2,1,0:T(8,128)(2,1)S(1)} collective-permute-done((bf16[2,8,32,256]{3,2,1,0:T(8,128)(2,1)S(1)}, bf16[2,8,32,256]{3,2,1,0:T(8,128)(2,1)S(1)}, u32[]{:S(2)}, u32[]{:S(2)}) %collective-permute-start.8) | collective-permute-done | bytes 262176 | tf_op jit(solution)/shard_map/ppermute | solution.py:313
  32.8 4.1 %collective-permute-done.18.rest_1_ = bf16[2,8,32,256]{3,2,1,0:T(8,128)(2,1)S(1)} collective-permute-done((bf16[2,8,32,256]{3,2,1,0:T(8,128)(2,1)S(1)}, bf16[2,8,32,256]{3,2,1,0:T(8,128)(2,1)S(1)}, u32[]{:S(2)}, u32[]{:S(2)}) %collective-permute-start.18) | collective-permute-done | bytes 262176 | tf_op jit(solution)/shard_map/ppermute | solution.py:313
  37.0 3.0 %collective-permute-start.14 = (bf16[2,8,32,256]{3,2,1,0:T(8,128)(2,1)S(1)}, bf16[2,8,32,256]{3,2,1,0:T(8,128)(2,1)S(1)}, u32[]{:S(2)}, u32[]{:S(2)}) collective-permute-start(bf16[2,8,32,256]{3,2,1,0:T(8,128)(2,1)S(1)} %get-tuple-element.87), channel_id=1, source_target_pairs={{0,24},{8,16},{16,8},{24,0},{1,25},{9,17},{17,9},{25,1},{2,26},{10... | collective-permute-start | bytes 786440 | tf_op jit(solution)/shard_map/ppermute | solution.py:313
  39.9 2.2 copy-done.1
  42.1 4.6 %feature.5 = (bf16[2,8,32,256]{3,2,1,0:T(8,128)(2,1)S(1)}, bf16[2,8,32,256]{3,2,1,0:T(8,128)(2,1)S(1)}, bf16[2,8,32,256]{3,2,1,0:T(8,128)(2,1)S(1)}, bf16[2,8,32...) custom-call(bf16[2,8,32,256]{3,2,1,0:T(8,128)(2,1)S(1)} %get-tuple-element.76.rest, ...), custom_call_target="tpu_custom_call" | custom-call | flops 1610612736 | bytes 6291456 | tf_op jit(solution)/shard_map/feature/pallas_call | solution.py:168
  47.3 1.5 collective-permute-start.2
  48.8 4.5 %feature.7 = (bf16[1,8,32,256]{3,2,1,0:T(8,128)(2,1)S(1)}, bf16[1,8,32,256]{3,2,1,0:T(8,128)(2,1)S(1)}, bf16[1,8,32,256]{3,2,1,0:T(8,128)(2,1)S(1)}, bf16[1,8,32...) custom-call(bf16[2,8,32,256]{3,2,1,0:T(8,128)(2,1)S(1)} %get-tuple-e, ...), custom_call_target="tpu_custom_call" | custom-call | flops 1610612736 | bytes 6291456 | tf_op jit(solution)/shard_map/feature/pallas_call | solution.py:168
  53.3 1.5 collective-permute-start.9
  55.5 4.5 %feature.6 = (bf16[1,8,32,256]{3,2,1,0:T(8,128)(2,1)S(1)}, bf16[1,8,32,256]{3,2,1,0:T(8,128)(2,1)S(1)}, bf16[1,8,32,256]{3,2,1,0:T(8,128)(2,1)S(1)}, bf16[1,8,32...) custom-call(bf16[2,8,32,256]{3,2,1,0:T(8,128)(2,1)S(1)} %get-tuple-e, ...), custom_call_target="tpu_custom_call" | custom-call | flops 1610612736 | bytes 6291456 | tf_op jit(solution)/shard_map/feature/pallas_call | solution.py:168
  60.0 5.2 %collective-permute-done.1.rest_2_ = bf16[2,8,32,256]{3,2,1,0:T(8,128)(2,1)S(1)} collective-permute-done((bf16[2,8,32,256]{3,2,1,0:T(8,128)(2,1)S(1)}, bf16[2,8,32,256]{3,2,1,0:T(8,128)(2,1)S(1)}, u32[]{:S(2)}, u32[]{:S(2)}) %collective-permute-start.1) | collective-permute-done | bytes 262176 | tf_op jit(solution)/shard_map/ppermute | solution.py:313
  65.7 1.4 collective-permute-start.15
  67.9 2.1 collective-permute-start.16
  70.0 1.4 collective-permute-start.17
  71.5 4.6 %feature.4 = (bf16[2,8,32,256]{3,2,1,0:T(8,128)(2,1)S(1)}, bf16[2,8,32,256]{3,2,1,0:T(8,128)(2,1)S(1)}, bf16[2,8,32,256]{3,2,1,0:T(8,128)(2,1)S(1)}, bf16[2,8,32...) custom-call(bf16[2,8,32,256]{3,2,1,0:T(8,128)(2,1)S(1)} %get-tuple-element.68.rest, ...), custom_call_target="tpu_custom_call" | custom-call | flops 1610612736 | bytes 6291456 | tf_op jit(solution)/shard_map/feature/pallas_call | solution.py:168
  76.0 1.6 collective-permute-start.10
  77.9 1.7 collective-permute-start.3
  79.6 2.7 %collective-permute-start.4 = (bf16[2,8,32,256]{3,2,1,0:T(8,128)(2,1)S(1)}, bf16[2,8,32,256]{3,2,1,0:T(8,128)(2,1)S(1)}, u32[]{:S(2)}, u32[]{:S(2)}) collective-permute-start(bf16[2,8,32,256]{3,2,1,0:T(8,128)(2,1)S(1)} %get-tuple-element.74), channel_id=1, source_target_pairs={{0,16},{8,24},{16,0},{24,8},{1,17},{9,25},{17,1},{25,9},{2,18},{10... | collective-permute-start | bytes 786440 | tf_op jit(solution)/shard_map/ppermute | solution.py:313
  82.3 10.0 %collective-permute-done.10.rest_6_ = bf16[2,8,32,256]{3,2,1,0:T(8,128)(2,1)S(1)} collective-permute-done((bf16[2,8,32,256]{3,2,1,0:T(8,128)(2,1)S(1)}, bf16[2,8,32,256]{3,2,1,0:T(8,128)(2,1)S(1)}, u32[]{:S(2)}, u32[]{:S(2)}) %collective-permute-start.10) | collective-permute-done | bytes 262176 | tf_op jit(solution)/shard_map/ppermute | solution.py:313
  92.7 3.4 %collective-permute-start.28 = (bf16[1,8,32,256]{3,2,1,0:T(8,128)(2,1)S(1)}, bf16[1,8,32,256]{3,2,1,0:T(8,128)(2,1)S(1)}, u32[]{:S(2)}, u32[]{:S(2)}) collective-permute-start(bf16[1,8,32,256]{3,2,1,0:T(8,128)(2,1)S(1)} %get-tuple-element.107), channel_id=1, source_target_pairs={{0,16},{8,24},{16,0},{24,8},{1,17},{9,25},{17,1},{25,9},{2,18},{10... | collective-permute-start | bytes 393224 | tf_op jit(solution)/shard_map/ppermute | solution.py:313
  96.2 7.3 %collective-permute-done.4.rest_2_ = bf16[2,8,32,256]{3,2,1,0:T(8,128)(2,1)S(1)} collective-permute-done((bf16[2,8,32,256]{3,2,1,0:T(8,128)(2,1)S(1)}, bf16[2,8,32,256]{3,2,1,0:T(8,128)(2,1)S(1)}, u32[]{:S(2)}, u32[]{:S(2)}) %collective-permute-start.4) | collective-permute-done | bytes 262176 | tf_op jit(solution)/shard_map/ppermute | solution.py:313
  103.5 3.6 %mix_out.2 = (bf16[256,4096]{1,0:T(8,128)(2,1)}, bf16[4,32,16,128]{3,2,1,0:T(8,128)(2,1)S(1)}, bf16[4,32,16,128]{3,2,1,0:T(8,128)(2,1)S(1)}) custom-call(bf16[2,8,32,256]{3,2,1,0:T(8,128)(2,1)S(1)} %get-tuple-element.72.rest_0_, bf16[2,8,32,256]{3,2,1,0:T(8,128)(2,1)S(1)} %collective-permute-done.3.rest_1_, ...), custom_call_target="tpu_custom_call" | custom-call | flops 536870912 | bytes 8388608 | tf_op jit(solution)/shard_map/mix_out/pallas_call | solution.py:238
  108.8 2.2 collective-permute-start.26
  111.0 2.9 %collective-permute-done.24.rest_9_ = bf16[1,8,32,256]{3,2,1,0:T(8,128)(2,1)S(1)} collective-permute-done((bf16[1,8,32,256]{3,2,1,0:T(8,128)(2,1)S(1)}, bf16[1,8,32,256]{3,2,1,0:T(8,128)(2,1)S(1)}, u32[]{:S(2)}, u32[]{:S(2)}) %collective-permute-start.24) | collective-permute-done | bytes 131104 | tf_op jit(solution)/shard_map/ppermute | solution.py:313
  113.9 2.1 collective-permute-done.25.rest_10_
  116.0 3.5 %mix_out.3 = (bf16[256,4096]{1,0:T(8,128)(2,1)}, bf16[4,32,16,128]{3,2,1,0:T(8,128)(2,1)S(1)}, bf16[4,32,16,128]{3,2,1,0:T(8,128)(2,1)S(1)}) custom-call(bf16[2,8,32,256]{3,2,1,0:T(8,128)(2,1)S(1)} %get-tuple-element.72.rest_0_, bf16[2,8,32,256]{3,2,1,0:T(8,128)(2,1)S(1)} %collective-permute-done.3.rest_1_, ...), custom_call_target="tpu_custom_call" | custom-call | flops 536870912 | bytes 8388608 | tf_op jit(solution)/shard_map/mix_out/pallas_call | solution.py:238
  121.5 1.6 collective-permute-start.46
  123.8 1.6 collective-permute-start.40
  126.3 1.6 collective-permute-start.34
  128.1 2.5 %collective-permute-done.46.rest_2_ = bf16[2,32,16,128]{3,2,1,0:T(8,128)(2,1)S(1)} collective-permute-done((bf16[2,32,16,128]{3,2,1,0:T(8,128)(2,1)S(1)}, bf16[2,32,16,128]{3,2,1,0:T(8,128)(2,1)S(1)}, u32[]{:S(2)}, u32[]{:S(2)}) %collective-permute-start.46) | collective-permute-done | bytes 262176 | tf_op jit(solution)/shard_map/ppermute | solution.py:295
  130.6 1.6 collective-permute-start.37
  132.3 15.2 %collective-permute-done.40.rest_2_ = bf16[2,8,32,512]{3,2,1,0:T(8,128)(2,1)S(1)} collective-permute-done((bf16[2,8,32,512]{3,2,1,0:T(8,128)(2,1)S(1)}, bf16[2,8,32,512]{3,2,1,0:T(8,128)(2,1)S(1)}, u32[]{:S(2)}, u32[]{:S(2)}) %collective-permute-start.40) | collective-permute-done | bytes 524320 | tf_op jit(solution)/shard_map/ppermute | solution.py:295
  147.5 2.6 %collective-permute-start.47 = (bf16[1,32,16,128]{3,2,1,0:T(8,128)(2,1)S(1)}, bf16[1,32,16,128]{3,2,1,0:T(8,128)(2,1)S(1)}, u32[]{:S(2)}, u32[]{:S(2)}) collective-permute-start(bf16[1,32,16,128]{3,2,1,0:T(8,128)(2,1)S(1)} %add_convert_fusion.10), channel_id=1, source_target_pairs={{0,4},{1,5},{2,6},{3,7},{4,0},{5,1},{6,2},{7,3},{8,12},{9,13},{10,... | collective-permute-start | bytes 393224 | tf_op jit(solution)/shard_map/ppermute | solution.py:295
  150.2 11.4 %collective-permute-done.43.rest_2_ = bf16[2,8,32,512]{3,2,1,0:T(8,128)(2,1)S(1)} collective-permute-done((bf16[2,8,32,512]{3,2,1,0:T(8,128)(2,1)S(1)}, bf16[2,8,32,512]{3,2,1,0:T(8,128)(2,1)S(1)}, u32[]{:S(2)}, u32[]{:S(2)}) %collective-permute-start.43) | collective-permute-done | bytes 524320 | tf_op jit(solution)/shard_map/ppermute | solution.py:295
  161.5 1.7 collective-permute-start.41
  163.3 15.1 %collective-permute-done.34.rest_2_ = bf16[2,8,32,512]{3,2,1,0:T(8,128)(2,1)S(1)} collective-permute-done((bf16[2,8,32,512]{3,2,1,0:T(8,128)(2,1)S(1)}, bf16[2,8,32,512]{3,2,1,0:T(8,128)(2,1)S(1)}, u32[]{:S(2)}, u32[]{:S(2)}) %collective-permute-start.34) | collective-permute-done | bytes 524320 | tf_op jit(solution)/shard_map/ppermute | solution.py:295
  178.4 1.7 collective-permute-start.44
  180.2 10.7 %collective-permute-done.37.rest_2_ = bf16[2,8,32,512]{3,2,1,0:T(8,128)(2,1)S(1)} collective-permute-done((bf16[2,8,32,512]{3,2,1,0:T(8,128)(2,1)S(1)}, bf16[2,8,32,512]{3,2,1,0:T(8,128)(2,1)S(1)}, u32[]{:S(2)}, u32[]{:S(2)}) %collective-permute-start.37) | collective-permute-done | bytes 524320 | tf_op jit(solution)/shard_map/ppermute | solution.py:295
  191.0 3.0 %collective-permute-start.38 = (bf16[1,8,32,512]{3,2,1,0:T(8,128)(2,1)S(1)}, bf16[1,8,32,512]{3,2,1,0:T(8,128)(2,1)S(1)}, u32[]{:S(2)}, u32[]{:S(2)}) collective-permute-start(bf16[1,8,32,512]{3,2,1,0:T(8,128)(2,1)S(1)} %add_convert_fusion.7), channel_id=1, source_target_pairs={{0,4},{1,5},{2,6},{3,7},{4,0},{5,1},{6,2},{7,3},{8,12},{9,13},{10,... | collective-permute-start | bytes 786440 | tf_op jit(solution)/shard_map/ppermute | solution.py:295
  195.5 32.6 %collective-permute-done.32.rest_3_ = bf16[1,32,16,128]{3,2,1,0:T(8,128)(2,1)S(1)} collective-permute-done((bf16[1,32,16,128]{3,2,1,0:T(8,128)(2,1)S(1)}, bf16[1,32,16,128]{3,2,1,0:T(8,128)(2,1)S(1)}, u32[]{:S(2)}, u32[]{:S(2)}) %collective-permute-start.32) | collective-permute-done | bytes 131104 | tf_op jit(solution)/shard_map/ppermute | solution.py:295
  (95 shorter events, 20.0 us)
Async XLA Ops:
  9.9 10.2 %collective-permute-start = (bf16[2,8,32,256]{3,2,1,0:T(8,128)(2,1)S(1)}, bf16[2,8,32,256]{3,2,1,0:T(8,128)(2,1)S(1)}, u32[]{:S(2)}, u32[]{:S(2)}) collective-permute-start(bf16[2,8,32,256]{3,2,1,0:T(8,128)(2,1)S(1)} %get-tuple-element.69), channel_id=1, source_target_pairs={{0,8},{8,0},{16,24},{24,16},{1,9},{9,1},{17,25},{25,17},{2,10},{10... | collective-permute-start | bytes 786440 | tf_op jit(solution)/shard_map/ppermute | solution.py:313
  12.9 12.8 %collective-permute-start.6 = (bf16[2,8,32,256]{3,2,1,0:T(8,128)(2,1)S(1)}, bf16[2,8,32,256]{3,2,1,0:T(8,128)(2,1)S(1)}, u32[]{:S(2)}, u32[]{:S(2)}) collective-permute-start(bf16[2,8,32,256]{3,2,1,0:T(8,128)(2,1)S(1)} %get-tuple-element.77), channel_id=1, source_target_pairs={{0,8},{8,0},{16,24},{24,16},{1,9},{9,1},{17,25},{25,17},{2,10},{10... | collective-permute-start | bytes 786440 | tf_op jit(solution)/shard_map/ppermute | solution.py:313
  13.0 15.7 %collective-permute-start.7 = (bf16[2,8,32,256]{3,2,1,0:T(8,128)(2,1)S(1)}, bf16[2,8,32,256]{3,2,1,0:T(8,128)(2,1)S(1)}, u32[]{:S(2)}, u32[]{:S(2)}) collective-permute-start(bf16[2,8,32,256]{3,2,1,0:T(8,128)(2,1)S(1)} %get-tuple-element.78), channel_id=1, source_target_pairs={{0,16},{8,24},{16,0},{24,8},{1,17},{9,25},{17,1},{25,9},{2,18},{10... | collective-permute-start | bytes 786440 | tf_op jit(solution)/shard_map/ppermute | solution.py:313
  15.0 17.9 %collective-permute-start.8 = (bf16[2,8,32,256]{3,2,1,0:T(8,128)(2,1)S(1)}, bf16[2,8,32,256]{3,2,1,0:T(8,128)(2,1)S(1)}, u32[]{:S(2)}, u32[]{:S(2)}) collective-permute-start(bf16[2,8,32,256]{3,2,1,0:T(8,128)(2,1)S(1)} %get-tuple-element.79), channel_id=1, source_target_pairs={{0,24},{8,16},{16,8},{24,0},{1,25},{9,17},{17,9},{25,1},{2,26},{10... | collective-permute-start | bytes 786440 | tf_op jit(solution)/shard_map/ppermute | solution.py:313
  16.4 20.6 %collective-permute-start.18 = (bf16[2,8,32,256]{3,2,1,0:T(8,128)(2,1)S(1)}, bf16[2,8,32,256]{3,2,1,0:T(8,128)(2,1)S(1)}, u32[]{:S(2)}, u32[]{:S(2)}) collective-permute-start(bf16[2,8,32,256]{3,2,1,0:T(8,128)(2,1)S(1)} %get-tuple-element.93), channel_id=1, source_target_pairs={{0,8},{8,0},{16,24},{24,16},{1,9},{9,1},{17,25},{25,17},{2,10},{10... | collective-permute-start | bytes 786440 | tf_op jit(solution)/shard_map/ppermute | solution.py:313
  20.1 26.6 %collective-permute-start.19 = (bf16[2,8,32,256]{3,2,1,0:T(8,128)(2,1)S(1)}, bf16[2,8,32,256]{3,2,1,0:T(8,128)(2,1)S(1)}, u32[]{:S(2)}, u32[]{:S(2)}) collective-permute-start(bf16[2,8,32,256]{3,2,1,0:T(8,128)(2,1)S(1)} %get-tuple-element.94), channel_id=1, source_target_pairs={{0,16},{8,24},{16,0},{24,8},{1,17},{9,25},{17,1},{25,9},{2,18},{10... | collective-permute-start | bytes 786440 | tf_op jit(solution)/shard_map/ppermute | solution.py:313
  25.7 21.6 %collective-permute-start.20 = (bf16[2,8,32,256]{3,2,1,0:T(8,128)(2,1)S(1)}, bf16[2,8,32,256]{3,2,1,0:T(8,128)(2,1)S(1)}, u32[]{:S(2)}, u32[]{:S(2)}) collective-permute-start(bf16[2,8,32,256]{3,2,1,0:T(8,128)(2,1)S(1)} %get-tuple-element.95), channel_id=1, source_target_pairs={{0,24},{8,16},{16,8},{24,0},{1,25},{9,17},{17,9},{25,1},{2,26},{10... | collective-permute-start | bytes 786440 | tf_op jit(solution)/shard_map/ppermute | solution.py:313
  28.7 24.7 %collective-permute-start.12 = (bf16[2,8,32,256]{3,2,1,0:T(8,128)(2,1)S(1)}, bf16[2,8,32,256]{3,2,1,0:T(8,128)(2,1)S(1)}, u32[]{:S(2)}, u32[]{:S(2)}) collective-permute-start(bf16[2,8,32,256]{3,2,1,0:T(8,128)(2,1)S(1)} %get-tuple-element.85), channel_id=1, source_target_pairs={{0,8},{8,0},{16,24},{24,16},{1,9},{9,1},{17,25},{25,17},{2,10},{10... | collective-permute-start | bytes 786440 | tf_op jit(solution)/shard_map/ppermute | solution.py:313
  32.8 22.0 %collective-permute-start.13 = (bf16[2,8,32,256]{3,2,1,0:T(8,128)(2,1)S(1)}, bf16[2,8,32,256]{3,2,1,0:T(8,128)(2,1)S(1)}, u32[]{:S(2)}, u32[]{:S(2)}) collective-permute-start(bf16[2,8,32,256]{3,2,1,0:T(8,128)(2,1)S(1)} %get-tuple-element.86), channel_id=1, source_target_pairs={{0,16},{8,24},{16,0},{24,8},{1,17},{9,25},{17,1},{25,9},{2,18},{10... | collective-permute-start | bytes 786440 | tf_op jit(solution)/shard_map/ppermute | solution.py:313
  37.0 18.5 %collective-permute-start.14 = (bf16[2,8,32,256]{3,2,1,0:T(8,128)(2,1)S(1)}, bf16[2,8,32,256]{3,2,1,0:T(8,128)(2,1)S(1)}, u32[]{:S(2)}, u32[]{:S(2)}) collective-permute-start(bf16[2,8,32,256]{3,2,1,0:T(8,128)(2,1)S(1)} %get-tuple-element.87), channel_id=1, source_target_pairs={{0,24},{8,16},{16,8},{24,0},{1,25},{9,17},{17,9},{25,1},{2,26},{10... | collective-permute-start | bytes 786440 | tf_op jit(solution)/shard_map/ppermute | solution.py:313
  46.7 18.5 %collective-permute-start.1 = (bf16[2,8,32,256]{3,2,1,0:T(8,128)(2,1)S(1)}, bf16[2,8,32,256]{3,2,1,0:T(8,128)(2,1)S(1)}, u32[]{:S(2)}, u32[]{:S(2)}) collective-permute-start(bf16[2,8,32,256]{3,2,1,0:T(8,128)(2,1)S(1)} %get-tuple-element.70), channel_id=1, source_target_pairs={{0,16},{8,24},{16,0},{24,8},{1,17},{9,25},{17,1},{25,9},{2,18},{10... | collective-permute-start | bytes 786440 | tf_op jit(solution)/shard_map/ppermute | solution.py:313
  47.3 18.4 %collective-permute-start.2 = (bf16[2,8,32,256]{3,2,1,0:T(8,128)(2,1)S(1)}, bf16[2,8,32,256]{3,2,1,0:T(8,128)(2,1)S(1)}, u32[]{:S(2)}, u32[]{:S(2)}) collective-permute-start(bf16[2,8,32,256]{3,2,1,0:T(8,128)(2,1)S(1)} %get-tuple-element.71), channel_id=1, source_target_pairs={{0,24},{8,16},{16,8},{24,0},{1,25},{9,17},{17,9},{25,1},{2,26},{10... | collective-permute-start | bytes 786440 | tf_op jit(solution)/shard_map/ppermute | solution.py:313
  53.3 28.9 %collective-permute-start.9 = (bf16[2,8,32,256]{3,2,1,0:T(8,128)(2,1)S(1)}, bf16[2,8,32,256]{3,2,1,0:T(8,128)(2,1)S(1)}, u32[]{:S(2)}, u32[]{:S(2)}) collective-permute-start(bf16[2,8,32,256]{3,2,1,0:T(8,128)(2,1)S(1)} %get-tuple-element.81), channel_id=1, source_target_pairs={{0,8},{8,0},{16,24},{24,16},{1,9},{9,1},{17,25},{25,17},{2,10},{10... | collective-permute-start | bytes 786440 | tf_op jit(solution)/shard_map/ppermute | solution.py:313
  54.9 13.1 %collective-permute-start.21 = (bf16[1,8,32,256]{3,2,1,0:T(8,128)(2,1)S(1)}, bf16[1,8,32,256]{3,2,1,0:T(8,128)(2,1)S(1)}, u32[]{:S(2)}, u32[]{:S(2)}) collective-permute-start(bf16[1,8,32,256]{3,2,1,0:T(8,128)(2,1)S(1)} %get-tuple-element.97), channel_id=1, source_target_pairs={{0,8},{8,0},{16,24},{24,16},{1,9},{9,1},{17,25},{25,17},{2,10},{10... | collective-permute-start | bytes 393224 | tf_op jit(solution)/shard_map/ppermute | solution.py:313
  55.5 14.6 %collective-permute-start.22 = (bf16[1,8,32,256]{3,2,1,0:T(8,128)(2,1)S(1)}, bf16[1,8,32,256]{3,2,1,0:T(8,128)(2,1)S(1)}, u32[]{:S(2)}, u32[]{:S(2)}) collective-permute-start(bf16[1,8,32,256]{3,2,1,0:T(8,128)(2,1)S(1)} %get-tuple-element.98), channel_id=1, source_target_pairs={{0,16},{8,24},{16,0},{24,8},{1,17},{9,25},{17,1},{25,9},{2,18},{10... | collective-permute-start | bytes 393224 | tf_op jit(solution)/shard_map/ppermute | solution.py:313
  65.2 10.8 %collective-permute-start.23 = (bf16[1,8,32,256]{3,2,1,0:T(8,128)(2,1)S(1)}, bf16[1,8,32,256]{3,2,1,0:T(8,128)(2,1)S(1)}, u32[]{:S(2)}, u32[]{:S(2)}) collective-permute-start(bf16[1,8,32,256]{3,2,1,0:T(8,128)(2,1)S(1)} %get-tuple-element.99), channel_id=1, source_target_pairs={{0,24},{8,16},{16,8},{24,0},{1,25},{9,17},{17,9},{25,1},{2,26},{10... | collective-permute-start | bytes 393224 | tf_op jit(solution)/shard_map/ppermute | solution.py:313
  65.7 11.9 %collective-permute-start.15 = (bf16[1,8,32,256]{3,2,1,0:T(8,128)(2,1)S(1)}, bf16[1,8,32,256]{3,2,1,0:T(8,128)(2,1)S(1)}, u32[]{:S(2)}, u32[]{:S(2)}) collective-permute-start(bf16[1,8,32,256]{3,2,1,0:T(8,128)(2,1)S(1)} %get-tuple-element.89), channel_id=1, source_target_pairs={{0,8},{8,0},{16,24},{24,16},{1,9},{9,1},{17,25},{25,17},{2,10},{10... | collective-permute-start | bytes 393224 | tf_op jit(solution)/shard_map/ppermute | solution.py:313
  67.9 9.9 %collective-permute-start.16 = (bf16[1,8,32,256]{3,2,1,0:T(8,128)(2,1)S(1)}, bf16[1,8,32,256]{3,2,1,0:T(8,128)(2,1)S(1)}, u32[]{:S(2)}, u32[]{:S(2)}) collective-permute-start(bf16[1,8,32,256]{3,2,1,0:T(8,128)(2,1)S(1)} %get-tuple-element.90), channel_id=1, source_target_pairs={{0,16},{8,24},{16,0},{24,8},{1,17},{9,25},{17,1},{25,9},{2,18},{10... | collective-permute-start | bytes 393224 | tf_op jit(solution)/shard_map/ppermute | solution.py:313
  70.0 9.6 %collective-permute-start.17 = (bf16[1,8,32,256]{3,2,1,0:T(8,128)(2,1)S(1)}, bf16[1,8,32,256]{3,2,1,0:T(8,128)(2,1)S(1)}, u32[]{:S(2)}, u32[]{:S(2)}) collective-permute-start(bf16[1,8,32,256]{3,2,1,0:T(8,128)(2,1)S(1)} %get-tuple-element.91), channel_id=1, source_target_pairs={{0,24},{8,16},{16,8},{24,0},{1,25},{9,17},{17,9},{25,1},{2,26},{10... | collective-permute-start | bytes 393224 | tf_op jit(solution)/shard_map/ppermute | solution.py:313
  76.0 16.2 %collective-permute-start.10 = (bf16[2,8,32,256]{3,2,1,0:T(8,128)(2,1)S(1)}, bf16[2,8,32,256]{3,2,1,0:T(8,128)(2,1)S(1)}, u32[]{:S(2)}, u32[]{:S(2)}) collective-permute-start(bf16[2,8,32,256]{3,2,1,0:T(8,128)(2,1)S(1)} %get-tuple-element.82), channel_id=1, source_target_pairs={{0,16},{8,24},{16,0},{24,8},{1,17},{9,25},{17,1},{25,9},{2,18},{10... | collective-permute-start | bytes 786440 | tf_op jit(solution)/shard_map/ppermute | solution.py:313
  77.6 15.1 %collective-permute-start.11 = (bf16[2,8,32,256]{3,2,1,0:T(8,128)(2,1)S(1)}, bf16[2,8,32,256]{3,2,1,0:T(8,128)(2,1)S(1)}, u32[]{:S(2)}, u32[]{:S(2)}) collective-permute-start(bf16[2,8,32,256]{3,2,1,0:T(8,128)(2,1)S(1)} %get-tuple-element.83), channel_id=1, source_target_pairs={{0,24},{8,16},{16,8},{24,0},{1,25},{9,17},{17,9},{25,1},{2,26},{10... | collective-permute-start | bytes 786440 | tf_op jit(solution)/shard_map/ppermute | solution.py:313
  77.9 18.3 %collective-permute-start.3 = (bf16[2,8,32,256]{3,2,1,0:T(8,128)(2,1)S(1)}, bf16[2,8,32,256]{3,2,1,0:T(8,128)(2,1)S(1)}, u32[]{:S(2)}, u32[]{:S(2)}) collective-permute-start(bf16[2,8,32,256]{3,2,1,0:T(8,128)(2,1)S(1)} %get-tuple-element.73), channel_id=1, source_target_pairs={{0,8},{8,0},{16,24},{24,16},{1,9},{9,1},{17,25},{25,17},{2,10},{10... | collective-permute-start | bytes 786440 | tf_op jit(solution)/shard_map/ppermute | solution.py:313
  79.6 23.8 %collective-permute-start.4 = (bf16[2,8,32,256]{3,2,1,0:T(8,128)(2,1)S(1)}, bf16[2,8,32,256]{3,2,1,0:T(8,128)(2,1)S(1)}, u32[]{:S(2)}, u32[]{:S(2)}) collective-permute-start(bf16[2,8,32,256]{3,2,1,0:T(8,128)(2,1)S(1)} %get-tuple-element.74), channel_id=1, source_target_pairs={{0,16},{8,24},{16,0},{24,8},{1,17},{9,25},{17,1},{25,9},{2,18},{10... | collective-permute-start | bytes 786440 | tf_op jit(solution)/shard_map/ppermute | solution.py:313
  82.3 21.2 %collective-permute-start.5 = (bf16[2,8,32,256]{3,2,1,0:T(8,128)(2,1)S(1)}, bf16[2,8,32,256]{3,2,1,0:T(8,128)(2,1)S(1)}, u32[]{:S(2)}, u32[]{:S(2)}) collective-permute-start(bf16[2,8,32,256]{3,2,1,0:T(8,128)(2,1)S(1)} %get-tuple-element.75), channel_id=1, source_target_pairs={{0,24},{8,16},{16,8},{24,0},{1,25},{9,17},{17,9},{25,1},{2,26},{10... | collective-permute-start | bytes 786440 | tf_op jit(solution)/shard_map/ppermute | solution.py:313
  92.3 15.3 %collective-permute-start.27 = (bf16[1,8,32,256]{3,2,1,0:T(8,128)(2,1)S(1)}, bf16[1,8,32,256]{3,2,1,0:T(8,128)(2,1)S(1)}, u32[]{:S(2)}, u32[]{:S(2)}) collective-permute-start(bf16[1,8,32,256]{3,2,1,0:T(8,128)(2,1)S(1)} %get-tuple-element.106), channel_id=1, source_target_pairs={{0,8},{8,0},{16,24},{24,16},{1,9},{9,1},{17,25},{25,17},{2,10},{10... | collective-permute-start | bytes 393224 | tf_op jit(solution)/shard_map/ppermute | solution.py:313
  92.7 15.3 %collective-permute-start.28 = (bf16[1,8,32,256]{3,2,1,0:T(8,128)(2,1)S(1)}, bf16[1,8,32,256]{3,2,1,0:T(8,128)(2,1)S(1)}, u32[]{:S(2)}, u32[]{:S(2)}) collective-permute-start(bf16[1,8,32,256]{3,2,1,0:T(8,128)(2,1)S(1)} %get-tuple-element.107), channel_id=1, source_target_pairs={{0,16},{8,24},{16,0},{24,8},{1,17},{9,25},{17,1},{25,9},{2,18},{10... | collective-permute-start | bytes 393224 | tf_op jit(solution)/shard_map/ppermute | solution.py:313
  96.2 12.7 %collective-permute-start.29 = (bf16[1,8,32,256]{3,2,1,0:T(8,128)(2,1)S(1)}, bf16[1,8,32,256]{3,2,1,0:T(8,128)(2,1)S(1)}, u32[]{:S(2)}, u32[]{:S(2)}) collective-permute-start(bf16[1,8,32,256]{3,2,1,0:T(8,128)(2,1)S(1)} %get-tuple-element.108), channel_id=1, source_target_pairs={{0,24},{8,16},{16,8},{24,0},{1,25},{9,17},{17,9},{25,1},{2,26},{10... | collective-permute-start | bytes 393224 | tf_op jit(solution)/shard_map/ppermute | solution.py:313
  103.4 19.7 %collective-permute-start.39 = (bf16[4,8,32,512]{3,2,1,0:T(8,128)(2,1)S(1)}, bf16[4,8,32,512]{3,2,1,0:T(8,128)(2,1)S(1)}, u32[]{:S(2)}, u32[]{:S(2)}) collective-permute-start(bf16[4,8,32,512]{3,2,1,0:T(8,128)(2,1)S(1)} %get-tuple-element.117), channel_id=1, source_target_pairs={{0,1},{1,0},{2,3},{3,2},{4,5},{5,4},{6,7},{7,6},{8,9},{9,8},{10,11... | collective-permute-start | bytes 3145736 | tf_op jit(solution)/shard_map/ppermute | solution.py:290
  107.0 13.0 %collective-permute-start.45 = (bf16[4,32,16,128]{3,2,1,0:T(8,128)(2,1)S(1)}, bf16[4,32,16,128]{3,2,1,0:T(8,128)(2,1)S(1)}, u32[]{:S(2)}, u32[]{:S(2)}) collective-permute-start(bf16[4,32,16,128]{3,2,1,0:T(8,128)(2,1)S(1)} %get-tuple-element.129), channel_id=1, source_target_pairs={{0,1},{1,0},{2,3},{3,2},{4,5},{5,4},{6,7},{7,6},{8,9},{9,8},{10,11... | collective-permute-start | bytes 1572872 | tf_op jit(solution)/shard_map/ppermute | solution.py:290
  107.5 6.4 %collective-permute-start.24 = (bf16[1,8,32,256]{3,2,1,0:T(8,128)(2,1)S(1)}, bf16[1,8,32,256]{3,2,1,0:T(8,128)(2,1)S(1)}, u32[]{:S(2)}, u32[]{:S(2)}) collective-permute-start(bf16[1,8,32,256]{3,2,1,0:T(8,128)(2,1)S(1)} %get-tuple-element.102), channel_id=1, source_target_pairs={{0,8},{8,0},{16,24},{24,16},{1,9},{9,1},{17,25},{25,17},{2,10},{10... | collective-permute-start | bytes 393224 | tf_op jit(solution)/shard_map/ppermute | solution.py:313
  108.1 7.9 %collective-permute-start.25 = (bf16[1,8,32,256]{3,2,1,0:T(8,128)(2,1)S(1)}, bf16[1,8,32,256]{3,2,1,0:T(8,128)(2,1)S(1)}, u32[]{:S(2)}, u32[]{:S(2)}) collective-permute-start(bf16[1,8,32,256]{3,2,1,0:T(8,128)(2,1)S(1)} %get-tuple-element.103), channel_id=1, source_target_pairs={{0,16},{8,24},{16,0},{24,8},{1,17},{9,25},{17,1},{25,9},{2,18},{10... | collective-permute-start | bytes 393224 | tf_op jit(solution)/shard_map/ppermute | solution.py:313
  108.8 7.2 %collective-permute-start.26 = (bf16[1,8,32,256]{3,2,1,0:T(8,128)(2,1)S(1)}, bf16[1,8,32,256]{3,2,1,0:T(8,128)(2,1)S(1)}, u32[]{:S(2)}, u32[]{:S(2)}) collective-permute-start(bf16[1,8,32,256]{3,2,1,0:T(8,128)(2,1)S(1)} %get-tuple-element.104), channel_id=1, source_target_pairs={{0,24},{8,16},{16,8},{24,0},{1,25},{9,17},{17,9},{25,1},{2,26},{10... | collective-permute-start | bytes 393224 | tf_op jit(solution)/shard_map/ppermute | solution.py:313
  113.9 9.9 %collective-permute-start.42 = (bf16[4,8,32,512]{3,2,1,0:T(8,128)(2,1)S(1)}, bf16[4,8,32,512]{3,2,1,0:T(8,128)(2,1)S(1)}, u32[]{:S(2)}, u32[]{:S(2)}) collective-permute-start(bf16[4,8,32,512]{3,2,1,0:T(8,128)(2,1)S(1)} %get-tuple-element.119), channel_id=1, source_target_pairs={{0,1},{1,0},{2,3},{3,2},{4,5},{5,4},{6,7},{7,6},{8,9},{9,8},{10,11... | collective-permute-start | bytes 3145736 | tf_op jit(solution)/shard_map/ppermute | solution.py:290
  119.6 1.9 collective-permute-start.30
  119.6 6.1 %collective-permute-start.33 = (bf16[4,8,32,512]{3,2,1,0:T(8,128)(2,1)S(1)}, bf16[4,8,32,512]{3,2,1,0:T(8,128)(2,1)S(1)}, u32[]{:S(2)}, u32[]{:S(2)}) collective-permute-start(bf16[4,8,32,512]{3,2,1,0:T(8,128)(2,1)S(1)} %get-tuple-element.113), channel_id=1, source_target_pairs={{0,1},{1,0},{2,3},{3,2},{4,5},{5,4},{6,7},{7,6},{8,9},{9,8},{10,11... | collective-permute-start | bytes 3145736 | tf_op jit(solution)/shard_map/ppermute | solution.py:290
  120.1 6.2 %collective-permute-start.36 = (bf16[4,8,32,512]{3,2,1,0:T(8,128)(2,1)S(1)}, bf16[4,8,32,512]{3,2,1,0:T(8,128)(2,1)S(1)}, u32[]{:S(2)}, u32[]{:S(2)}) collective-permute-start(bf16[4,8,32,512]{3,2,1,0:T(8,128)(2,1)S(1)} %get-tuple-element.115), channel_id=1, source_target_pairs={{0,1},{1,0},{2,3},{3,2},{4,5},{5,4},{6,7},{7,6},{8,9},{9,8},{10,11... | collective-permute-start | bytes 3145736 | tf_op jit(solution)/shard_map/ppermute | solution.py:290
  121.5 9.2 %collective-permute-start.46 = (bf16[2,32,16,128]{3,2,1,0:T(8,128)(2,1)S(1)}, bf16[2,32,16,128]{3,2,1,0:T(8,128)(2,1)S(1)}, u32[]{:S(2)}, u32[]{:S(2)}) collective-permute-start(bf16[2,32,16,128]{3,2,1,0:T(8,128)(2,1)S(1)} %add_convert_fusion.4), channel_id=1, source_target_pairs={{0,2},{1,3},{2,0},{3,1},{4,6},{5,7},{6,4},{7,5},{8,10},{9,11},{10,... | collective-permute-start | bytes 786440 | tf_op jit(solution)/shard_map/ppermute | solution.py:295
  123.1 67.9 %collective-permute-start.31 = (bf16[2,32,16,128]{3,2,1,0:T(8,128)(2,1)S(1)}, bf16[2,32,16,128]{3,2,1,0:T(8,128)(2,1)S(1)}, u32[]{:S(2)}, u32[]{:S(2)}) collective-permute-start(bf16[2,32,16,128]{3,2,1,0:T(8,128)(2,1)S(1)} %add_convert_fusion.9), channel_id=1, source_target_pairs={{0,2},{1,3},{2,0},{3,1},{4,6},{5,7},{6,4},{7,5},{8,10},{9,11},{10,... | collective-permute-start | bytes 786440 | tf_op jit(solution)/shard_map/ppermute | solution.py:295
  123.8 23.7 %collective-permute-start.40 = (bf16[2,8,32,512]{3,2,1,0:T(8,128)(2,1)S(1)}, bf16[2,8,32,512]{3,2,1,0:T(8,128)(2,1)S(1)}, u32[]{:S(2)}, u32[]{:S(2)}) collective-permute-start(bf16[2,8,32,512]{3,2,1,0:T(8,128)(2,1)S(1)} %add_convert_fusion.1), channel_id=1, source_target_pairs={{0,2},{1,3},{2,0},{3,1},{4,6},{5,7},{6,4},{7,5},{8,10},{9,11},{10,... | collective-permute-start | bytes 1572872 | tf_op jit(solution)/shard_map/ppermute | solution.py:295
  125.6 35.9 %collective-permute-start.43 = (bf16[2,8,32,512]{3,2,1,0:T(8,128)(2,1)S(1)}, bf16[2,8,32,512]{3,2,1,0:T(8,128)(2,1)S(1)}, u32[]{:S(2)}, u32[]{:S(2)}) collective-permute-start(bf16[2,8,32,512]{3,2,1,0:T(8,128)(2,1)S(1)} %add_convert_fusion), channel_id=1, source_target_pairs={{0,2},{1,3},{2,0},{3,1},{4,6},{5,7},{6,4},{7,5},{8,10},{9,11},{10,... | collective-permute-start | bytes 1572872 | tf_op jit(solution)/shard_map/ppermute | solution.py:295
  126.3 52.1 %collective-permute-start.34 = (bf16[2,8,32,512]{3,2,1,0:T(8,128)(2,1)S(1)}, bf16[2,8,32,512]{3,2,1,0:T(8,128)(2,1)S(1)}, u32[]{:S(2)}, u32[]{:S(2)}) collective-permute-start(bf16[2,8,32,512]{3,2,1,0:T(8,128)(2,1)S(1)} %add_convert_fusion.3), channel_id=1, source_target_pairs={{0,2},{1,3},{2,0},{3,1},{4,6},{5,7},{6,4},{7,5},{8,10},{9,11},{10,... | collective-permute-start | bytes 1572872 | tf_op jit(solution)/shard_map/ppermute | solution.py:295
  130.6 60.3 %collective-permute-start.37 = (bf16[2,8,32,512]{3,2,1,0:T(8,128)(2,1)S(1)}, bf16[2,8,32,512]{3,2,1,0:T(8,128)(2,1)S(1)}, u32[]{:S(2)}, u32[]{:S(2)}) collective-permute-start(bf16[2,8,32,512]{3,2,1,0:T(8,128)(2,1)S(1)} %add_convert_fusion.2), channel_id=1, source_target_pairs={{0,2},{1,3},{2,0},{3,1},{4,6},{5,7},{6,4},{7,5},{8,10},{9,11},{10,... | collective-permute-start | bytes 1572872 | tf_op jit(solution)/shard_map/ppermute | solution.py:295
  147.5 46.6 %collective-permute-start.47 = (bf16[1,32,16,128]{3,2,1,0:T(8,128)(2,1)S(1)}, bf16[1,32,16,128]{3,2,1,0:T(8,128)(2,1)S(1)}, u32[]{:S(2)}, u32[]{:S(2)}) collective-permute-start(bf16[1,32,16,128]{3,2,1,0:T(8,128)(2,1)S(1)} %add_convert_fusion.10), channel_id=1, source_target_pairs={{0,4},{1,5},{2,6},{3,7},{4,0},{5,1},{6,2},{7,3},{8,12},{9,13},{10,... | collective-permute-start | bytes 393224 | tf_op jit(solution)/shard_map/ppermute | solution.py:295
  161.5 68.8 %collective-permute-start.41 = (bf16[1,8,32,512]{3,2,1,0:T(8,128)(2,1)S(1)}, bf16[1,8,32,512]{3,2,1,0:T(8,128)(2,1)S(1)}, u32[]{:S(2)}, u32[]{:S(2)}) collective-permute-start(bf16[1,8,32,512]{3,2,1,0:T(8,128)(2,1)S(1)} %add_convert_fusion.6), channel_id=1, source_target_pairs={{0,4},{1,5},{2,6},{3,7},{4,0},{5,1},{6,2},{7,3},{8,12},{9,13},{10,... | collective-permute-start | bytes 786440 | tf_op jit(solution)/shard_map/ppermute | solution.py:295
  178.4 51.1 %collective-permute-start.44 = (bf16[1,8,32,512]{3,2,1,0:T(8,128)(2,1)S(1)}, bf16[1,8,32,512]{3,2,1,0:T(8,128)(2,1)S(1)}, u32[]{:S(2)}, u32[]{:S(2)}) collective-permute-start(bf16[1,8,32,512]{3,2,1,0:T(8,128)(2,1)S(1)} %add_convert_fusion.5), channel_id=1, source_target_pairs={{0,4},{1,5},{2,6},{3,7},{4,0},{5,1},{6,2},{7,3},{8,12},{9,13},{10,... | collective-permute-start | bytes 786440 | tf_op jit(solution)/shard_map/ppermute | solution.py:295
  190.9 41.1 %collective-permute-start.35 = (bf16[1,8,32,512]{3,2,1,0:T(8,128)(2,1)S(1)}, bf16[1,8,32,512]{3,2,1,0:T(8,128)(2,1)S(1)}, u32[]{:S(2)}, u32[]{:S(2)}) collective-permute-start(bf16[1,8,32,512]{3,2,1,0:T(8,128)(2,1)S(1)} %add_convert_fusion.8), channel_id=1, source_target_pairs={{0,4},{1,5},{2,6},{3,7},{4,0},{5,1},{6,2},{7,3},{8,12},{9,13},{10,... | collective-permute-start | bytes 786440 | tf_op jit(solution)/shard_map/ppermute | solution.py:295
  191.0 40.1 %collective-permute-start.38 = (bf16[1,8,32,512]{3,2,1,0:T(8,128)(2,1)S(1)}, bf16[1,8,32,512]{3,2,1,0:T(8,128)(2,1)S(1)}, u32[]{:S(2)}, u32[]{:S(2)}) collective-permute-start(bf16[1,8,32,512]{3,2,1,0:T(8,128)(2,1)S(1)} %add_convert_fusion.7), channel_id=1, source_target_pairs={{0,4},{1,5},{2,6},{3,7},{4,0},{5,1},{6,2},{7,3},{8,12},{9,13},{10,... | collective-permute-start | bytes 786440 | tf_op jit(solution)/shard_map/ppermute | solution.py:295
  194.1 34.0 %collective-permute-start.32 = (bf16[1,32,16,128]{3,2,1,0:T(8,128)(2,1)S(1)}, bf16[1,32,16,128]{3,2,1,0:T(8,128)(2,1)S(1)}, u32[]{:S(2)}, u32[]{:S(2)}) collective-permute-start(bf16[1,32,16,128]{3,2,1,0:T(8,128)(2,1)S(1)} %add_convert_fusion.11), channel_id=1, source_target_pairs={{0,4},{1,5},{2,6},{3,7},{4,0},{5,1},{6,2},{7,3},{8,12},{9,13},{10,... | collective-permute-start | bytes 393224 | tf_op jit(solution)/shard_map/ppermute | solution.py:295
  (11 other events, 146.5 us)

commit v2 on v1

--- a/solution.py
+++ b/solution.py
@@ -13,7 +13,7 @@
 WIDE = jnp.float32
 LANES = 128
 ROWS = 16
-PITCH = 24
+PITCH = 20
 SHARES = (2, 2, 2, 2)
 TILE = 128
 MIB = 1 << 20
@@ -313,7 +313,8 @@
             got.append(lax.ppermute(arrays[s], "block", [(i, i ^ s) for i in range(groups)]))
         return got
 
-    packed = mix_in(tokens, cotangent, first_up, second_down, groups)
+    first_in = [pltpu.with_memory_space_constraint(a, pltpu.HBM) for a in (tokens, cotangent, first_up, second_down)]
+    packed = mix_in(*first_in, groups)
     packed = [exchange(a) for a in packed]
     fold = second_up.shape[2] // second_up.shape[1]
     for_v, for_d, sums = [], [], []
@@ -399,6 +400,7 @@
             and line & (line - 1) == 0
             and blocks % ROWS == 0
             and width % LANES == 0
+            and width // groups % sum(SHARES) == 0
             and hidden % width == 0
             and width % (n_dp * ROWS) == 0
             and tokens.shape[0] // n_dp % LANES == 0

time: 233 us -> 228 us (0.979)
  local copies, waits for them, and re-layouts: 7.84 us -> 2.22 us
    unnamed x22 -> x14, local copies, waits for them, and re-layouts: 7.84 us -> 2.22 us
where the time goes in v2:
time: 228 us
  waiting for transfers between devices  134 us (59%)
  starting transfers between devices  54.5 us (24%)
  Pallas kernels  35.7 us (16%)
    ppermute x12, waiting for transfers between devices, line_sum(): lax.ppermute(total, 'dp', [(i, i ^ hop) for i in range(CORES * line)])  87.5 us
    ppermute x30, waiting for transfers between devices, exchange(): lax.ppermute(arrays[s], 'block', [(i, i ^ s) for i in range(groups)])  44.7 us
    ppermute x30, starting transfers between devices, exchange(): lax.ppermute(arrays[s], 'block', [(i, i ^ s) for i in range(groups)])  36.9 us
    pallas_call x4, Pallas kernels, feature(): pl.pallas_call(functools.partial(feature_body, groups, line), grid=(steps...  18.4 us
    ppermute x12, starting transfers between devices, line_sum(): lax.ppermute(total, 'dp', [(i, i ^ hop) for i in range(CORES * line)])  16.5 us
    pallas_call x2, Pallas kernels, mix_out(): pl.pallas_call(functools.partial(mix_out_body, groups, line, to_output),...  6.53 us
    pallas_call x6, Pallas kernels, settle(): pl.pallas_call(functools.partial(settle_body, fold, len(parts)), grid=(pa...  6.12 us
    pallas_call x1, Pallas kernels, mix_in(): pl.pallas_call(functools.partial(mix_in_body, groups), grid=(blocks // RO...  4.68 us
  transfers between devices with their start and end apart: 48, of which 17 were waited for; matrix products, arithmetic and copies ran while one was open for 1% of the time, Pallas kernels for 13%

profile of v2, /device:TPU:0, one launch (start us, length us, event | category | flops | bytes accessed | tf_op | source)
XLA Modules:
  0.0 228.1 jit_solution(1091923427020574229)
XLA Ops:
  0.6 4.7 %mix_in.1 = (bf16[2,8,32,256]{3,2,1,0:T(8,128)(2,1)S(1)}, bf16[2,8,32,256]{3,2,1,0:T(8,128)(2,1)S(1)}, bf16[2,8,32,256]{3,2,1,0:T(8,128)(2,1)S(1)}, bf16[2,8,32,...) custom-call(bf16[256,4096]{1,0:T(8,128)(2,1)} %rest_16_.3, ...), custom_call_target="tpu_custom_call" | custom-call | flops 536870912 | bytes 8388608 | tf_op jit(solution)/shard_map/mix_in/pallas_call | solution.py:76
  5.3 3.0 %collective-permute-start = (bf16[2,8,32,256]{3,2,1,0:T(8,128)(2,1)S(1)}, bf16[2,8,32,256]{3,2,1,0:T(8,128)(2,1)S(1)}, u32[]{:S(2)}, u32[]{:S(2)}) collective-permute-start(bf16[2,8,32,256]{3,2,1,0:T(8,128)(2,1)S(1)} %get-tuple-element.69), channel_id=1, source_target_pairs={{0,8},{8,0},{16,24},{24,16},{1,9},{9,1},{17,25},{25,17},{2,10},{10... | collective-permute-start | bytes 786440 | tf_op jit(solution)/shard_map/ppermute | solution.py:313
  8.4 2.0 collective-permute-start.7
  10.4 1.4 collective-permute-start.8
  11.9 3.6 %collective-permute-done.rest_1_ = bf16[2,8,32,256]{3,2,1,0:T(8,128)(2,1)S(1)} collective-permute-done((bf16[2,8,32,256]{3,2,1,0:T(8,128)(2,1)S(1)}, bf16[2,8,32,256]{3,2,1,0:T(8,128)(2,1)S(1)}, u32[]{:S(2)}, u32[]{:S(2)}) %collective-permute-start) | collective-permute-done | bytes 262176 | tf_op jit(solution)/shard_map/ppermute | solution.py:313
  15.5 2.0 collective-permute-start.19
  17.6 3.6 %collective-permute-done.6.rest_1_ = bf16[2,8,32,256]{3,2,1,0:T(8,128)(2,1)S(1)} collective-permute-done((bf16[2,8,32,256]{3,2,1,0:T(8,128)(2,1)S(1)}, bf16[2,8,32,256]{3,2,1,0:T(8,128)(2,1)S(1)}, u32[]{:S(2)}, u32[]{:S(2)}) %collective-permute-start.6) | collective-permute-done | bytes 262176 | tf_op jit(solution)/shard_map/ppermute | solution.py:313
  21.1 3.0 %collective-permute-start.20 = (bf16[2,8,32,256]{3,2,1,0:T(8,128)(2,1)S(1)}, bf16[2,8,32,256]{3,2,1,0:T(8,128)(2,1)S(1)}, u32[]{:S(2)}, u32[]{:S(2)}) collective-permute-start(bf16[2,8,32,256]{3,2,1,0:T(8,128)(2,1)S(1)} %get-tuple-element.95), channel_id=1, source_target_pairs={{0,24},{8,16},{16,8},{24,0},{1,25},{9,17},{17,9},{25,1},{2,26},{10... | collective-permute-start | bytes 786440 | tf_op jit(solution)/shard_map/ppermute | solution.py:313
  24.7 3.6 %collective-permute-done.8.rest_3_ = bf16[2,8,32,256]{3,2,1,0:T(8,128)(2,1)S(1)} collective-permute-done((bf16[2,8,32,256]{3,2,1,0:T(8,128)(2,1)S(1)}, bf16[2,8,32,256]{3,2,1,0:T(8,128)(2,1)S(1)}, u32[]{:S(2)}, u32[]{:S(2)}) %collective-permute-start.8) | collective-permute-done | bytes 262176 | tf_op jit(solution)/shard_map/ppermute | solution.py:313
  28.3 4.1 %collective-permute-done.18.rest_1_ = bf16[2,8,32,256]{3,2,1,0:T(8,128)(2,1)S(1)} collective-permute-done((bf16[2,8,32,256]{3,2,1,0:T(8,128)(2,1)S(1)}, bf16[2,8,32,256]{3,2,1,0:T(8,128)(2,1)S(1)}, u32[]{:S(2)}, u32[]{:S(2)}) %collective-permute-start.18) | collective-permute-done | bytes 262176 | tf_op jit(solution)/shard_map/ppermute | solution.py:313
  32.4 3.0 %collective-permute-start.14 = (bf16[2,8,32,256]{3,2,1,0:T(8,128)(2,1)S(1)}, bf16[2,8,32,256]{3,2,1,0:T(8,128)(2,1)S(1)}, u32[]{:S(2)}, u32[]{:S(2)}) collective-permute-start(bf16[2,8,32,256]{3,2,1,0:T(8,128)(2,1)S(1)} %get-tuple-element.87), channel_id=1, source_target_pairs={{0,24},{8,16},{16,8},{24,0},{1,25},{9,17},{17,9},{25,1},{2,26},{10... | collective-permute-start | bytes 786440 | tf_op jit(solution)/shard_map/ppermute | solution.py:313
  35.4 2.2 copy-done.1
  37.6 4.6 %feature.5 = (bf16[2,8,32,256]{3,2,1,0:T(8,128)(2,1)S(1)}, bf16[2,8,32,256]{3,2,1,0:T(8,128)(2,1)S(1)}, bf16[2,8,32,256]{3,2,1,0:T(8,128)(2,1)S(1)}, bf16[2,8,32...) custom-call(bf16[2,8,32,256]{3,2,1,0:T(8,128)(2,1)S(1)} %get-tuple-element.76.rest, ...), custom_call_target="tpu_custom_call" | custom-call | flops 1610612736 | bytes 6291456 | tf_op jit(solution)/shard_map/feature/pallas_call | solution.py:168
  42.7 1.5 collective-permute-start.2
  44.2 4.5 %feature.7 = (bf16[1,8,32,256]{3,2,1,0:T(8,128)(2,1)S(1)}, bf16[1,8,32,256]{3,2,1,0:T(8,128)(2,1)S(1)}, bf16[1,8,32,256]{3,2,1,0:T(8,128)(2,1)S(1)}, bf16[1,8,32...) custom-call(bf16[2,8,32,256]{3,2,1,0:T(8,128)(2,1)S(1)} %get-tuple-e, ...), custom_call_target="tpu_custom_call" | custom-call | flops 1610612736 | bytes 6291456 | tf_op jit(solution)/shard_map/feature/pallas_call | solution.py:168
  48.8 1.6 collective-permute-start.9
  51.0 4.5 %feature.6 = (bf16[1,8,32,256]{3,2,1,0:T(8,128)(2,1)S(1)}, bf16[1,8,32,256]{3,2,1,0:T(8,128)(2,1)S(1)}, bf16[1,8,32,256]{3,2,1,0:T(8,128)(2,1)S(1)}, bf16[1,8,32...) custom-call(bf16[2,8,32,256]{3,2,1,0:T(8,128)(2,1)S(1)} %get-tuple-e, ...), custom_call_target="tpu_custom_call" | custom-call | flops 1610612736 | bytes 6291456 | tf_op jit(solution)/shard_map/feature/pallas_call | solution.py:168
  55.5 5.2 %collective-permute-done.1.rest_2_ = bf16[2,8,32,256]{3,2,1,0:T(8,128)(2,1)S(1)} collective-permute-done((bf16[2,8,32,256]{3,2,1,0:T(8,128)(2,1)S(1)}, bf16[2,8,32,256]{3,2,1,0:T(8,128)(2,1)S(1)}, u32[]{:S(2)}, u32[]{:S(2)}) %collective-permute-start.1) | collective-permute-done | bytes 262176 | tf_op jit(solution)/shard_map/ppermute | solution.py:313
  61.2 1.4 collective-permute-start.15
  63.4 2.1 collective-permute-start.16
  65.5 1.4 collective-permute-start.17
  66.9 4.7 %feature.4 = (bf16[2,8,32,256]{3,2,1,0:T(8,128)(2,1)S(1)}, bf16[2,8,32,256]{3,2,1,0:T(8,128)(2,1)S(1)}, bf16[2,8,32,256]{3,2,1,0:T(8,128)(2,1)S(1)}, bf16[2,8,32...) custom-call(bf16[2,8,32,256]{3,2,1,0:T(8,128)(2,1)S(1)} %get-tuple-element.68.rest, ...), custom_call_target="tpu_custom_call" | custom-call | flops 1610612736 | bytes 6291456 | tf_op jit(solution)/shard_map/feature/pallas_call | solution.py:168
  71.7 1.6 collective-permute-start.10
  73.3 1.9 collective-permute-start.3
  75.2 1.5 collective-permute-start.4
  76.8 11.1 %collective-permute-done.10.rest_6_ = bf16[2,8,32,256]{3,2,1,0:T(8,128)(2,1)S(1)} collective-permute-done((bf16[2,8,32,256]{3,2,1,0:T(8,128)(2,1)S(1)}, bf16[2,8,32,256]{3,2,1,0:T(8,128)(2,1)S(1)}, u32[]{:S(2)}, u32[]{:S(2)}) %collective-permute-start.10) | collective-permute-done | bytes 262176 | tf_op jit(solution)/shard_map/ppermute | solution.py:313
  89.0 2.4 %collective-permute-start.29 = (bf16[1,8,32,256]{3,2,1,0:T(8,128)(2,1)S(1)}, bf16[1,8,32,256]{3,2,1,0:T(8,128)(2,1)S(1)}, u32[]{:S(2)}, u32[]{:S(2)}) collective-permute-start(bf16[1,8,32,256]{3,2,1,0:T(8,128)(2,1)S(1)} %get-tuple-element.108), channel_id=1, source_target_pairs={{0,24},{8,16},{16,8},{24,0},{1,25},{9,17},{17,9},{25,1},{2,26},{10... | collective-permute-start | bytes 393224 | tf_op jit(solution)/shard_map/ppermute | solution.py:313
  91.4 7.5 %collective-permute-done.4.rest_2_ = bf16[2,8,32,256]{3,2,1,0:T(8,128)(2,1)S(1)} collective-permute-done((bf16[2,8,32,256]{3,2,1,0:T(8,128)(2,1)S(1)}, bf16[2,8,32,256]{3,2,1,0:T(8,128)(2,1)S(1)}, u32[]{:S(2)}, u32[]{:S(2)}) %collective-permute-start.4) | collective-permute-done | bytes 262176 | tf_op jit(solution)/shard_map/ppermute | solution.py:313
  98.9 3.2 %mix_out.2 = (bf16[256,4096]{1,0:T(8,128)(2,1)}, bf16[4,32,16,128]{3,2,1,0:T(8,128)(2,1)S(1)}, bf16[4,32,16,128]{3,2,1,0:T(8,128)(2,1)S(1)}) custom-call(bf16[2,8,32,256]{3,2,1,0:T(8,128)(2,1)S(1)} %get-tuple-element.72.rest_0_, bf16[2,8,32,256]{3,2,1,0:T(8,128)(2,1)S(1)} %collective-permute-done.3.rest_1_, ...), custom_call_target="tpu_custom_call" | custom-call | flops 536870912 | bytes 8388608 | tf_op jit(solution)/shard_map/mix_out/pallas_call | solution.py:238
  104.0 2.2 collective-permute-start.26
  106.2 2.9 %collective-permute-done.24.rest_9_ = bf16[1,8,32,256]{3,2,1,0:T(8,128)(2,1)S(1)} collective-permute-done((bf16[1,8,32,256]{3,2,1,0:T(8,128)(2,1)S(1)}, bf16[1,8,32,256]{3,2,1,0:T(8,128)(2,1)S(1)}, u32[]{:S(2)}, u32[]{:S(2)}) %collective-permute-start.24) | collective-permute-done | bytes 131104 | tf_op jit(solution)/shard_map/ppermute | solution.py:313
  109.0 2.4 %collective-permute-done.25.rest_10_ = bf16[1,8,32,256]{3,2,1,0:T(8,128)(2,1)S(1)} collective-permute-done((bf16[1,8,32,256]{3,2,1,0:T(8,128)(2,1)S(1)}, bf16[1,8,32,256]{3,2,1,0:T(8,128)(2,1)S(1)}, u32[]{:S(2)}, u32[]{:S(2)}) %collective-permute-start.25) | collective-permute-done | bytes 131104 | tf_op jit(solution)/shard_map/ppermute | solution.py:313
  111.4 3.3 %mix_out.3 = (bf16[256,4096]{1,0:T(8,128)(2,1)}, bf16[4,32,16,128]{3,2,1,0:T(8,128)(2,1)S(1)}, bf16[4,32,16,128]{3,2,1,0:T(8,128)(2,1)S(1)}) custom-call(bf16[2,8,32,256]{3,2,1,0:T(8,128)(2,1)S(1)} %get-tuple-element.72.rest_0_, bf16[2,8,32,256]{3,2,1,0:T(8,128)(2,1)S(1)} %collective-permute-done.3.rest_1_, ...), custom_call_target="tpu_custom_call" | custom-call | flops 536870912 | bytes 8388608 | tf_op jit(solution)/shard_map/mix_out/pallas_call | solution.py:238
  116.6 1.6 collective-permute-start.46
  119.0 1.6 collective-permute-start.40
  121.5 1.6 collective-permute-start.34
  123.3 2.5 %collective-permute-done.46.rest_2_ = bf16[2,32,16,128]{3,2,1,0:T(8,128)(2,1)S(1)} collective-permute-done((bf16[2,32,16,128]{3,2,1,0:T(8,128)(2,1)S(1)}, bf16[2,32,16,128]{3,2,1,0:T(8,128)(2,1)S(1)}, u32[]{:S(2)}, u32[]{:S(2)}) %collective-permute-start.46) | collective-permute-done | bytes 262176 | tf_op jit(solution)/shard_map/ppermute | solution.py:295
  125.8 1.6 collective-permute-start.37
  127.4 15.2 %collective-permute-done.40.rest_2_ = bf16[2,8,32,512]{3,2,1,0:T(8,128)(2,1)S(1)} collective-permute-done((bf16[2,8,32,512]{3,2,1,0:T(8,128)(2,1)S(1)}, bf16[2,8,32,512]{3,2,1,0:T(8,128)(2,1)S(1)}, u32[]{:S(2)}, u32[]{:S(2)}) %collective-permute-start.40) | collective-permute-done | bytes 524320 | tf_op jit(solution)/shard_map/ppermute | solution.py:295
  142.7 2.6 %collective-permute-start.47 = (bf16[1,32,16,128]{3,2,1,0:T(8,128)(2,1)S(1)}, bf16[1,32,16,128]{3,2,1,0:T(8,128)(2,1)S(1)}, u32[]{:S(2)}, u32[]{:S(2)}) collective-permute-start(bf16[1,32,16,128]{3,2,1,0:T(8,128)(2,1)S(1)} %add_convert_fusion.10), channel_id=1, source_target_pairs={{0,4},{1,5},{2,6},{3,7},{4,0},{5,1},{6,2},{7,3},{8,12},{9,13},{10,... | collective-permute-start | bytes 393224 | tf_op jit(solution)/shard_map/ppermute | solution.py:295
  145.3 11.3 %collective-permute-done.43.rest_2_ = bf16[2,8,32,512]{3,2,1,0:T(8,128)(2,1)S(1)} collective-permute-done((bf16[2,8,32,512]{3,2,1,0:T(8,128)(2,1)S(1)}, bf16[2,8,32,512]{3,2,1,0:T(8,128)(2,1)S(1)}, u32[]{:S(2)}, u32[]{:S(2)}) %collective-permute-start.43) | collective-permute-done | bytes 524320 | tf_op jit(solution)/shard_map/ppermute | solution.py:295
  156.7 1.7 collective-permute-start.41
  158.5 15.1 %collective-permute-done.34.rest_2_ = bf16[2,8,32,512]{3,2,1,0:T(8,128)(2,1)S(1)} collective-permute-done((bf16[2,8,32,512]{3,2,1,0:T(8,128)(2,1)S(1)}, bf16[2,8,32,512]{3,2,1,0:T(8,128)(2,1)S(1)}, u32[]{:S(2)}, u32[]{:S(2)}) %collective-permute-start.34) | collective-permute-done | bytes 524320 | tf_op jit(solution)/shard_map/ppermute | solution.py:295
  173.5 1.7 collective-permute-start.44
  175.3 10.7 %collective-permute-done.37.rest_2_ = bf16[2,8,32,512]{3,2,1,0:T(8,128)(2,1)S(1)} collective-permute-done((bf16[2,8,32,512]{3,2,1,0:T(8,128)(2,1)S(1)}, bf16[2,8,32,512]{3,2,1,0:T(8,128)(2,1)S(1)}, u32[]{:S(2)}, u32[]{:S(2)}) %collective-permute-start.37) | collective-permute-done | bytes 524320 | tf_op jit(solution)/shard_map/ppermute | solution.py:295
  186.2 3.0 %collective-permute-start.38 = (bf16[1,8,32,512]{3,2,1,0:T(8,128)(2,1)S(1)}, bf16[1,8,32,512]{3,2,1,0:T(8,128)(2,1)S(1)}, u32[]{:S(2)}, u32[]{:S(2)}) collective-permute-start(bf16[1,8,32,512]{3,2,1,0:T(8,128)(2,1)S(1)} %add_convert_fusion.7), channel_id=1, source_target_pairs={{0,4},{1,5},{2,6},{3,7},{4,0},{5,1},{6,2},{7,3},{8,12},{9,13},{10,... | collective-permute-start | bytes 786440 | tf_op jit(solution)/shard_map/ppermute | solution.py:295
  189.3 1.4 settle.11
  190.7 32.6 %collective-permute-done.32.rest_3_ = bf16[1,32,16,128]{3,2,1,0:T(8,128)(2,1)S(1)} collective-permute-done((bf16[1,32,16,128]{3,2,1,0:T(8,128)(2,1)S(1)}, bf16[1,32,16,128]{3,2,1,0:T(8,128)(2,1)S(1)}, u32[]{:S(2)}, u32[]{:S(2)}) %collective-permute-start.32) | collective-permute-done | bytes 131104 | tf_op jit(solution)/shard_map/ppermute | solution.py:295
  (87 shorter events, 15.3 us)
Async XLA Ops:
  5.3 10.2 %collective-permute-start = (bf16[2,8,32,256]{3,2,1,0:T(8,128)(2,1)S(1)}, bf16[2,8,32,256]{3,2,1,0:T(8,128)(2,1)S(1)}, u32[]{:S(2)}, u32[]{:S(2)}) collective-permute-start(bf16[2,8,32,256]{3,2,1,0:T(8,128)(2,1)S(1)} %get-tuple-element.69), channel_id=1, source_target_pairs={{0,8},{8,0},{16,24},{24,16},{1,9},{9,1},{17,25},{25,17},{2,10},{10... | collective-permute-start | bytes 786440 | tf_op jit(solution)/shard_map/ppermute | solution.py:313
  8.4 12.8 %collective-permute-start.6 = (bf16[2,8,32,256]{3,2,1,0:T(8,128)(2,1)S(1)}, bf16[2,8,32,256]{3,2,1,0:T(8,128)(2,1)S(1)}, u32[]{:S(2)}, u32[]{:S(2)}) collective-permute-start(bf16[2,8,32,256]{3,2,1,0:T(8,128)(2,1)S(1)} %get-tuple-element.77), channel_id=1, source_target_pairs={{0,8},{8,0},{16,24},{24,16},{1,9},{9,1},{17,25},{25,17},{2,10},{10... | collective-permute-start | bytes 786440 | tf_op jit(solution)/shard_map/ppermute | solution.py:313
  8.4 15.7 %collective-permute-start.7 = (bf16[2,8,32,256]{3,2,1,0:T(8,128)(2,1)S(1)}, bf16[2,8,32,256]{3,2,1,0:T(8,128)(2,1)S(1)}, u32[]{:S(2)}, u32[]{:S(2)}) collective-permute-start(bf16[2,8,32,256]{3,2,1,0:T(8,128)(2,1)S(1)} %get-tuple-element.78), channel_id=1, source_target_pairs={{0,16},{8,24},{16,0},{24,8},{1,17},{9,25},{17,1},{25,9},{2,18},{10... | collective-permute-start | bytes 786440 | tf_op jit(solution)/shard_map/ppermute | solution.py:313
  10.4 17.9 %collective-permute-start.8 = (bf16[2,8,32,256]{3,2,1,0:T(8,128)(2,1)S(1)}, bf16[2,8,32,256]{3,2,1,0:T(8,128)(2,1)S(1)}, u32[]{:S(2)}, u32[]{:S(2)}) collective-permute-start(bf16[2,8,32,256]{3,2,1,0:T(8,128)(2,1)S(1)} %get-tuple-element.79), channel_id=1, source_target_pairs={{0,24},{8,16},{16,8},{24,0},{1,25},{9,17},{17,9},{25,1},{2,26},{10... | collective-permute-start | bytes 786440 | tf_op jit(solution)/shard_map/ppermute | solution.py:313
  11.9 20.6 %collective-permute-start.18 = (bf16[2,8,32,256]{3,2,1,0:T(8,128)(2,1)S(1)}, bf16[2,8,32,256]{3,2,1,0:T(8,128)(2,1)S(1)}, u32[]{:S(2)}, u32[]{:S(2)}) collective-permute-start(bf16[2,8,32,256]{3,2,1,0:T(8,128)(2,1)S(1)} %get-tuple-element.93), channel_id=1, source_target_pairs={{0,8},{8,0},{16,24},{24,16},{1,9},{9,1},{17,25},{25,17},{2,10},{10... | collective-permute-start | bytes 786440 | tf_op jit(solution)/shard_map/ppermute | solution.py:313
  15.5 26.7 %collective-permute-start.19 = (bf16[2,8,32,256]{3,2,1,0:T(8,128)(2,1)S(1)}, bf16[2,8,32,256]{3,2,1,0:T(8,128)(2,1)S(1)}, u32[]{:S(2)}, u32[]{:S(2)}) collective-permute-start(bf16[2,8,32,256]{3,2,1,0:T(8,128)(2,1)S(1)} %get-tuple-element.94), channel_id=1, source_target_pairs={{0,16},{8,24},{16,0},{24,8},{1,17},{9,25},{17,1},{25,9},{2,18},{10... | collective-permute-start | bytes 786440 | tf_op jit(solution)/shard_map/ppermute | solution.py:313
  21.1 21.6 %collective-permute-start.20 = (bf16[2,8,32,256]{3,2,1,0:T(8,128)(2,1)S(1)}, bf16[2,8,32,256]{3,2,1,0:T(8,128)(2,1)S(1)}, u32[]{:S(2)}, u32[]{:S(2)}) collective-permute-start(bf16[2,8,32,256]{3,2,1,0:T(8,128)(2,1)S(1)} %get-tuple-element.95), channel_id=1, source_target_pairs={{0,24},{8,16},{16,8},{24,0},{1,25},{9,17},{17,9},{25,1},{2,26},{10... | collective-permute-start | bytes 786440 | tf_op jit(solution)/shard_map/ppermute | solution.py:313
  24.1 24.7 %collective-permute-start.12 = (bf16[2,8,32,256]{3,2,1,0:T(8,128)(2,1)S(1)}, bf16[2,8,32,256]{3,2,1,0:T(8,128)(2,1)S(1)}, u32[]{:S(2)}, u32[]{:S(2)}) collective-permute-start(bf16[2,8,32,256]{3,2,1,0:T(8,128)(2,1)S(1)} %get-tuple-element.85), channel_id=1, source_target_pairs={{0,8},{8,0},{16,24},{24,16},{1,9},{9,1},{17,25},{25,17},{2,10},{10... | collective-permute-start | bytes 786440 | tf_op jit(solution)/shard_map/ppermute | solution.py:313
  28.3 22.1 %collective-permute-start.13 = (bf16[2,8,32,256]{3,2,1,0:T(8,128)(2,1)S(1)}, bf16[2,8,32,256]{3,2,1,0:T(8,128)(2,1)S(1)}, u32[]{:S(2)}, u32[]{:S(2)}) collective-permute-start(bf16[2,8,32,256]{3,2,1,0:T(8,128)(2,1)S(1)} %get-tuple-element.86), channel_id=1, source_target_pairs={{0,16},{8,24},{16,0},{24,8},{1,17},{9,25},{17,1},{25,9},{2,18},{10... | collective-permute-start | bytes 786440 | tf_op jit(solution)/shard_map/ppermute | solution.py:313
  32.4 18.5 %collective-permute-start.14 = (bf16[2,8,32,256]{3,2,1,0:T(8,128)(2,1)S(1)}, bf16[2,8,32,256]{3,2,1,0:T(8,128)(2,1)S(1)}, u32[]{:S(2)}, u32[]{:S(2)}) collective-permute-start(bf16[2,8,32,256]{3,2,1,0:T(8,128)(2,1)S(1)} %get-tuple-element.87), channel_id=1, source_target_pairs={{0,24},{8,16},{16,8},{24,0},{1,25},{9,17},{17,9},{25,1},{2,26},{10... | collective-permute-start | bytes 786440 | tf_op jit(solution)/shard_map/ppermute | solution.py:313
  42.2 18.5 %collective-permute-start.1 = (bf16[2,8,32,256]{3,2,1,0:T(8,128)(2,1)S(1)}, bf16[2,8,32,256]{3,2,1,0:T(8,128)(2,1)S(1)}, u32[]{:S(2)}, u32[]{:S(2)}) collective-permute-start(bf16[2,8,32,256]{3,2,1,0:T(8,128)(2,1)S(1)} %get-tuple-element.70), channel_id=1, source_target_pairs={{0,16},{8,24},{16,0},{24,8},{1,17},{9,25},{17,1},{25,9},{2,18},{10... | collective-permute-start | bytes 786440 | tf_op jit(solution)/shard_map/ppermute | solution.py:313
  42.7 18.4 %collective-permute-start.2 = (bf16[2,8,32,256]{3,2,1,0:T(8,128)(2,1)S(1)}, bf16[2,8,32,256]{3,2,1,0:T(8,128)(2,1)S(1)}, u32[]{:S(2)}, u32[]{:S(2)}) collective-permute-start(bf16[2,8,32,256]{3,2,1,0:T(8,128)(2,1)S(1)} %get-tuple-element.71), channel_id=1, source_target_pairs={{0,24},{8,16},{16,8},{24,0},{1,25},{9,17},{17,9},{25,1},{2,26},{10... | collective-permute-start | bytes 786440 | tf_op jit(solution)/shard_map/ppermute | solution.py:313
  48.8 28.0 %collective-permute-start.9 = (bf16[2,8,32,256]{3,2,1,0:T(8,128)(2,1)S(1)}, bf16[2,8,32,256]{3,2,1,0:T(8,128)(2,1)S(1)}, u32[]{:S(2)}, u32[]{:S(2)}) collective-permute-start(bf16[2,8,32,256]{3,2,1,0:T(8,128)(2,1)S(1)} %get-tuple-element.81), channel_id=1, source_target_pairs={{0,8},{8,0},{16,24},{24,16},{1,9},{9,1},{17,25},{25,17},{2,10},{10... | collective-permute-start | bytes 786440 | tf_op jit(solution)/shard_map/ppermute | solution.py:313
  50.3 13.1 %collective-permute-start.21 = (bf16[1,8,32,256]{3,2,1,0:T(8,128)(2,1)S(1)}, bf16[1,8,32,256]{3,2,1,0:T(8,128)(2,1)S(1)}, u32[]{:S(2)}, u32[]{:S(2)}) collective-permute-start(bf16[1,8,32,256]{3,2,1,0:T(8,128)(2,1)S(1)} %get-tuple-element.97), channel_id=1, source_target_pairs={{0,8},{8,0},{16,24},{24,16},{1,9},{9,1},{17,25},{25,17},{2,10},{10... | collective-permute-start | bytes 393224 | tf_op jit(solution)/shard_map/ppermute | solution.py:313
  50.9 14.6 %collective-permute-start.22 = (bf16[1,8,32,256]{3,2,1,0:T(8,128)(2,1)S(1)}, bf16[1,8,32,256]{3,2,1,0:T(8,128)(2,1)S(1)}, u32[]{:S(2)}, u32[]{:S(2)}) collective-permute-start(bf16[1,8,32,256]{3,2,1,0:T(8,128)(2,1)S(1)} %get-tuple-element.98), channel_id=1, source_target_pairs={{0,16},{8,24},{16,0},{24,8},{1,17},{9,25},{17,1},{25,9},{2,18},{10... | collective-permute-start | bytes 393224 | tf_op jit(solution)/shard_map/ppermute | solution.py:313
  60.7 11.0 %collective-permute-start.23 = (bf16[1,8,32,256]{3,2,1,0:T(8,128)(2,1)S(1)}, bf16[1,8,32,256]{3,2,1,0:T(8,128)(2,1)S(1)}, u32[]{:S(2)}, u32[]{:S(2)}) collective-permute-start(bf16[1,8,32,256]{3,2,1,0:T(8,128)(2,1)S(1)} %get-tuple-element.99), channel_id=1, source_target_pairs={{0,24},{8,16},{16,8},{24,0},{1,25},{9,17},{17,9},{25,1},{2,26},{10... | collective-permute-start | bytes 393224 | tf_op jit(solution)/shard_map/ppermute | solution.py:313
  61.2 12.1 %collective-permute-start.15 = (bf16[1,8,32,256]{3,2,1,0:T(8,128)(2,1)S(1)}, bf16[1,8,32,256]{3,2,1,0:T(8,128)(2,1)S(1)}, u32[]{:S(2)}, u32[]{:S(2)}) collective-permute-start(bf16[1,8,32,256]{3,2,1,0:T(8,128)(2,1)S(1)} %get-tuple-element.89), channel_id=1, source_target_pairs={{0,8},{8,0},{16,24},{24,16},{1,9},{9,1},{17,25},{25,17},{2,10},{10... | collective-permute-start | bytes 393224 | tf_op jit(solution)/shard_map/ppermute | solution.py:313
  63.4 9.9 %collective-permute-start.16 = (bf16[1,8,32,256]{3,2,1,0:T(8,128)(2,1)S(1)}, bf16[1,8,32,256]{3,2,1,0:T(8,128)(2,1)S(1)}, u32[]{:S(2)}, u32[]{:S(2)}) collective-permute-start(bf16[1,8,32,256]{3,2,1,0:T(8,128)(2,1)S(1)} %get-tuple-element.90), channel_id=1, source_target_pairs={{0,16},{8,24},{16,0},{24,8},{1,17},{9,25},{17,1},{25,9},{2,18},{10... | collective-permute-start | bytes 393224 | tf_op jit(solution)/shard_map/ppermute | solution.py:313
  65.5 9.8 %collective-permute-start.17 = (bf16[1,8,32,256]{3,2,1,0:T(8,128)(2,1)S(1)}, bf16[1,8,32,256]{3,2,1,0:T(8,128)(2,1)S(1)}, u32[]{:S(2)}, u32[]{:S(2)}) collective-permute-start(bf16[1,8,32,256]{3,2,1,0:T(8,128)(2,1)S(1)} %get-tuple-element.91), channel_id=1, source_target_pairs={{0,24},{8,16},{16,8},{24,0},{1,25},{9,17},{17,9},{25,1},{2,26},{10... | collective-permute-start | bytes 393224 | tf_op jit(solution)/shard_map/ppermute | solution.py:313
  71.7 16.2 %collective-permute-start.10 = (bf16[2,8,32,256]{3,2,1,0:T(8,128)(2,1)S(1)}, bf16[2,8,32,256]{3,2,1,0:T(8,128)(2,1)S(1)}, u32[]{:S(2)}, u32[]{:S(2)}) collective-permute-start(bf16[2,8,32,256]{3,2,1,0:T(8,128)(2,1)S(1)} %get-tuple-element.82), channel_id=1, source_target_pairs={{0,16},{8,24},{16,0},{24,8},{1,17},{9,25},{17,1},{25,9},{2,18},{10... | collective-permute-start | bytes 786440 | tf_op jit(solution)/shard_map/ppermute | solution.py:313
  73.2 15.2 %collective-permute-start.11 = (bf16[2,8,32,256]{3,2,1,0:T(8,128)(2,1)S(1)}, bf16[2,8,32,256]{3,2,1,0:T(8,128)(2,1)S(1)}, u32[]{:S(2)}, u32[]{:S(2)}) collective-permute-start(bf16[2,8,32,256]{3,2,1,0:T(8,128)(2,1)S(1)} %get-tuple-element.83), channel_id=1, source_target_pairs={{0,24},{8,16},{16,8},{24,0},{1,25},{9,17},{17,9},{25,1},{2,26},{10... | collective-permute-start | bytes 786440 | tf_op jit(solution)/shard_map/ppermute | solution.py:313
  73.3 15.7 %collective-permute-start.3 = (bf16[2,8,32,256]{3,2,1,0:T(8,128)(2,1)S(1)}, bf16[2,8,32,256]{3,2,1,0:T(8,128)(2,1)S(1)}, u32[]{:S(2)}, u32[]{:S(2)}) collective-permute-start(bf16[2,8,32,256]{3,2,1,0:T(8,128)(2,1)S(1)} %get-tuple-element.73), channel_id=1, source_target_pairs={{0,8},{8,0},{16,24},{24,16},{1,9},{9,1},{17,25},{25,17},{2,10},{10... | collective-permute-start | bytes 786440 | tf_op jit(solution)/shard_map/ppermute | solution.py:313
  75.2 23.6 %collective-permute-start.4 = (bf16[2,8,32,256]{3,2,1,0:T(8,128)(2,1)S(1)}, bf16[2,8,32,256]{3,2,1,0:T(8,128)(2,1)S(1)}, u32[]{:S(2)}, u32[]{:S(2)}) collective-permute-start(bf16[2,8,32,256]{3,2,1,0:T(8,128)(2,1)S(1)} %get-tuple-element.74), channel_id=1, source_target_pairs={{0,16},{8,24},{16,0},{24,8},{1,17},{9,25},{17,1},{25,9},{2,18},{10... | collective-permute-start | bytes 786440 | tf_op jit(solution)/shard_map/ppermute | solution.py:313
  76.8 22.1 %collective-permute-start.5 = (bf16[2,8,32,256]{3,2,1,0:T(8,128)(2,1)S(1)}, bf16[2,8,32,256]{3,2,1,0:T(8,128)(2,1)S(1)}, u32[]{:S(2)}, u32[]{:S(2)}) collective-permute-start(bf16[2,8,32,256]{3,2,1,0:T(8,128)(2,1)S(1)} %get-tuple-element.75), channel_id=1, source_target_pairs={{0,24},{8,16},{16,8},{24,0},{1,25},{9,17},{17,9},{25,1},{2,26},{10... | collective-permute-start | bytes 786440 | tf_op jit(solution)/shard_map/ppermute | solution.py:313
  87.9 14.8 %collective-permute-start.27 = (bf16[1,8,32,256]{3,2,1,0:T(8,128)(2,1)S(1)}, bf16[1,8,32,256]{3,2,1,0:T(8,128)(2,1)S(1)}, u32[]{:S(2)}, u32[]{:S(2)}) collective-permute-start(bf16[1,8,32,256]{3,2,1,0:T(8,128)(2,1)S(1)} %get-tuple-element.106), channel_id=1, source_target_pairs={{0,8},{8,0},{16,24},{24,16},{1,9},{9,1},{17,25},{25,17},{2,10},{10... | collective-permute-start | bytes 393224 | tf_op jit(solution)/shard_map/ppermute | solution.py:313
  88.5 15.0 %collective-permute-start.28 = (bf16[1,8,32,256]{3,2,1,0:T(8,128)(2,1)S(1)}, bf16[1,8,32,256]{3,2,1,0:T(8,128)(2,1)S(1)}, u32[]{:S(2)}, u32[]{:S(2)}) collective-permute-start(bf16[1,8,32,256]{3,2,1,0:T(8,128)(2,1)S(1)} %get-tuple-element.107), channel_id=1, source_target_pairs={{0,16},{8,24},{16,0},{24,8},{1,17},{9,25},{17,1},{25,9},{2,18},{10... | collective-permute-start | bytes 393224 | tf_op jit(solution)/shard_map/ppermute | solution.py:313
  89.0 15.0 %collective-permute-start.29 = (bf16[1,8,32,256]{3,2,1,0:T(8,128)(2,1)S(1)}, bf16[1,8,32,256]{3,2,1,0:T(8,128)(2,1)S(1)}, u32[]{:S(2)}, u32[]{:S(2)}) collective-permute-start(bf16[1,8,32,256]{3,2,1,0:T(8,128)(2,1)S(1)} %get-tuple-element.108), channel_id=1, source_target_pairs={{0,24},{8,16},{16,8},{24,0},{1,25},{9,17},{17,9},{25,1},{2,26},{10... | collective-permute-start | bytes 393224 | tf_op jit(solution)/shard_map/ppermute | solution.py:313
  98.9 19.4 %collective-permute-start.39 = (bf16[4,8,32,512]{3,2,1,0:T(8,128)(2,1)S(1)}, bf16[4,8,32,512]{3,2,1,0:T(8,128)(2,1)S(1)}, u32[]{:S(2)}, u32[]{:S(2)}) collective-permute-start(bf16[4,8,32,512]{3,2,1,0:T(8,128)(2,1)S(1)} %get-tuple-element.117), channel_id=1, source_target_pairs={{0,1},{1,0},{2,3},{3,2},{4,5},{5,4},{6,7},{7,6},{8,9},{9,8},{10,11... | collective-permute-start | bytes 3145736 | tf_op jit(solution)/shard_map/ppermute | solution.py:290
  102.2 13.1 %collective-permute-start.45 = (bf16[4,32,16,128]{3,2,1,0:T(8,128)(2,1)S(1)}, bf16[4,32,16,128]{3,2,1,0:T(8,128)(2,1)S(1)}, u32[]{:S(2)}, u32[]{:S(2)}) collective-permute-start(bf16[4,32,16,128]{3,2,1,0:T(8,128)(2,1)S(1)} %get-tuple-element.129), channel_id=1, source_target_pairs={{0,1},{1,0},{2,3},{3,2},{4,5},{5,4},{6,7},{7,6},{8,9},{9,8},{10,11... | collective-permute-start | bytes 1572872 | tf_op jit(solution)/shard_map/ppermute | solution.py:290
  102.7 6.4 %collective-permute-start.24 = (bf16[1,8,32,256]{3,2,1,0:T(8,128)(2,1)S(1)}, bf16[1,8,32,256]{3,2,1,0:T(8,128)(2,1)S(1)}, u32[]{:S(2)}, u32[]{:S(2)}) collective-permute-start(bf16[1,8,32,256]{3,2,1,0:T(8,128)(2,1)S(1)} %get-tuple-element.102), channel_id=1, source_target_pairs={{0,8},{8,0},{16,24},{24,16},{1,9},{9,1},{17,25},{25,17},{2,10},{10... | collective-permute-start | bytes 393224 | tf_op jit(solution)/shard_map/ppermute | solution.py:313
  103.5 7.9 %collective-permute-start.25 = (bf16[1,8,32,256]{3,2,1,0:T(8,128)(2,1)S(1)}, bf16[1,8,32,256]{3,2,1,0:T(8,128)(2,1)S(1)}, u32[]{:S(2)}, u32[]{:S(2)}) collective-permute-start(bf16[1,8,32,256]{3,2,1,0:T(8,128)(2,1)S(1)} %get-tuple-element.103), channel_id=1, source_target_pairs={{0,16},{8,24},{16,0},{24,8},{1,17},{9,25},{17,1},{25,9},{2,18},{10... | collective-permute-start | bytes 393224 | tf_op jit(solution)/shard_map/ppermute | solution.py:313
  104.0 7.4 %collective-permute-start.26 = (bf16[1,8,32,256]{3,2,1,0:T(8,128)(2,1)S(1)}, bf16[1,8,32,256]{3,2,1,0:T(8,128)(2,1)S(1)}, u32[]{:S(2)}, u32[]{:S(2)}) collective-permute-start(bf16[1,8,32,256]{3,2,1,0:T(8,128)(2,1)S(1)} %get-tuple-element.104), channel_id=1, source_target_pairs={{0,24},{8,16},{16,8},{24,0},{1,25},{9,17},{17,9},{25,1},{2,26},{10... | collective-permute-start | bytes 393224 | tf_op jit(solution)/shard_map/ppermute | solution.py:313
  109.0 9.9 %collective-permute-start.42 = (bf16[4,8,32,512]{3,2,1,0:T(8,128)(2,1)S(1)}, bf16[4,8,32,512]{3,2,1,0:T(8,128)(2,1)S(1)}, u32[]{:S(2)}, u32[]{:S(2)}) collective-permute-start(bf16[4,8,32,512]{3,2,1,0:T(8,128)(2,1)S(1)} %get-tuple-element.119), channel_id=1, source_target_pairs={{0,1},{1,0},{2,3},{3,2},{4,5},{5,4},{6,7},{7,6},{8,9},{9,8},{10,11... | collective-permute-start | bytes 3145736 | tf_op jit(solution)/shard_map/ppermute | solution.py:290
  114.7 1.9 collective-permute-start.30
  114.7 6.1 %collective-permute-start.33 = (bf16[4,8,32,512]{3,2,1,0:T(8,128)(2,1)S(1)}, bf16[4,8,32,512]{3,2,1,0:T(8,128)(2,1)S(1)}, u32[]{:S(2)}, u32[]{:S(2)}) collective-permute-start(bf16[4,8,32,512]{3,2,1,0:T(8,128)(2,1)S(1)} %get-tuple-element.113), channel_id=1, source_target_pairs={{0,1},{1,0},{2,3},{3,2},{4,5},{5,4},{6,7},{7,6},{8,9},{9,8},{10,11... | collective-permute-start | bytes 3145736 | tf_op jit(solution)/shard_map/ppermute | solution.py:290
  115.2 6.2 %collective-permute-start.36 = (bf16[4,8,32,512]{3,2,1,0:T(8,128)(2,1)S(1)}, bf16[4,8,32,512]{3,2,1,0:T(8,128)(2,1)S(1)}, u32[]{:S(2)}, u32[]{:S(2)}) collective-permute-start(bf16[4,8,32,512]{3,2,1,0:T(8,128)(2,1)S(1)} %get-tuple-element.115), channel_id=1, source_target_pairs={{0,1},{1,0},{2,3},{3,2},{4,5},{5,4},{6,7},{7,6},{8,9},{9,8},{10,11... | collective-permute-start | bytes 3145736 | tf_op jit(solution)/shard_map/ppermute | solution.py:290
  116.6 9.2 %collective-permute-start.46 = (bf16[2,32,16,128]{3,2,1,0:T(8,128)(2,1)S(1)}, bf16[2,32,16,128]{3,2,1,0:T(8,128)(2,1)S(1)}, u32[]{:S(2)}, u32[]{:S(2)}) collective-permute-start(bf16[2,32,16,128]{3,2,1,0:T(8,128)(2,1)S(1)} %add_convert_fusion.4), channel_id=1, source_target_pairs={{0,2},{1,3},{2,0},{3,1},{4,6},{5,7},{6,4},{7,5},{8,10},{9,11},{10,... | collective-permute-start | bytes 786440 | tf_op jit(solution)/shard_map/ppermute | solution.py:295
  118.3 67.9 %collective-permute-start.31 = (bf16[2,32,16,128]{3,2,1,0:T(8,128)(2,1)S(1)}, bf16[2,32,16,128]{3,2,1,0:T(8,128)(2,1)S(1)}, u32[]{:S(2)}, u32[]{:S(2)}) collective-permute-start(bf16[2,32,16,128]{3,2,1,0:T(8,128)(2,1)S(1)} %add_convert_fusion.9), channel_id=1, source_target_pairs={{0,2},{1,3},{2,0},{3,1},{4,6},{5,7},{6,4},{7,5},{8,10},{9,11},{10,... | collective-permute-start | bytes 786440 | tf_op jit(solution)/shard_map/ppermute | solution.py:295
  119.0 23.7 %collective-permute-start.40 = (bf16[2,8,32,512]{3,2,1,0:T(8,128)(2,1)S(1)}, bf16[2,8,32,512]{3,2,1,0:T(8,128)(2,1)S(1)}, u32[]{:S(2)}, u32[]{:S(2)}) collective-permute-start(bf16[2,8,32,512]{3,2,1,0:T(8,128)(2,1)S(1)} %add_convert_fusion.1), channel_id=1, source_target_pairs={{0,2},{1,3},{2,0},{3,1},{4,6},{5,7},{6,4},{7,5},{8,10},{9,11},{10,... | collective-permute-start | bytes 1572872 | tf_op jit(solution)/shard_map/ppermute | solution.py:295
  120.8 35.9 %collective-permute-start.43 = (bf16[2,8,32,512]{3,2,1,0:T(8,128)(2,1)S(1)}, bf16[2,8,32,512]{3,2,1,0:T(8,128)(2,1)S(1)}, u32[]{:S(2)}, u32[]{:S(2)}) collective-permute-start(bf16[2,8,32,512]{3,2,1,0:T(8,128)(2,1)S(1)} %add_convert_fusion), channel_id=1, source_target_pairs={{0,2},{1,3},{2,0},{3,1},{4,6},{5,7},{6,4},{7,5},{8,10},{9,11},{10,... | collective-permute-start | bytes 1572872 | tf_op jit(solution)/shard_map/ppermute | solution.py:295
  121.5 52.1 %collective-permute-start.34 = (bf16[2,8,32,512]{3,2,1,0:T(8,128)(2,1)S(1)}, bf16[2,8,32,512]{3,2,1,0:T(8,128)(2,1)S(1)}, u32[]{:S(2)}, u32[]{:S(2)}) collective-permute-start(bf16[2,8,32,512]{3,2,1,0:T(8,128)(2,1)S(1)} %add_convert_fusion.3), channel_id=1, source_target_pairs={{0,2},{1,3},{2,0},{3,1},{4,6},{5,7},{6,4},{7,5},{8,10},{9,11},{10,... | collective-permute-start | bytes 1572872 | tf_op jit(solution)/shard_map/ppermute | solution.py:295
  125.8 60.3 %collective-permute-start.37 = (bf16[2,8,32,512]{3,2,1,0:T(8,128)(2,1)S(1)}, bf16[2,8,32,512]{3,2,1,0:T(8,128)(2,1)S(1)}, u32[]{:S(2)}, u32[]{:S(2)}) collective-permute-start(bf16[2,8,32,512]{3,2,1,0:T(8,128)(2,1)S(1)} %add_convert_fusion.2), channel_id=1, source_target_pairs={{0,2},{1,3},{2,0},{3,1},{4,6},{5,7},{6,4},{7,5},{8,10},{9,11},{10,... | collective-permute-start | bytes 1572872 | tf_op jit(solution)/shard_map/ppermute | solution.py:295
  142.7 46.6 %collective-permute-start.47 = (bf16[1,32,16,128]{3,2,1,0:T(8,128)(2,1)S(1)}, bf16[1,32,16,128]{3,2,1,0:T(8,128)(2,1)S(1)}, u32[]{:S(2)}, u32[]{:S(2)}) collective-permute-start(bf16[1,32,16,128]{3,2,1,0:T(8,128)(2,1)S(1)} %add_convert_fusion.10), channel_id=1, source_target_pairs={{0,4},{1,5},{2,6},{3,7},{4,0},{5,1},{6,2},{7,3},{8,12},{9,13},{10,... | collective-permute-start | bytes 393224 | tf_op jit(solution)/shard_map/ppermute | solution.py:295
  156.7 68.8 %collective-permute-start.41 = (bf16[1,8,32,512]{3,2,1,0:T(8,128)(2,1)S(1)}, bf16[1,8,32,512]{3,2,1,0:T(8,128)(2,1)S(1)}, u32[]{:S(2)}, u32[]{:S(2)}) collective-permute-start(bf16[1,8,32,512]{3,2,1,0:T(8,128)(2,1)S(1)} %add_convert_fusion.6), channel_id=1, source_target_pairs={{0,4},{1,5},{2,6},{3,7},{4,0},{5,1},{6,2},{7,3},{8,12},{9,13},{10,... | collective-permute-start | bytes 786440 | tf_op jit(solution)/shard_map/ppermute | solution.py:295
  173.5 51.1 %collective-permute-start.44 = (bf16[1,8,32,512]{3,2,1,0:T(8,128)(2,1)S(1)}, bf16[1,8,32,512]{3,2,1,0:T(8,128)(2,1)S(1)}, u32[]{:S(2)}, u32[]{:S(2)}) collective-permute-start(bf16[1,8,32,512]{3,2,1,0:T(8,128)(2,1)S(1)} %add_convert_fusion.5), channel_id=1, source_target_pairs={{0,4},{1,5},{2,6},{3,7},{4,0},{5,1},{6,2},{7,3},{8,12},{9,13},{10,... | collective-permute-start | bytes 786440 | tf_op jit(solution)/shard_map/ppermute | solution.py:295
  186.1 41.1 %collective-permute-start.35 = (bf16[1,8,32,512]{3,2,1,0:T(8,128)(2,1)S(1)}, bf16[1,8,32,512]{3,2,1,0:T(8,128)(2,1)S(1)}, u32[]{:S(2)}, u32[]{:S(2)}) collective-permute-start(bf16[1,8,32,512]{3,2,1,0:T(8,128)(2,1)S(1)} %add_convert_fusion.8), channel_id=1, source_target_pairs={{0,4},{1,5},{2,6},{3,7},{4,0},{5,1},{6,2},{7,3},{8,12},{9,13},{10,... | collective-permute-start | bytes 786440 | tf_op jit(solution)/shard_map/ppermute | solution.py:295
  186.2 40.2 %collective-permute-start.38 = (bf16[1,8,32,512]{3,2,1,0:T(8,128)(2,1)S(1)}, bf16[1,8,32,512]{3,2,1,0:T(8,128)(2,1)S(1)}, u32[]{:S(2)}, u32[]{:S(2)}) collective-permute-start(bf16[1,8,32,512]{3,2,1,0:T(8,128)(2,1)S(1)} %add_convert_fusion.7), channel_id=1, source_target_pairs={{0,4},{1,5},{2,6},{3,7},{4,0},{5,1},{6,2},{7,3},{8,12},{9,13},{10,... | collective-permute-start | bytes 786440 | tf_op jit(solution)/shard_map/ppermute | solution.py:295
  189.3 34.0 %collective-permute-start.32 = (bf16[1,32,16,128]{3,2,1,0:T(8,128)(2,1)S(1)}, bf16[1,32,16,128]{3,2,1,0:T(8,128)(2,1)S(1)}, u32[]{:S(2)}, u32[]{:S(2)}) collective-permute-start(bf16[1,32,16,128]{3,2,1,0:T(8,128)(2,1)S(1)} %add_convert_fusion.11), channel_id=1, source_target_pairs={{0,4},{1,5},{2,6},{3,7},{4,0},{5,1},{6,2},{7,3},{8,12},{9,13},{10,... | collective-permute-start | bytes 393224 | tf_op jit(solution)/shard_map/ppermute | solution.py:295
  (7 other events, 141.9 us)

commit v3 on v2

--- a/solution.py
+++ b/solution.py
@@ -14,7 +14,7 @@
 LANES = 128
 ROWS = 16
 PITCH = 20
-SHARES = (2, 2, 2, 2)
+SHARES = (1, 2, 2, 2, 1)
 TILE = 128
 MIB = 1 << 20
 STEP = 4
@@ -313,6 +313,7 @@
             got.append(lax.ppermute(arrays[s], "block", [(i, i ^ s) for i in range(groups)]))
         return got
 
+    factors = [pltpu.with_memory_space_constraint(a, pltpu.HBM) for a in (second_up, first_down)]
     first_in = [pltpu.with_memory_space_constraint(a, pltpu.HBM) for a in (tokens, cotangent, first_up, second_down)]
     packed = mix_in(*first_in, groups)
     packed = [exchange(a) for a in packed]
@@ -320,7 +321,8 @@
     for_v, for_d, sums = [], [], []
     for c, (_, begin) in enumerate(chunks):
         joint = is_joint(c, len(chunks))
-        back, keep, send = feature(packed[c], second_up, first_down, begin, joint, line)
+        mats = factors if c == 0 else (second_up, first_down)
+        back, keep, send = feature(packed[c], *mats, begin, joint, line)
         for_v.append(exchange(back[:groups]))
         for_d.append(for_v[-1] if joint else exchange(back[groups:]))
         sums.append(line_sum(keep, send, line))

time: 228 us -> 241 us (1.057)
  starting transfers between devices: 54.5 us -> 71.7 us
  waiting for transfers between devices: 134 us -> 127 us
    ppermute x30 -> x36, starting transfers between devices: 36.9 us -> 48.4 us  [exchange(): lax.ppermute(arrays[s], 'block', [(i, i ^ s) for i in range(groups)])]
    ppermute x12 -> x14, waiting for transfers between devices: 87.5 us -> 79.7 us  [line_sum(): lax.ppermute(total, 'dp', [(i, i ^ hop) for i in range(CORES * line)])]
    ppermute x12 -> x14, starting transfers between devices: 16.5 us -> 23.1 us  [line_sum(): lax.ppermute(total, 'dp', [(i, i ^ hop) for i in range(CORES * line)])]
    ppermute x30 -> x36, waiting for transfers between devices: 44.7 us -> 47.5 us  [exchange(): lax.ppermute(arrays[s], 'block', [(i, i ^ s) for i in range(groups)])]
    pallas_call x4 -> x5, Pallas kernels: 18.4 us -> 19.4 us  [feature(): pl.pallas_call(functools.partial(feature_body, groups, line), grid=(steps...]
    pallas_call x6 -> x7, Pallas kernels: 6.12 us -> 6.57 us  [settle(): pl.pallas_call(functools.partial(settle_body, fold, len(parts)), grid=(pa...]
  transfers between devices with their start and end apart: 48 -> 57, of which waited for: 17 -> 20; matrix products, arithmetic and copies ran while one was open for 1% -> 1% of each run, Pallas kernels for 13% -> 13%
where the time goes in v3:
time: 241 us
  waiting for transfers between devices  127 us (53%)
  starting transfers between devices  71.7 us (30%)
  Pallas kernels  37.3 us (15%)
  local copies, waits for them, and re-layouts  2.54 us (1%)
    ppermute x14, waiting for transfers between devices, line_sum(): lax.ppermute(total, 'dp', [(i, i ^ hop) for i in range(CORES * line)])  79.7 us
    ppermute x36, starting transfers between devices, exchange(): lax.ppermute(arrays[s], 'block', [(i, i ^ s) for i in range(groups)])  48.4 us
    ppermute x36, waiting for transfers between devices, exchange(): lax.ppermute(arrays[s], 'block', [(i, i ^ s) for i in range(groups)])  47.5 us
    ppermute x14, starting transfers between devices, line_sum(): lax.ppermute(total, 'dp', [(i, i ^ hop) for i in range(CORES * line)])  23.1 us
    pallas_call x5, Pallas kernels, feature(): pl.pallas_call(functools.partial(feature_body, groups, line), grid=(steps...  19.4 us
    pallas_call x2, Pallas kernels, mix_out(): pl.pallas_call(functools.partial(mix_out_body, groups, line, to_output),...  6.64 us
    pallas_call x7, Pallas kernels, settle(): pl.pallas_call(functools.partial(settle_body, fold, len(parts)), grid=(pa...  6.57 us
  transfers between devices with their start and end apart: 57, of which 20 were waited for; matrix products, arithmetic and copies ran while one was open for 1% of the time, Pallas kernels for 13%

profile of v3, /device:TPU:0, one launch (start us, length us, event | category | flops | bytes accessed | tf_op | source)
XLA Modules:
  0.0 240.9 jit_solution(4963276220223048299)
XLA Ops:
  0.6 4.7 %mix_in.1 = (bf16[2,4,32,256]{3,2,1,0:T(8,128)(2,1)S(1)}, bf16[2,4,32,256]{3,2,1,0:T(8,128)(2,1)S(1)}, bf16[2,4,32,256]{3,2,1,0:T(8,128)(2,1)S(1)}, bf16[2,4,32,...) custom-call(bf16[256,4096]{1,0:T(8,128)(2,1)} %rest_20_.3, ...), custom_call_target="tpu_custom_call" | custom-call | flops 536870912 | bytes 8388608 | tf_op jit(solution)/shard_map/mix_in/pallas_call | solution.py:76
  5.4 3.0 %collective-permute-start = (bf16[2,4,32,256]{3,2,1,0:T(8,128)(2,1)S(1)}, bf16[2,4,32,256]{3,2,1,0:T(8,128)(2,1)S(1)}, u32[]{:S(2)}, u32[]{:S(2)}) collective-permute-start(bf16[2,4,32,256]{3,2,1,0:T(8,128)(2,1)S(1)} %get-tuple-element.81), channel_id=1, source_target_pairs={{0,8},{8,0},{16,24},{24,16},{1,9},{9,1},{17,25},{25,17},{2,10},{10... | collective-permute-start | bytes 393224 | tf_op jit(solution)/shard_map/ppermute | solution.py:313
  10.5 2.9 %collective-permute-start.26 = (bf16[2,4,32,256]{3,2,1,0:T(8,128)(2,1)S(1)}, bf16[2,4,32,256]{3,2,1,0:T(8,128)(2,1)S(1)}, u32[]{:S(2)}, u32[]{:S(2)}) collective-permute-start(bf16[2,4,32,256]{3,2,1,0:T(8,128)(2,1)S(1)} %get-tuple-element.115), channel_id=1, source_target_pairs={{0,24},{8,16},{16,8},{24,0},{1,25},{9,17},{17,9},{25,1},{2,26},{10... | collective-permute-start | bytes 393224 | tf_op jit(solution)/shard_map/ppermute | solution.py:313
  13.4 2.3 collective-permute-start.2
  17.8 3.1 %collective-permute-done.25.rest_2_ = bf16[2,4,32,256]{3,2,1,0:T(8,128)(2,1)S(1)} collective-permute-done((bf16[2,4,32,256]{3,2,1,0:T(8,128)(2,1)S(1)}, bf16[2,4,32,256]{3,2,1,0:T(8,128)(2,1)S(1)}, u32[]{:S(2)}, u32[]{:S(2)}) %collective-permute-start.25) | collective-permute-done | bytes 131104 | tf_op jit(solution)/shard_map/ppermute | solution.py:313
  20.9 2.5 %collective-permute-start.19 = (bf16[2,8,32,256]{3,2,1,0:T(8,128)(2,1)S(1)}, bf16[2,8,32,256]{3,2,1,0:T(8,128)(2,1)S(1)}, u32[]{:S(2)}, u32[]{:S(2)}) collective-permute-start(bf16[2,8,32,256]{3,2,1,0:T(8,128)(2,1)S(1)} %get-tuple-element.106), channel_id=1, source_target_pairs={{0,16},{8,24},{16,0},{24,8},{1,17},{9,25},{17,1},{25,9},{2,18},{10... | collective-permute-start | bytes 786440 | tf_op jit(solution)/shard_map/ppermute | solution.py:313
  23.4 2.2 copy-done.2
  25.6 2.1 feature.9
  29.2 9.4 %collective-permute-done.33.rest_17_ = bf16[1,4,32,256]{3,2,1,0:T(8,128)(2,1)S(1)} collective-permute-done((bf16[1,4,32,256]{3,2,1,0:T(8,128)(2,1)S(1)}, bf16[1,4,32,256]{3,2,1,0:T(8,128)(2,1)S(1)}, u32[]{:S(2)}, u32[]{:S(2)}) %collective-permute-start.33) | collective-permute-done | bytes 65568 | tf_op jit(solution)/shard_map/ppermute | solution.py:313
  38.6 1.8 collective-permute-start.34
  40.4 2.5 %collective-permute-done.34.rest_18_ = bf16[1,4,32,256]{3,2,1,0:T(8,128)(2,1)S(1)} collective-permute-done((bf16[1,4,32,256]{3,2,1,0:T(8,128)(2,1)S(1)}, bf16[1,4,32,256]{3,2,1,0:T(8,128)(2,1)S(1)}, u32[]{:S(2)}, u32[]{:S(2)}) %collective-permute-start.34) | collective-permute-done | bytes 65568 | tf_op jit(solution)/shard_map/ppermute | solution.py:313
  42.8 2.7 %collective-permute-start.35 = (bf16[1,4,32,256]{3,2,1,0:T(8,128)(2,1)S(1)}, bf16[1,4,32,256]{3,2,1,0:T(8,128)(2,1)S(1)}, u32[]{:S(2)}, u32[]{:S(2)}) collective-permute-start(bf16[1,4,32,256]{3,2,1,0:T(8,128)(2,1)S(1)} %get-tuple-element.128), channel_id=1, source_target_pairs={{0,24},{8,16},{16,8},{24,0},{1,25},{9,17},{17,9},{25,1},{2,26},{10... | collective-permute-start | bytes 196616 | tf_op jit(solution)/shard_map/ppermute | solution.py:313
  45.6 2.5 %collective-permute-done.35.rest_19_ = bf16[1,4,32,256]{3,2,1,0:T(8,128)(2,1)S(1)} collective-permute-done((bf16[1,4,32,256]{3,2,1,0:T(8,128)(2,1)S(1)}, bf16[1,4,32,256]{3,2,1,0:T(8,128)(2,1)S(1)}, u32[]{:S(2)}, u32[]{:S(2)}) %collective-permute-start.35) | collective-permute-done | bytes 65568 | tf_op jit(solution)/shard_map/ppermute | solution.py:313
  48.1 1.9 collective-permute-start.7
  51.6 1.9 collective-permute-start.13
  54.9 3.4 %feature.5 = (bf16[2,4,32,256]{3,2,1,0:T(8,128)(2,1)S(1)}, bf16[2,4,32,256]{3,2,1,0:T(8,128)(2,1)S(1)}, bf16[2,4,32,256]{3,2,1,0:T(8,128)(2,1)S(1)}, bf16[2,4,32...) custom-call(bf16[2,4,32,256]{3,2,1,0:T(8,128)(2,1)S(1)} %get-tuple-element.80.rest, ...), custom_call_target="tpu_custom_call" | custom-call | flops 805306368 | bytes 3145728 | tf_op jit(solution)/shard_map/feature/pallas_call | solution.py:168
  58.7 4.5 %feature.8 = (bf16[1,8,32,256]{3,2,1,0:T(8,128)(2,1)S(1)}, bf16[1,8,32,256]{3,2,1,0:T(8,128)(2,1)S(1)}, bf16[1,8,32,256]{3,2,1,0:T(8,128)(2,1)S(1)}, bf16[1,8,32...) custom-call(bf16[2,8,32,256]{3,2,1,0:T(8,128)(2,1)S(1)} %get-tuple-e, ...), custom_call_target="tpu_custom_call" | custom-call | flops 1610612736 | bytes 6291456 | tf_op jit(solution)/shard_map/feature/pallas_call | solution.py:168
  63.3 2.1 collective-permute-start.3
  67.8 6.6 %collective-permute-done.13.rest_2_ = bf16[2,8,32,256]{3,2,1,0:T(8,128)(2,1)S(1)} collective-permute-done((bf16[2,8,32,256]{3,2,1,0:T(8,128)(2,1)S(1)}, bf16[2,8,32,256]{3,2,1,0:T(8,128)(2,1)S(1)}, u32[]{:S(2)}, u32[]{:S(2)}) %collective-permute-start.13) | collective-permute-done | bytes 262176 | tf_op jit(solution)/shard_map/ppermute | solution.py:313
  74.4 2.1 collective-permute-start.30
  77.5 4.8 %feature.7 = (bf16[2,8,32,256]{3,2,1,0:T(8,128)(2,1)S(1)}, bf16[2,8,32,256]{3,2,1,0:T(8,128)(2,1)S(1)}, bf16[2,8,32,256]{3,2,1,0:T(8,128)(2,1)S(1)}, bf16[2,8,32...) custom-call(bf16[2,8,32,256]{3,2,1,0:T(8,128)(2,1)S(1)} %get-tuple-element.96.rest, ...), custom_call_target="tpu_custom_call" | custom-call | flops 1610612736 | bytes 6291456 | tf_op jit(solution)/shard_map/feature/pallas_call | solution.py:168
  83.4 2.4 %collective-permute-start.17 = (bf16[2,8,32,256]{3,2,1,0:T(8,128)(2,1)S(1)}, bf16[2,8,32,256]{3,2,1,0:T(8,128)(2,1)S(1)}, u32[]{:S(2)}, u32[]{:S(2)}) collective-permute-start(bf16[2,8,32,256]{3,2,1,0:T(8,128)(2,1)S(1)} %get-tuple-element.103), channel_id=1, source_target_pairs={{0,24},{8,16},{16,8},{24,0},{1,25},{9,17},{17,9},{25,1},{2,26},{10... | collective-permute-start | bytes 786440 | tf_op jit(solution)/shard_map/ppermute | solution.py:313
  86.4 4.6 %feature.6 = (bf16[2,8,32,256]{3,2,1,0:T(8,128)(2,1)S(1)}, bf16[2,8,32,256]{3,2,1,0:T(8,128)(2,1)S(1)}, bf16[2,8,32,256]{3,2,1,0:T(8,128)(2,1)S(1)}, bf16[2,8,32...) custom-call(bf16[2,8,32,256]{3,2,1,0:T(8,128)(2,1)S(1)} %get-tuple-element.88.rest, ...), custom_call_target="tpu_custom_call" | custom-call | flops 1610612736 | bytes 6291456 | tf_op jit(solution)/shard_map/feature/pallas_call | solution.py:168
  91.0 6.6 %collective-permute-done.32.rest_15_ = bf16[1,8,32,256]{3,2,1,0:T(8,128)(2,1)S(1)} collective-permute-done((bf16[1,8,32,256]{3,2,1,0:T(8,128)(2,1)S(1)}, bf16[1,8,32,256]{3,2,1,0:T(8,128)(2,1)S(1)}, u32[]{:S(2)}, u32[]{:S(2)}) %collective-permute-start.32) | collective-permute-done | bytes 131104 | tf_op jit(solution)/shard_map/ppermute | solution.py:313
  99.0 2.1 collective-permute-start.11
  101.1 5.7 %collective-permute-done.9.rest_5_ = bf16[2,8,32,256]{3,2,1,0:T(8,128)(2,1)S(1)} collective-permute-done((bf16[2,8,32,256]{3,2,1,0:T(8,128)(2,1)S(1)}, bf16[2,8,32,256]{3,2,1,0:T(8,128)(2,1)S(1)}, u32[]{:S(2)}, u32[]{:S(2)}) %collective-permute-start.9) | collective-permute-done | bytes 262176 | tf_op jit(solution)/shard_map/ppermute | solution.py:313
  107.1 4.3 %collective-permute-done.10.rest_6_ = bf16[2,8,32,256]{3,2,1,0:T(8,128)(2,1)S(1)} collective-permute-done((bf16[2,8,32,256]{3,2,1,0:T(8,128)(2,1)S(1)}, bf16[2,8,32,256]{3,2,1,0:T(8,128)(2,1)S(1)}, u32[]{:S(2)}, u32[]{:S(2)}) %collective-permute-start.10) | collective-permute-done | bytes 262176 | tf_op jit(solution)/shard_map/ppermute | solution.py:313
  112.9 3.3 %mix_out.3 = (bf16[256,4096]{1,0:T(8,128)(2,1)}, bf16[4,32,16,128]{3,2,1,0:T(8,128)(2,1)S(1)}, bf16[4,32,16,128]{3,2,1,0:T(8,128)(2,1)S(1)}) custom-call(bf16[2,4,32,256]{3,2,1,0:T(8,128)(2,1)S(1)} %get-tuple-element.84.rest_0_, bf16[2,4,32,256]{3,2,1,0:T(8,128)(2,1)S(1)} %collective-permute-done.3.rest_1_, ...), custom_call_target="tpu_custom_call" | custom-call | flops 536870912 | bytes 8388608 | tf_op jit(solution)/shard_map/mix_out/pallas_call | solution.py:238
  116.2 2.0 collective-permute-start.21
  119.9 2.6 %collective-permute-done.21.rest_13_ = bf16[1,8,32,256]{3,2,1,0:T(8,128)(2,1)S(1)} collective-permute-done((bf16[1,8,32,256]{3,2,1,0:T(8,128)(2,1)S(1)}, bf16[1,8,32,256]{3,2,1,0:T(8,128)(2,1)S(1)}, u32[]{:S(2)}, u32[]{:S(2)}) %collective-permute-start.21) | collective-permute-done | bytes 131104 | tf_op jit(solution)/shard_map/ppermute | solution.py:313
  122.5 4.1 %collective-permute-done.22.rest_14_ = bf16[1,8,32,256]{3,2,1,0:T(8,128)(2,1)S(1)} collective-permute-done((bf16[1,8,32,256]{3,2,1,0:T(8,128)(2,1)S(1)}, bf16[1,8,32,256]{3,2,1,0:T(8,128)(2,1)S(1)}, u32[]{:S(2)}, u32[]{:S(2)}) %collective-permute-start.22) | collective-permute-done | bytes 131104 | tf_op jit(solution)/shard_map/ppermute | solution.py:313
  126.7 1.8 collective-permute-start.52
  128.5 3.3 %mix_out.2 = (bf16[256,4096]{1,0:T(8,128)(2,1)}, bf16[4,32,16,128]{3,2,1,0:T(8,128)(2,1)S(1)}, bf16[4,32,16,128]{3,2,1,0:T(8,128)(2,1)S(1)}) custom-call(bf16[2,4,32,256]{3,2,1,0:T(8,128)(2,1)S(1)} %get-tuple-element.84.rest_0_, bf16[2,4,32,256]{3,2,1,0:T(8,128)(2,1)S(1)} %collective-permute-done.3.rest_1_, ...), custom_call_target="tpu_custom_call" | custom-call | flops 536870912 | bytes 8388608 | tf_op jit(solution)/shard_map/mix_out/pallas_call | solution.py:238
  132.1 3.4 %collective-permute-done.52.rest_2_ = bf16[2,4,32,512]{3,2,1,0:T(8,128)(2,1)S(1)} collective-permute-done((bf16[2,4,32,512]{3,2,1,0:T(8,128)(2,1)S(1)}, bf16[2,4,32,512]{3,2,1,0:T(8,128)(2,1)S(1)}, u32[]{:S(2)}, u32[]{:S(2)}) %collective-permute-start.52) | collective-permute-done | bytes 262176 | tf_op jit(solution)/shard_map/ppermute | solution.py:295
  135.5 1.8 collective-permute-start.40
  137.4 2.7 %collective-permute-start.53 = (bf16[1,4,32,512]{3,2,1,0:T(8,128)(2,1)S(1)}, bf16[1,4,32,512]{3,2,1,0:T(8,128)(2,1)S(1)}, u32[]{:S(2)}, u32[]{:S(2)}) collective-permute-start(bf16[1,4,32,512]{3,2,1,0:T(8,128)(2,1)S(1)} %add_convert_fusion.11), channel_id=1, source_target_pairs={{0,4},{1,5},{2,6},{3,7},{4,0},{5,1},{6,2},{7,3},{8,12},{9,13},{10,... | collective-permute-start | bytes 393224 | tf_op jit(solution)/shard_map/ppermute | solution.py:295
  143.4 9.8 %collective-permute-done.37.rest_2_ = bf16[2,32,16,128]{3,2,1,0:T(8,128)(2,1)S(1)} collective-permute-done((bf16[2,32,16,128]{3,2,1,0:T(8,128)(2,1)S(1)}, bf16[2,32,16,128]{3,2,1,0:T(8,128)(2,1)S(1)}, u32[]{:S(2)}, u32[]{:S(2)}) %collective-permute-start.37) | collective-permute-done | bytes 262176 | tf_op jit(solution)/shard_map/ppermute | solution.py:295
  153.2 1.7 collective-permute-start.49
  155.0 3.8 %collective-permute-done.55.rest_2_ = bf16[2,32,16,128]{3,2,1,0:T(8,128)(2,1)S(1)} collective-permute-done((bf16[2,32,16,128]{3,2,1,0:T(8,128)(2,1)S(1)}, bf16[2,32,16,128]{3,2,1,0:T(8,128)(2,1)S(1)}, u32[]{:S(2)}, u32[]{:S(2)}) %collective-permute-start.55) | collective-permute-done | bytes 262176 | tf_op jit(solution)/shard_map/ppermute | solution.py:295
  160.6 9.4 %collective-permute-done.46.rest_2_ = bf16[2,8,32,512]{3,2,1,0:T(8,128)(2,1)S(1)} collective-permute-done((bf16[2,8,32,512]{3,2,1,0:T(8,128)(2,1)S(1)}, bf16[2,8,32,512]{3,2,1,0:T(8,128)(2,1)S(1)}, u32[]{:S(2)}, u32[]{:S(2)}) %collective-permute-start.46) | collective-permute-done | bytes 524320 | tf_op jit(solution)/shard_map/ppermute | solution.py:295
  170.1 2.8 %collective-permute-start.38 = (bf16[1,32,16,128]{3,2,1,0:T(8,128)(2,1)S(1)}, bf16[1,32,16,128]{3,2,1,0:T(8,128)(2,1)S(1)}, u32[]{:S(2)}, u32[]{:S(2)}) collective-permute-start(bf16[1,32,16,128]{3,2,1,0:T(8,128)(2,1)S(1)} %add_convert_fusion.13), channel_id=1, source_target_pairs={{0,4},{1,5},{2,6},{3,7},{4,0},{5,1},{6,2},{7,3},{8,12},{9,13},{10,... | collective-permute-start | bytes 393224 | tf_op jit(solution)/shard_map/ppermute | solution.py:295
  172.9 11.2 %collective-permute-done.49.rest_2_ = bf16[2,8,32,512]{3,2,1,0:T(8,128)(2,1)S(1)} collective-permute-done((bf16[2,8,32,512]{3,2,1,0:T(8,128)(2,1)S(1)}, bf16[2,8,32,512]{3,2,1,0:T(8,128)(2,1)S(1)}, u32[]{:S(2)}, u32[]{:S(2)}) %collective-permute-start.49) | collective-permute-done | bytes 524320 | tf_op jit(solution)/shard_map/ppermute | solution.py:295
  184.1 1.9 collective-permute-start.56
  186.1 11.6 %collective-permute-done.43.rest_2_ = bf16[2,8,32,512]{3,2,1,0:T(8,128)(2,1)S(1)} collective-permute-done((bf16[2,8,32,512]{3,2,1,0:T(8,128)(2,1)S(1)}, bf16[2,8,32,512]{3,2,1,0:T(8,128)(2,1)S(1)}, u32[]{:S(2)}, u32[]{:S(2)}) %collective-permute-start.43) | collective-permute-done | bytes 524320 | tf_op jit(solution)/shard_map/ppermute | solution.py:295
  197.7 1.9 collective-permute-start.47
  200.8 1.9 collective-permute-start.44
  207.2 25.7 %collective-permute-done.50.rest_3_ = bf16[1,8,32,512]{3,2,1,0:T(8,128)(2,1)S(1)} collective-permute-done((bf16[1,8,32,512]{3,2,1,0:T(8,128)(2,1)S(1)}, bf16[1,8,32,512]{3,2,1,0:T(8,128)(2,1)S(1)}, u32[]{:S(2)}, u32[]{:S(2)}) %collective-permute-start.50) | collective-permute-done | bytes 262176 | tf_op jit(solution)/shard_map/ppermute | solution.py:295
  234.6 4.0 %collective-permute-done.44.rest_3_ = bf16[1,8,32,512]{3,2,1,0:T(8,128)(2,1)S(1)} collective-permute-done((bf16[1,8,32,512]{3,2,1,0:T(8,128)(2,1)S(1)}, bf16[1,8,32,512]{3,2,1,0:T(8,128)(2,1)S(1)}, u32[]{:S(2)}, u32[]{:S(2)}) %collective-permute-start.44) | collective-permute-done | bytes 262176 | tf_op jit(solution)/shard_map/ppermute | solution.py:295
  (111 shorter events, 34.7 us)
Async XLA Ops:
  5.4 8.0 %collective-permute-start = (bf16[2,4,32,256]{3,2,1,0:T(8,128)(2,1)S(1)}, bf16[2,4,32,256]{3,2,1,0:T(8,128)(2,1)S(1)}, u32[]{:S(2)}, u32[]{:S(2)}) collective-permute-start(bf16[2,4,32,256]{3,2,1,0:T(8,128)(2,1)S(1)} %get-tuple-element.81), channel_id=1, source_target_pairs={{0,8},{8,0},{16,24},{24,16},{1,9},{9,1},{17,25},{25,17},{2,10},{10... | collective-permute-start | bytes 393224 | tf_op jit(solution)/shard_map/ppermute | solution.py:313
  8.4 7.3 %collective-permute-start.1 = (bf16[2,4,32,256]{3,2,1,0:T(8,128)(2,1)S(1)}, bf16[2,4,32,256]{3,2,1,0:T(8,128)(2,1)S(1)}, u32[]{:S(2)}, u32[]{:S(2)}) collective-permute-start(bf16[2,4,32,256]{3,2,1,0:T(8,128)(2,1)S(1)} %get-tuple-element.82), channel_id=1, source_target_pairs={{0,16},{8,24},{16,0},{24,8},{1,17},{9,25},{17,1},{25,9},{2,18},{10... | collective-permute-start | bytes 393224 | tf_op jit(solution)/shard_map/ppermute | solution.py:313
  10.5 10.4 %collective-permute-start.25 = (bf16[2,4,32,256]{3,2,1,0:T(8,128)(2,1)S(1)}, bf16[2,4,32,256]{3,2,1,0:T(8,128)(2,1)S(1)}, u32[]{:S(2)}, u32[]{:S(2)}) collective-permute-start(bf16[2,4,32,256]{3,2,1,0:T(8,128)(2,1)S(1)} %get-tuple-element.114), channel_id=1, source_target_pairs={{0,16},{8,24},{16,0},{24,8},{1,17},{9,25},{17,1},{25,9},{2,18},{10... | collective-permute-start | bytes 393224 | tf_op jit(solution)/shard_map/ppermute | solution.py:313
  10.5 12.9 %collective-permute-start.26 = (bf16[2,4,32,256]{3,2,1,0:T(8,128)(2,1)S(1)}, bf16[2,4,32,256]{3,2,1,0:T(8,128)(2,1)S(1)}, u32[]{:S(2)}, u32[]{:S(2)}) collective-permute-start(bf16[2,4,32,256]{3,2,1,0:T(8,128)(2,1)S(1)} %get-tuple-element.115), channel_id=1, source_target_pairs={{0,24},{8,16},{16,8},{24,0},{1,25},{9,17},{17,9},{25,1},{2,26},{10... | collective-permute-start | bytes 393224 | tf_op jit(solution)/shard_map/ppermute | solution.py:313
  13.4 14.2 %collective-permute-start.2 = (bf16[2,4,32,256]{3,2,1,0:T(8,128)(2,1)S(1)}, bf16[2,4,32,256]{3,2,1,0:T(8,128)(2,1)S(1)}, u32[]{:S(2)}, u32[]{:S(2)}) collective-permute-start(bf16[2,4,32,256]{3,2,1,0:T(8,128)(2,1)S(1)} %get-tuple-element.83), channel_id=1, source_target_pairs={{0,24},{8,16},{16,8},{24,0},{1,25},{9,17},{17,9},{25,1},{2,26},{10... | collective-permute-start | bytes 393224 | tf_op jit(solution)/shard_map/ppermute | solution.py:313
  15.7 34.2 %collective-permute-start.6 = (bf16[2,8,32,256]{3,2,1,0:T(8,128)(2,1)S(1)}, bf16[2,8,32,256]{3,2,1,0:T(8,128)(2,1)S(1)}, u32[]{:S(2)}, u32[]{:S(2)}) collective-permute-start(bf16[2,8,32,256]{3,2,1,0:T(8,128)(2,1)S(1)} %get-tuple-element.89), channel_id=1, source_target_pairs={{0,8},{8,0},{16,24},{24,16},{1,9},{9,1},{17,25},{25,17},{2,10},{10... | collective-permute-start | bytes 786440 | tf_op jit(solution)/shard_map/ppermute | solution.py:313
  16.3 35.1 %collective-permute-start.18 = (bf16[2,8,32,256]{3,2,1,0:T(8,128)(2,1)S(1)}, bf16[2,8,32,256]{3,2,1,0:T(8,128)(2,1)S(1)}, u32[]{:S(2)}, u32[]{:S(2)}) collective-permute-start(bf16[2,8,32,256]{3,2,1,0:T(8,128)(2,1)S(1)} %get-tuple-element.105), channel_id=1, source_target_pairs={{0,8},{8,0},{16,24},{24,16},{1,9},{9,1},{17,25},{25,17},{2,10},{10... | collective-permute-start | bytes 786440 | tf_op jit(solution)/shard_map/ppermute | solution.py:313
  20.9 30.7 %collective-permute-start.19 = (bf16[2,8,32,256]{3,2,1,0:T(8,128)(2,1)S(1)}, bf16[2,8,32,256]{3,2,1,0:T(8,128)(2,1)S(1)}, u32[]{:S(2)}, u32[]{:S(2)}) collective-permute-start(bf16[2,8,32,256]{3,2,1,0:T(8,128)(2,1)S(1)} %get-tuple-element.106), channel_id=1, source_target_pairs={{0,16},{8,24},{16,0},{24,8},{1,17},{9,25},{17,1},{25,9},{2,18},{10... | collective-permute-start | bytes 786440 | tf_op jit(solution)/shard_map/ppermute | solution.py:313
  23.4 30.1 %collective-permute-start.20 = (bf16[2,8,32,256]{3,2,1,0:T(8,128)(2,1)S(1)}, bf16[2,8,32,256]{3,2,1,0:T(8,128)(2,1)S(1)}, u32[]{:S(2)}, u32[]{:S(2)}) collective-permute-start(bf16[2,8,32,256]{3,2,1,0:T(8,128)(2,1)S(1)} %get-tuple-element.107), channel_id=1, source_target_pairs={{0,24},{8,16},{16,8},{24,0},{1,25},{9,17},{17,9},{25,1},{2,26},{10... | collective-permute-start | bytes 786440 | tf_op jit(solution)/shard_map/ppermute | solution.py:313
  27.7 10.9 %collective-permute-start.33 = (bf16[1,4,32,256]{3,2,1,0:T(8,128)(2,1)S(1)}, bf16[1,4,32,256]{3,2,1,0:T(8,128)(2,1)S(1)}, u32[]{:S(2)}, u32[]{:S(2)}) collective-permute-start(bf16[1,4,32,256]{3,2,1,0:T(8,128)(2,1)S(1)} %get-tuple-element.126), channel_id=1, source_target_pairs={{0,8},{8,0},{16,24},{24,16},{1,9},{9,1},{17,25},{25,17},{2,10},{10... | collective-permute-start | bytes 196616 | tf_op jit(solution)/shard_map/ppermute | solution.py:313
  48.1 15.2 %collective-permute-start.7 = (bf16[2,8,32,256]{3,2,1,0:T(8,128)(2,1)S(1)}, bf16[2,8,32,256]{3,2,1,0:T(8,128)(2,1)S(1)}, u32[]{:S(2)}, u32[]{:S(2)}) collective-permute-start(bf16[2,8,32,256]{3,2,1,0:T(8,128)(2,1)S(1)} %get-tuple-element.90), channel_id=1, source_target_pairs={{0,16},{8,24},{16,0},{24,8},{1,17},{9,25},{17,1},{25,9},{2,18},{10... | collective-permute-start | bytes 786440 | tf_op jit(solution)/shard_map/ppermute | solution.py:313
  49.9 15.4 %collective-permute-start.8 = (bf16[2,8,32,256]{3,2,1,0:T(8,128)(2,1)S(1)}, bf16[2,8,32,256]{3,2,1,0:T(8,128)(2,1)S(1)}, u32[]{:S(2)}, u32[]{:S(2)}) collective-permute-start(bf16[2,8,32,256]{3,2,1,0:T(8,128)(2,1)S(1)} %get-tuple-element.91), channel_id=1, source_target_pairs={{0,24},{8,16},{16,8},{24,0},{1,25},{9,17},{17,9},{25,1},{2,26},{10... | collective-permute-start | bytes 786440 | tf_op jit(solution)/shard_map/ppermute | solution.py:313
  51.4 15.5 %collective-permute-start.12 = (bf16[2,8,32,256]{3,2,1,0:T(8,128)(2,1)S(1)}, bf16[2,8,32,256]{3,2,1,0:T(8,128)(2,1)S(1)}, u32[]{:S(2)}, u32[]{:S(2)}) collective-permute-start(bf16[2,8,32,256]{3,2,1,0:T(8,128)(2,1)S(1)} %get-tuple-element.97), channel_id=1, source_target_pairs={{0,8},{8,0},{16,24},{24,16},{1,9},{9,1},{17,25},{25,17},{2,10},{10... | collective-permute-start | bytes 786440 | tf_op jit(solution)/shard_map/ppermute | solution.py:313
  51.6 22.8 %collective-permute-start.13 = (bf16[2,8,32,256]{3,2,1,0:T(8,128)(2,1)S(1)}, bf16[2,8,32,256]{3,2,1,0:T(8,128)(2,1)S(1)}, u32[]{:S(2)}, u32[]{:S(2)}) collective-permute-start(bf16[2,8,32,256]{3,2,1,0:T(8,128)(2,1)S(1)} %get-tuple-element.98), channel_id=1, source_target_pairs={{0,16},{8,24},{16,0},{24,8},{1,17},{9,25},{17,1},{25,9},{2,18},{10... | collective-permute-start | bytes 786440 | tf_op jit(solution)/shard_map/ppermute | solution.py:313
  53.4 23.0 %collective-permute-start.14 = (bf16[2,8,32,256]{3,2,1,0:T(8,128)(2,1)S(1)}, bf16[2,8,32,256]{3,2,1,0:T(8,128)(2,1)S(1)}, u32[]{:S(2)}, u32[]{:S(2)}) collective-permute-start(bf16[2,8,32,256]{3,2,1,0:T(8,128)(2,1)S(1)} %get-tuple-element.99), channel_id=1, source_target_pairs={{0,24},{8,16},{16,8},{24,0},{1,25},{9,17},{17,9},{25,1},{2,26},{10... | collective-permute-start | bytes 786440 | tf_op jit(solution)/shard_map/ppermute | solution.py:313
  63.3 19.0 %collective-permute-start.3 = (bf16[2,4,32,256]{3,2,1,0:T(8,128)(2,1)S(1)}, bf16[2,4,32,256]{3,2,1,0:T(8,128)(2,1)S(1)}, u32[]{:S(2)}, u32[]{:S(2)}) collective-permute-start(bf16[2,4,32,256]{3,2,1,0:T(8,128)(2,1)S(1)} %get-tuple-element.85), channel_id=1, source_target_pairs={{0,8},{8,0},{16,24},{24,16},{1,9},{9,1},{17,25},{25,17},{2,10},{10... | collective-permute-start | bytes 393224 | tf_op jit(solution)/shard_map/ppermute | solution.py:313
  65.4 17.3 %collective-permute-start.4 = (bf16[2,4,32,256]{3,2,1,0:T(8,128)(2,1)S(1)}, bf16[2,4,32,256]{3,2,1,0:T(8,128)(2,1)S(1)}, u32[]{:S(2)}, u32[]{:S(2)}) collective-permute-start(bf16[2,4,32,256]{3,2,1,0:T(8,128)(2,1)S(1)} %get-tuple-element.86), channel_id=1, source_target_pairs={{0,16},{8,24},{16,0},{24,8},{1,17},{9,25},{17,1},{25,9},{2,18},{10... | collective-permute-start | bytes 393224 | tf_op jit(solution)/shard_map/ppermute | solution.py:313
  66.8 16.6 %collective-permute-start.5 = (bf16[2,4,32,256]{3,2,1,0:T(8,128)(2,1)S(1)}, bf16[2,4,32,256]{3,2,1,0:T(8,128)(2,1)S(1)}, u32[]{:S(2)}, u32[]{:S(2)}) collective-permute-start(bf16[2,4,32,256]{3,2,1,0:T(8,128)(2,1)S(1)} %get-tuple-element.87), channel_id=1, source_target_pairs={{0,24},{8,16},{16,8},{24,0},{1,25},{9,17},{17,9},{25,1},{2,26},{10... | collective-permute-start | bytes 393224 | tf_op jit(solution)/shard_map/ppermute | solution.py:313
  74.4 9.0 %collective-permute-start.30 = (bf16[1,8,32,256]{3,2,1,0:T(8,128)(2,1)S(1)}, bf16[1,8,32,256]{3,2,1,0:T(8,128)(2,1)S(1)}, u32[]{:S(2)}, u32[]{:S(2)}) collective-permute-start(bf16[1,8,32,256]{3,2,1,0:T(8,128)(2,1)S(1)} %get-tuple-element.122), channel_id=1, source_target_pairs={{0,8},{8,0},{16,24},{24,16},{1,9},{9,1},{17,25},{25,17},{2,10},{10... | collective-permute-start | bytes 393224 | tf_op jit(solution)/shard_map/ppermute | solution.py:313
  76.5 9.4 %collective-permute-start.31 = (bf16[1,8,32,256]{3,2,1,0:T(8,128)(2,1)S(1)}, bf16[1,8,32,256]{3,2,1,0:T(8,128)(2,1)S(1)}, u32[]{:S(2)}, u32[]{:S(2)}) collective-permute-start(bf16[1,8,32,256]{3,2,1,0:T(8,128)(2,1)S(1)} %get-tuple-element.123), channel_id=1, source_target_pairs={{0,16},{8,24},{16,0},{24,8},{1,17},{9,25},{17,1},{25,9},{2,18},{10... | collective-permute-start | bytes 393224 | tf_op jit(solution)/shard_map/ppermute | solution.py:313
  82.2 15.7 %collective-permute-start.15 = (bf16[2,8,32,256]{3,2,1,0:T(8,128)(2,1)S(1)}, bf16[2,8,32,256]{3,2,1,0:T(8,128)(2,1)S(1)}, u32[]{:S(2)}, u32[]{:S(2)}) collective-permute-start(bf16[2,8,32,256]{3,2,1,0:T(8,128)(2,1)S(1)} %get-tuple-element.101), channel_id=1, source_target_pairs={{0,8},{8,0},{16,24},{24,16},{1,9},{9,1},{17,25},{25,17},{2,10},{10... | collective-permute-start | bytes 786440 | tf_op jit(solution)/shard_map/ppermute | solution.py:313
  82.6 16.4 %collective-permute-start.16 = (bf16[2,8,32,256]{3,2,1,0:T(8,128)(2,1)S(1)}, bf16[2,8,32,256]{3,2,1,0:T(8,128)(2,1)S(1)}, u32[]{:S(2)}, u32[]{:S(2)}) collective-permute-start(bf16[2,8,32,256]{3,2,1,0:T(8,128)(2,1)S(1)} %get-tuple-element.102), channel_id=1, source_target_pairs={{0,16},{8,24},{16,0},{24,8},{1,17},{9,25},{17,1},{25,9},{2,18},{10... | collective-permute-start | bytes 786440 | tf_op jit(solution)/shard_map/ppermute | solution.py:313
  83.4 36.2 %collective-permute-start.51 = (bf16[4,4,32,512]{3,2,1,0:T(8,128)(2,1)S(1)}, bf16[4,4,32,512]{3,2,1,0:T(8,128)(2,1)S(1)}, u32[]{:S(2)}, u32[]{:S(2)}) collective-permute-start(bf16[4,4,32,512]{3,2,1,0:T(8,128)(2,1)S(1)} %get-tuple-element.141), channel_id=1, source_target_pairs={{0,1},{1,0},{2,3},{3,2},{4,5},{5,4},{6,7},{7,6},{8,9},{9,8},{10,11... | collective-permute-start | bytes 1572872 | tf_op jit(solution)/shard_map/ppermute | solution.py:290
  83.4 17.6 %collective-permute-start.17 = (bf16[2,8,32,256]{3,2,1,0:T(8,128)(2,1)S(1)}, bf16[2,8,32,256]{3,2,1,0:T(8,128)(2,1)S(1)}, u32[]{:S(2)}, u32[]{:S(2)}) collective-permute-start(bf16[2,8,32,256]{3,2,1,0:T(8,128)(2,1)S(1)} %get-tuple-element.103), channel_id=1, source_target_pairs={{0,24},{8,16},{16,8},{24,0},{1,25},{9,17},{17,9},{25,1},{2,26},{10... | collective-permute-start | bytes 786440 | tf_op jit(solution)/shard_map/ppermute | solution.py:313
  85.9 11.7 %collective-permute-start.32 = (bf16[1,8,32,256]{3,2,1,0:T(8,128)(2,1)S(1)}, bf16[1,8,32,256]{3,2,1,0:T(8,128)(2,1)S(1)}, u32[]{:S(2)}, u32[]{:S(2)}) collective-permute-start(bf16[1,8,32,256]{3,2,1,0:T(8,128)(2,1)S(1)} %get-tuple-element.124), channel_id=1, source_target_pairs={{0,24},{8,16},{16,8},{24,0},{1,25},{9,17},{17,9},{25,1},{2,26},{10... | collective-permute-start | bytes 393224 | tf_op jit(solution)/shard_map/ppermute | solution.py:313
  97.6 9.2 %collective-permute-start.9 = (bf16[2,8,32,256]{3,2,1,0:T(8,128)(2,1)S(1)}, bf16[2,8,32,256]{3,2,1,0:T(8,128)(2,1)S(1)}, u32[]{:S(2)}, u32[]{:S(2)}) collective-permute-start(bf16[2,8,32,256]{3,2,1,0:T(8,128)(2,1)S(1)} %get-tuple-element.93), channel_id=1, source_target_pairs={{0,8},{8,0},{16,24},{24,16},{1,9},{9,1},{17,25},{25,17},{2,10},{10... | collective-permute-start | bytes 786440 | tf_op jit(solution)/shard_map/ppermute | solution.py:313
  97.9 13.5 %collective-permute-start.10 = (bf16[2,8,32,256]{3,2,1,0:T(8,128)(2,1)S(1)}, bf16[2,8,32,256]{3,2,1,0:T(8,128)(2,1)S(1)}, u32[]{:S(2)}, u32[]{:S(2)}) collective-permute-start(bf16[2,8,32,256]{3,2,1,0:T(8,128)(2,1)S(1)} %get-tuple-element.94), channel_id=1, source_target_pairs={{0,16},{8,24},{16,0},{24,8},{1,17},{9,25},{17,1},{25,9},{2,18},{10... | collective-permute-start | bytes 786440 | tf_op jit(solution)/shard_map/ppermute | solution.py:313
  99.0 13.7 %collective-permute-start.11 = (bf16[2,8,32,256]{3,2,1,0:T(8,128)(2,1)S(1)}, bf16[2,8,32,256]{3,2,1,0:T(8,128)(2,1)S(1)}, u32[]{:S(2)}, u32[]{:S(2)}) collective-permute-start(bf16[2,8,32,256]{3,2,1,0:T(8,128)(2,1)S(1)} %get-tuple-element.95), channel_id=1, source_target_pairs={{0,24},{8,16},{16,8},{24,0},{1,25},{9,17},{17,9},{25,1},{2,26},{10... | collective-permute-start | bytes 786440 | tf_op jit(solution)/shard_map/ppermute | solution.py:313
  101.1 30.8 %collective-permute-start.39 = (bf16[4,4,32,512]{3,2,1,0:T(8,128)(2,1)S(1)}, bf16[4,4,32,512]{3,2,1,0:T(8,128)(2,1)S(1)}, u32[]{:S(2)}, u32[]{:S(2)}) collective-permute-start(bf16[4,4,32,512]{3,2,1,0:T(8,128)(2,1)S(1)} %get-tuple-element.133), channel_id=1, source_target_pairs={{0,1},{1,0},{2,3},{3,2},{4,5},{5,4},{6,7},{7,6},{8,9},{9,8},{10,11... | collective-permute-start | bytes 1572872 | tf_op jit(solution)/shard_map/ppermute | solution.py:290
  106.7 9.5 %collective-permute-start.27 = (bf16[1,4,32,256]{3,2,1,0:T(8,128)(2,1)S(1)}, bf16[1,4,32,256]{3,2,1,0:T(8,128)(2,1)S(1)}, u32[]{:S(2)}, u32[]{:S(2)}) collective-permute-start(bf16[1,4,32,256]{3,2,1,0:T(8,128)(2,1)S(1)} %get-tuple-element.117), channel_id=1, source_target_pairs={{0,8},{8,0},{16,24},{24,16},{1,9},{9,1},{17,25},{25,17},{2,10},{10... | collective-permute-start | bytes 196616 | tf_op jit(solution)/shard_map/ppermute | solution.py:313
  116.2 24.0 %collective-permute-start.45 = (bf16[4,8,32,512]{3,2,1,0:T(8,128)(2,1)S(1)}, bf16[4,8,32,512]{3,2,1,0:T(8,128)(2,1)S(1)}, u32[]{:S(2)}, u32[]{:S(2)}) collective-permute-start(bf16[4,8,32,512]{3,2,1,0:T(8,128)(2,1)S(1)} %get-tuple-element.137), channel_id=1, source_target_pairs={{0,1},{1,0},{2,3},{3,2},{4,5},{5,4},{6,7},{7,6},{8,9},{9,8},{10,11... | collective-permute-start | bytes 3145736 | tf_op jit(solution)/shard_map/ppermute | solution.py:290
  118.3 8.4 %collective-permute-start.22 = (bf16[1,8,32,256]{3,2,1,0:T(8,128)(2,1)S(1)}, bf16[1,8,32,256]{3,2,1,0:T(8,128)(2,1)S(1)}, u32[]{:S(2)}, u32[]{:S(2)}) collective-permute-start(bf16[1,8,32,256]{3,2,1,0:T(8,128)(2,1)S(1)} %get-tuple-element.110), channel_id=1, source_target_pairs={{0,16},{8,24},{16,0},{24,8},{1,17},{9,25},{17,1},{25,9},{2,18},{10... | collective-permute-start | bytes 393224 | tf_op jit(solution)/shard_map/ppermute | solution.py:313
  122.5 18.3 %collective-permute-start.48 = (bf16[4,8,32,512]{3,2,1,0:T(8,128)(2,1)S(1)}, bf16[4,8,32,512]{3,2,1,0:T(8,128)(2,1)S(1)}, u32[]{:S(2)}, u32[]{:S(2)}) collective-permute-start(bf16[4,8,32,512]{3,2,1,0:T(8,128)(2,1)S(1)} %get-tuple-element.139), channel_id=1, source_target_pairs={{0,1},{1,0},{2,3},{3,2},{4,5},{5,4},{6,7},{7,6},{8,9},{9,8},{10,11... | collective-permute-start | bytes 3145736 | tf_op jit(solution)/shard_map/ppermute | solution.py:290
  126.6 8.9 %collective-permute-start.36 = (bf16[4,32,16,128]{3,2,1,0:T(8,128)(2,1)S(1)}, bf16[4,32,16,128]{3,2,1,0:T(8,128)(2,1)S(1)}, u32[]{:S(2)}, u32[]{:S(2)}) collective-permute-start(bf16[4,32,16,128]{3,2,1,0:T(8,128)(2,1)S(1)} %get-tuple-element.131), channel_id=1, source_target_pairs={{0,1},{1,0},{2,3},{3,2},{4,5},{5,4},{6,7},{7,6},{8,9},{9,8},{10,11... | collective-permute-start | bytes 1572872 | tf_op jit(solution)/shard_map/ppermute | solution.py:290
  126.7 8.8 %collective-permute-start.52 = (bf16[2,4,32,512]{3,2,1,0:T(8,128)(2,1)S(1)}, bf16[2,4,32,512]{3,2,1,0:T(8,128)(2,1)S(1)}, u32[]{:S(2)}, u32[]{:S(2)}) collective-permute-start(bf16[2,4,32,512]{3,2,1,0:T(8,128)(2,1)S(1)} %add_convert_fusion.4), channel_id=1, source_target_pairs={{0,2},{1,3},{2,0},{3,1},{4,6},{5,7},{6,4},{7,5},{8,10},{9,11},{10,... | collective-permute-start | bytes 786440 | tf_op jit(solution)/shard_map/ppermute | solution.py:295
  135.5 64.1 %collective-permute-start.40 = (bf16[2,4,32,512]{3,2,1,0:T(8,128)(2,1)S(1)}, bf16[2,4,32,512]{3,2,1,0:T(8,128)(2,1)S(1)}, u32[]{:S(2)}, u32[]{:S(2)}) collective-permute-start(bf16[2,4,32,512]{3,2,1,0:T(8,128)(2,1)S(1)} %add_convert_fusion.8), channel_id=1, source_target_pairs={{0,2},{1,3},{2,0},{3,1},{4,6},{5,7},{6,4},{7,5},{8,10},{9,11},{10,... | collective-permute-start | bytes 786440 | tf_op jit(solution)/shard_map/ppermute | solution.py:295
  137.4 63.4 %collective-permute-start.53 = (bf16[1,4,32,512]{3,2,1,0:T(8,128)(2,1)S(1)}, bf16[1,4,32,512]{3,2,1,0:T(8,128)(2,1)S(1)}, u32[]{:S(2)}, u32[]{:S(2)}) collective-permute-start(bf16[1,4,32,512]{3,2,1,0:T(8,128)(2,1)S(1)} %add_convert_fusion.11), channel_id=1, source_target_pairs={{0,4},{1,5},{2,6},{3,7},{4,0},{5,1},{6,2},{7,3},{8,12},{9,13},{10,... | collective-permute-start | bytes 393224 | tf_op jit(solution)/shard_map/ppermute | solution.py:295
  140.2 13.0 %collective-permute-start.37 = (bf16[2,32,16,128]{3,2,1,0:T(8,128)(2,1)S(1)}, bf16[2,32,16,128]{3,2,1,0:T(8,128)(2,1)S(1)}, u32[]{:S(2)}, u32[]{:S(2)}) collective-permute-start(bf16[2,32,16,128]{3,2,1,0:T(8,128)(2,1)S(1)} %add_convert_fusion.9), channel_id=1, source_target_pairs={{0,2},{1,3},{2,0},{3,1},{4,6},{5,7},{6,4},{7,5},{8,10},{9,11},{10,... | collective-permute-start | bytes 786440 | tf_op jit(solution)/shard_map/ppermute | solution.py:295
  140.9 18.0 %collective-permute-start.55 = (bf16[2,32,16,128]{3,2,1,0:T(8,128)(2,1)S(1)}, bf16[2,32,16,128]{3,2,1,0:T(8,128)(2,1)S(1)}, u32[]{:S(2)}, u32[]{:S(2)}) collective-permute-start(bf16[2,32,16,128]{3,2,1,0:T(8,128)(2,1)S(1)} %add_convert_fusion.3), channel_id=1, source_target_pairs={{0,2},{1,3},{2,0},{3,1},{4,6},{5,7},{6,4},{7,5},{8,10},{9,11},{10,... | collective-permute-start | bytes 786440 | tf_op jit(solution)/shard_map/ppermute | solution.py:295
  142.7 27.4 %collective-permute-start.46 = (bf16[2,8,32,512]{3,2,1,0:T(8,128)(2,1)S(1)}, bf16[2,8,32,512]{3,2,1,0:T(8,128)(2,1)S(1)}, u32[]{:S(2)}, u32[]{:S(2)}) collective-permute-start(bf16[2,8,32,512]{3,2,1,0:T(8,128)(2,1)S(1)} %add_convert_fusion.1), channel_id=1, source_target_pairs={{0,2},{1,3},{2,0},{3,1},{4,6},{5,7},{6,4},{7,5},{8,10},{9,11},{10,... | collective-permute-start | bytes 1572872 | tf_op jit(solution)/shard_map/ppermute | solution.py:295
  153.2 30.9 %collective-permute-start.49 = (bf16[2,8,32,512]{3,2,1,0:T(8,128)(2,1)S(1)}, bf16[2,8,32,512]{3,2,1,0:T(8,128)(2,1)S(1)}, u32[]{:S(2)}, u32[]{:S(2)}) collective-permute-start(bf16[2,8,32,512]{3,2,1,0:T(8,128)(2,1)S(1)} %add_convert_fusion), channel_id=1, source_target_pairs={{0,2},{1,3},{2,0},{3,1},{4,6},{5,7},{6,4},{7,5},{8,10},{9,11},{10,... | collective-permute-start | bytes 1572872 | tf_op jit(solution)/shard_map/ppermute | solution.py:295
  158.8 38.9 %collective-permute-start.43 = (bf16[2,8,32,512]{3,2,1,0:T(8,128)(2,1)S(1)}, bf16[2,8,32,512]{3,2,1,0:T(8,128)(2,1)S(1)}, u32[]{:S(2)}, u32[]{:S(2)}) collective-permute-start(bf16[2,8,32,512]{3,2,1,0:T(8,128)(2,1)S(1)} %add_convert_fusion.2), channel_id=1, source_target_pairs={{0,2},{1,3},{2,0},{3,1},{4,6},{5,7},{6,4},{7,5},{8,10},{9,11},{10,... | collective-permute-start | bytes 1572872 | tf_op jit(solution)/shard_map/ppermute | solution.py:295
  170.1 32.7 %collective-permute-start.38 = (bf16[1,32,16,128]{3,2,1,0:T(8,128)(2,1)S(1)}, bf16[1,32,16,128]{3,2,1,0:T(8,128)(2,1)S(1)}, u32[]{:S(2)}, u32[]{:S(2)}) collective-permute-start(bf16[1,32,16,128]{3,2,1,0:T(8,128)(2,1)S(1)} %add_convert_fusion.13), channel_id=1, source_target_pairs={{0,4},{1,5},{2,6},{3,7},{4,0},{5,1},{6,2},{7,3},{8,12},{9,13},{10,... | collective-permute-start | bytes 393224 | tf_op jit(solution)/shard_map/ppermute | solution.py:295
  184.1 21.8 %collective-permute-start.56 = (bf16[1,32,16,128]{3,2,1,0:T(8,128)(2,1)S(1)}, bf16[1,32,16,128]{3,2,1,0:T(8,128)(2,1)S(1)}, u32[]{:S(2)}, u32[]{:S(2)}) collective-permute-start(bf16[1,32,16,128]{3,2,1,0:T(8,128)(2,1)S(1)} %add_convert_fusion.10), channel_id=1, source_target_pairs={{0,4},{1,5},{2,6},{3,7},{4,0},{5,1},{6,2},{7,3},{8,12},{9,13},{10,... | collective-permute-start | bytes 393224 | tf_op jit(solution)/shard_map/ppermute | solution.py:295
  197.7 36.1 %collective-permute-start.47 = (bf16[1,8,32,512]{3,2,1,0:T(8,128)(2,1)S(1)}, bf16[1,8,32,512]{3,2,1,0:T(8,128)(2,1)S(1)}, u32[]{:S(2)}, u32[]{:S(2)}) collective-permute-start(bf16[1,8,32,512]{3,2,1,0:T(8,128)(2,1)S(1)} %add_convert_fusion.6), channel_id=1, source_target_pairs={{0,4},{1,5},{2,6},{3,7},{4,0},{5,1},{6,2},{7,3},{8,12},{9,13},{10,... | collective-permute-start | bytes 786440 | tf_op jit(solution)/shard_map/ppermute | solution.py:295
  199.7 33.3 %collective-permute-start.50 = (bf16[1,8,32,512]{3,2,1,0:T(8,128)(2,1)S(1)}, bf16[1,8,32,512]{3,2,1,0:T(8,128)(2,1)S(1)}, u32[]{:S(2)}, u32[]{:S(2)}) collective-permute-start(bf16[1,8,32,512]{3,2,1,0:T(8,128)(2,1)S(1)} %add_convert_fusion.5), channel_id=1, source_target_pairs={{0,4},{1,5},{2,6},{3,7},{4,0},{5,1},{6,2},{7,3},{8,12},{9,13},{10,... | collective-permute-start | bytes 786440 | tf_op jit(solution)/shard_map/ppermute | solution.py:295
  200.8 37.8 %collective-permute-start.44 = (bf16[1,8,32,512]{3,2,1,0:T(8,128)(2,1)S(1)}, bf16[1,8,32,512]{3,2,1,0:T(8,128)(2,1)S(1)}, u32[]{:S(2)}, u32[]{:S(2)}) collective-permute-start(bf16[1,8,32,512]{3,2,1,0:T(8,128)(2,1)S(1)} %add_convert_fusion.7), channel_id=1, source_target_pairs={{0,4},{1,5},{2,6},{3,7},{4,0},{5,1},{6,2},{7,3},{8,12},{9,13},{10,... | collective-permute-start | bytes 786440 | tf_op jit(solution)/shard_map/ppermute | solution.py:295
  202.8 37.4 %collective-permute-start.41 = (bf16[1,4,32,512]{3,2,1,0:T(8,128)(2,1)S(1)}, bf16[1,4,32,512]{3,2,1,0:T(8,128)(2,1)S(1)}, u32[]{:S(2)}, u32[]{:S(2)}) collective-permute-start(bf16[1,4,32,512]{3,2,1,0:T(8,128)(2,1)S(1)} %add_convert_fusion.12), channel_id=1, source_target_pairs={{0,4},{1,5},{2,6},{3,7},{4,0},{5,1},{6,2},{7,3},{8,12},{9,13},{10,... | collective-permute-start | bytes 393224 | tf_op jit(solution)/shard_map/ppermute | solution.py:295
  (17 other events, 168.8 us)
